TPU v7x, 256 devices: a whole 4x4x8 slice. The times are simulated.
256 devices in a mesh: probe: 2 (over x_lo), row: 16 (over x_hi, y, core), col: 8 (over z).
Axes of the slice: x: 4 (x_hi: 2, x_lo: 2; x = x_hi * 2 + x_lo), y: 4, z: 8, core: 2. Of those that a mesh axis runs over, the one named last changes fastest.
Arguments:
- flow_state: bfloat16 [2, 5, 192, 192, 384], P('probe', None, 'row', 'col'), may hold values from -6 to 6
- forcing: bfloat16 [2, 5, 192, 192, 384], P('probe', None, 'row', 'col'), may hold values from -6 to 6
- advect_x: bfloat16 [192, 192, 384], P('row', 'col'), may hold values from 0.19921875 to 1.5
- advect_y: bfloat16 [192, 192, 384], P('row', 'col'), may hold values from 0.19921875 to 1.5
- advect_z: bfloat16 [192, 192, 384], P('row', 'col'), may hold values from 0.19921875 to 1.5
- diffusivity: float32 [5], replicated, may hold values from 0.2 to 1
- deriv_x: bfloat16 [2, 384, 384], replicated, may hold values from -0.3125 to 0.3125
- deriv_y: bfloat16 [2, 192, 192], replicated, may hold values from -0.4375 to 0.4375
- deriv_z: bfloat16 [2, 192, 192], replicated, may hold values from -0.4375 to 0.4375
- test_mix: float32 [2, 2], replicated, may hold values from -4 to 4
Outputs:
- section_out: bfloat16 [2, 5, 192, 192, 384], P('probe', None, 'row', 'col')
- sketch: bfloat16 [2, 5, 192, 192, 384], P(None, None, 'row', 'col', 'probe')
All inputs are finite; a program needn't handle non-finite values.
Results may differ from a plain program's by a relative error of at most 0.0095.
Values may be sent and summed in bfloat16 or wider, within the bound.
No kernel may reach another device: no remote copies, remote signals or barrier semaphores. Data moves between devices by JAX's collectives and lax.ppermute only.
A program may use at most 128 MiB of HBM per device.

v0:
```python
import jax
import jax.numpy as jnp
import numpy as np
from jax import lax
from jax.experimental import pallas as pl
from jax.experimental.pallas import tpu as pltpu
from jax.sharding import PartitionSpec as P

step_size = 0.25

VMEM = pltpu.VMEM
F32 = jnp.float32
BF16 = jnp.bfloat16


def vspec():
    return pl.BlockSpec(memory_space=pltpu.VMEM)


def sspec():
    return pl.BlockSpec(memory_space=pltpu.SMEM)


def swap(x):
    return pltpu.roll(x, 64, x.ndim - 1)


def low_lanes(shape):
    return lax.broadcasted_iota(jnp.int32, shape, len(shape) - 1) < 64


def merge(half, first, second):
    low = low_lanes(first.shape)
    if half == 0:
        return jnp.where(low, first, swap(second))
    return jnp.where(low, swap(first), second)


def z_pack_kernel(state, adv, out):
    def body(a, carry):
        for yl in range(3):
            y = 3 * a + yl
            rows = [state[v, y].astype(F32) for v in range(5)] + [adv[y].astype(F32)]
            for b in range(2):
                for u in range(6):
                    at = yl * 216 + 24 * u
                    out[2 * a + b, at : at + 24, :] = rows[u][:, 256 * b : 256 * b + 128].astype(BF16)
                for q in range(3):
                    at = yl * 216 + 144 + 24 * q
                    tile = merge(b, rows[2 * q][:, 128:256], rows[2 * q + 1][:, 128:256])
                    out[2 * a + b, at : at + 24, :] = tile.astype(BF16)
        return carry

    lax.fori_loop(0, 4, body, 0)


def y_pack_kernel(state, adv, out):
    def lines(p, c):
        lanes = slice(128 * c, 128 * c + 128)
        if p < 2:
            block = state[2 * p : 2 * p + 2, :, :, lanes].astype(F32).reshape(24, 24, 128)
        else:
            block = jnp.concatenate([state[4, :, :, lanes], adv[:, :, lanes]], axis=0).astype(F32)
        return jnp.swapaxes(block, 0, 1)

    for p in range(3):
        for b in range(2):
            out[:, b, 72 * p : 72 * p + 72, :] = lines(p, 2 * b).reshape(8, 72, 128).astype(BF16)
    mid = [lines(p, 1) for p in range(2)]
    for b in range(2):
        tile = merge(b, mid[0], mid[1])
        out[:, b, 216:288, :] = tile.reshape(8, 72, 128).astype(BF16)
    last = lines(2, 1).reshape(8, 3, 24, 128)
    none = jnp.zeros((8, 24, 128), F32)
    for b in range(2):
        out[:, b, 288:312, :] = merge(b, last[:, 0], last[:, 1]).astype(BF16)
        out[:, b, 312:336, :] = merge(b, last[:, 2], none).astype(BF16)


def x_kernel(coef, state, forcing, adv, mat, out):
    lhs_mat = mat[...].reshape(768, 384)
    for v in range(5):
        for h in range(2):
            ys = slice(6 * h, 6 * h + 6)
            field = state[v, ys].astype(F32).reshape(144, 384)
            grad = lax.dot_general(
                field.astype(BF16), lhs_mat, (((1,), (1,)), ((), ())), preferred_element_type=F32
            )
            vel = adv[ys].astype(F32).reshape(144, 384)
            frc = forcing[v, ys].astype(F32).reshape(144, 384)
            term = coef[v] * grad[:, 384:] - vel * grad[:, :384]
            out[v, ys] = (field + step_size * (term + frc)).reshape(6, 24, 384)


def z_kernel(coef, recv, mat, out):
    lhs = mat[...].reshape(384, 192)
    low = low_lanes((192, 128))

    def tile(yl, t):
        at = yl * 216 + 24 * t
        return recv[:, at : at + 24, :].astype(F32).reshape(192, 128)

    def put(t, term):
        out[:, 24 * t : 24 * t + 24, :] = term.reshape(8, 24, 128).astype(BF16)

    tails = []
    for yl in range(3):
        tiles = [tile(yl, t) for t in range(9)]
        vel = tiles[5]
        vel_half = jnp.where(low, swap(tiles[8]), tiles[8])
        names = [0, 1, 2, 3, 4, 6, 7, 8]
        for n in range(0, 8, 2):
            rhs = jnp.concatenate([tiles[names[n]], tiles[names[n + 1]]], axis=1).astype(BF16)
            grad = jnp.dot(lhs, rhs, preferred_element_type=F32)
            for j in range(2):
                t = names[n + j]
                g0 = grad[:192, 128 * j : 128 * j + 128]
                g1 = grad[192:, 128 * j : 128 * j + 128]
                if t < 5:
                    put(yl * 7 + t, coef[t] * g1 - vel * g0)
                elif t < 8:
                    q = t - 6
                    c = jnp.where(low, coef[2 * q], coef[2 * q + 1])
                    put(yl * 7 + 5 + q, c * g1 - vel_half * g0)
                else:
                    tails.append(coef[4] * g1 - vel_half * g0)
    put(21, jnp.where(low, tails[0], swap(tails[1])))
    put(22, jnp.where(low, tails[2], 0.0))


def y_terms_kernel(coef, recv, mat, spread, gather, out, both):
    half = [spread[m] for m in range(2)]
    for k in range(2):
        acc = jnp.zeros((384, 384), F32)
        for m in range(2):
            left = jnp.dot(half[m], mat[k], preferred_element_type=F32).astype(BF16)
            acc = acc + lax.dot_general(
                left, half[m], (((1,), (1,)), ((), ())), preferred_element_type=F32
            )
        both[384 * k : 384 * k + 384, :] = acc.astype(BF16)
    lhs = both[...]
    take = gather[...]
    low = low_lanes((384, 128))
    member = lax.broadcasted_iota(jnp.int32, (16, 24, 128), 1).reshape(384, 128) >= 12

    def tile(t):
        return recv[:, 24 * t : 24 * t + 24, :].astype(F32).reshape(384, 128).astype(BF16)

    def put(t, term):
        out[:, 24 * t : 24 * t + 24, :] = term.reshape(16, 24, 128).astype(BF16)

    def coef_of(p):
        if p == 2:
            return jnp.where(member, 0.0, coef[4])
        return jnp.where(member, coef[2 * p + 1], coef[2 * p])

    vel_tail = jnp.dot(
        take, jnp.concatenate([tile(12), tile(13)], axis=1), preferred_element_type=F32
    )
    tail = [vel_tail[:, :128], vel_tail[:, 128:]]
    vel_half = [
        jnp.where(low, tail[0], swap(tail[0])),
        jnp.where(low, swap(tail[0]), tail[0]),
        jnp.where(low, tail[1], swap(tail[1])),
    ]

    def terms(t, vel, c):
        grad = jnp.dot(lhs, tile(t), preferred_element_type=F32)
        put(t, c * grad[384:] - vel * grad[:384])

    for zl in range(3):
        vel = jnp.dot(take, tile(6 + zl), preferred_element_type=F32)
        for p in range(3):
            terms(3 * p + zl, vel, coef_of(p))
        terms(9 + zl, vel_half[zl], jnp.where(low, coef_of(0), coef_of(1)))
    for j in range(2):
        terms(12 + j, tail[j], coef_of(2))


def join_kernel(probe, base, back_z, back_y, out, send, own, work):
    first = probe[0] == 0

    def put_lines(c, block):
        work[:, :, 128 * c : 128 * c + 128] = jnp.swapaxes(block, 0, 1)

    def y_tile(b, at, n):
        return back_y[:, b, at : at + 24 * n, :].astype(F32)

    low3 = low_lanes((24, 24, 128))
    low8 = low_lanes((8, 24, 128))
    low = low_lanes((24, 128))
    for p in range(3):
        for b in range(2):
            put_lines(2 * b, y_tile(b, 72 * p, 3).reshape(24, 24, 128))
        if p < 2:
            m = [y_tile(b, 216, 3).reshape(24, 24, 128) for b in range(2)]
            if p == 0:
                put_lines(1, jnp.where(low3, m[0], swap(m[1])))
            else:
                put_lines(1, jnp.where(low3, swap(m[0]), m[1]))
        else:
            m = [[y_tile(b, 288 + 24 * j, 1) for j in range(2)] for b in range(2)]
            parts = [
                jnp.where(low8, m[0][0], swap(m[1][0])),
                jnp.where(low8, swap(m[0][0]), m[1][0]),
                jnp.where(low8, m[0][1], swap(m[1][1])),
            ]
            put_lines(1, jnp.stack(parts, axis=1).reshape(24, 24, 128))
        for i in range(2 if p < 2 else 1):
            v = 2 * p + i

            def z_tile(d, t):
                return back_z[d, 24 * t : 24 * t + 24, :].astype(F32)

            def one(a, yl, v=v, i=i):
                y = 3 * a + yl
                full = [z_tile(2 * a + b, 7 * yl + v) for b in range(2)]
                if v < 4:
                    t, odd = 7 * yl + 5 + v // 2, v % 2
                else:
                    t, odd = 21 + yl // 2, yl % 2
                m = [z_tile(2 * a + b, t) for b in range(2)]
                if odd:
                    mid = jnp.where(low, swap(m[0]), m[1])
                else:
                    mid = jnp.where(low, m[0], swap(m[1]))
                res = []
                for c, part in enumerate((full[0], mid, full[1])):
                    lanes = slice(128 * c, 128 * c + 128)
                    total = base[v, y, :, lanes] + step_size * (part + work[12 * i + y, :, lanes])
                    total = total.astype(BF16)
                    out[v, y, :, lanes] = total
                    res.append(total.astype(F32))
                f = 12 * v + y
                send[f] = jnp.where(first, res[2], res[0]).astype(BF16)
                own[f] = jnp.where(first, res[0], res[2]).astype(BF16)
                return res[1]

            def body(a2, carry):
                mids = [one(2 * a2 + k // 3, k % 3) for k in range(6)]
                for j in range(3):
                    h = 60 + 6 * v + 3 * a2 + j
                    part0 = merge(0, mids[2 * j], mids[2 * j + 1])
                    part1 = merge(1, mids[2 * j], mids[2 * j + 1])
                    send[h] = jnp.where(first, part1, part0).astype(BF16)
                    own[h] = jnp.where(first, part0, part1).astype(BF16)
                return carry

            lax.fori_loop(0, 2, body, 0)


def sketch_kernel(probe, mix, own, recv, out):
    p = probe[0]
    low = low_lanes((24, 128))

    def body(i, carry):
        v = i // 6
        j = i % 6
        at = 12 * v + 2 * j
        for g in range(2):
            m_own = mix[p, g]
            m_recv = mix[1 - p, g]

            def mixed(n):
                a = (own[n].astype(F32) * m_own).astype(BF16).astype(F32)
                b = (recv[n].astype(F32) * m_recv).astype(BF16).astype(F32)
                return a + b

            half = mixed(60 + i)
            for k in range(2):
                full = mixed(at + k)
                piece = half if k == 0 else swap(half)
                turned = swap(full)
                head = jnp.where(p == 0, full, jnp.where(low, piece, turned))
                tail = jnp.where(p == 0, piece, turned)
                out[g, v, 2 * j + k, :, 0:128] = head.astype(BF16)
                out[g, v, 2 * j + k, :, 128:192] = tail[:, :64].astype(BF16)
        return carry

    lax.fori_loop(0, 30, body, 0)


def call(kernel, out_shapes, specs, scratch=(), name=None):
    many = isinstance(out_shapes, (list, tuple))
    return pl.pallas_call(
        kernel,
        out_shape=out_shapes,
        in_specs=specs,
        out_specs=[vspec() for _ in out_shapes] if many else vspec(),
        scratch_shapes=scratch,
        name=name,
    )


def row_tables():
    rows = np.arange(384)
    q = rows // 12
    point = 12 * (q // 2) + rows % 12
    spread = np.zeros((2, 384, 192), np.float32)
    spread[q % 2, rows, point] = 1.0
    gather = (spread[0] + spread[1]) @ spread[1].T
    return spread, gather


def on_device(
    flow_state,
    forcing,
    advect_x,
    advect_y,
    advect_z,
    diffusivity,
    deriv_x,
    deriv_y,
    deriv_z,
    test_mix,
):
    state = flow_state.reshape(5, 12, 24, 384)
    forced = forcing.reshape(5, 12, 24, 384)
    probe = lax.axis_index("probe").astype(jnp.int32).reshape(1)
    spread, gather = row_tables()
    spread = jnp.asarray(spread, BF16)
    gather = jnp.asarray(gather, BF16)

    def shape(s, t=BF16):
        return jax.ShapeDtypeStruct(s, t)

    to_z = call(z_pack_kernel, shape((8, 648, 128)), [vspec()] * 2, name="z_pack")(state, advect_z)
    at_z = lax.all_to_all(to_z, "col", split_axis=0, concat_axis=0, tiled=True)
    to_y = call(y_pack_kernel, shape((8, 2, 336, 128)), [vspec()] * 2, name="y_pack")(state, advect_y)
    at_y = lax.all_to_all(
        to_y.reshape(16, 336, 128), "row", split_axis=0, concat_axis=0, tiled=True
    )
    base = call(
        x_kernel, shape((5, 12, 24, 384), F32), [sspec()] + [vspec()] * 4, name="x_term"
    )(diffusivity, state, forced, advect_x, deriv_x)
    term_z = call(z_kernel, shape((8, 552, 128)), [sspec()] + [vspec()] * 2, name="z_term")(
        diffusivity, at_z, deriv_z
    )
    back_z = lax.all_to_all(term_z, "col", split_axis=0, concat_axis=0, tiled=True)
    term_y = call(
        y_terms_kernel,
        shape((16, 336, 128)),
        [sspec()] + [vspec()] * 4,
        [pltpu.VMEM((768, 384), BF16)],
        name="y_term",
    )(diffusivity, at_y, deriv_y, spread, gather)
    back_y = lax.all_to_all(term_y, "row", split_axis=0, concat_axis=0, tiled=True)
    section, send, own = call(
        join_kernel,
        [shape((5, 12, 24, 384)), shape((90, 24, 128)), shape((90, 24, 128))],
        [sspec()] + [vspec()] * 3,
        [pltpu.VMEM((24, 24, 384), F32)],
        name="join",
    )(probe, base, back_z, back_y.reshape(8, 2, 336, 128))
    recv = lax.ppermute(send, "probe", [(0, 1), (1, 0)])
    sketch = call(
        sketch_kernel, shape((2, 5, 12, 24, 192)), [sspec()] * 2 + [vspec()] * 2, name="sketch"
    )(probe, test_mix, own, recv)
    return (section[None], sketch)


def solution(mesh):
    placed = (
        P("probe", None, "row", "col", None),
        P("probe", None, "row", "col", None),
        P("row", "col", None),
        P("row", "col", None),
        P("row", "col", None),
        P(),
        P(),
        P(),
        P(),
        P(),
    )
    return jax.shard_map(
        on_device,
        mesh=mesh,
        in_specs=placed,
        out_specs=(P("probe", None, "row", "col", None), P(None, None, "row", "col", "probe")),
        check_vma=False,
    )
```

profile of v0, /device:TPU:1, one launch (start us, length us, event | category | flops | bytes accessed | tf_op | source)
XLA Modules:
  0.0 164.9 jit_solution(2574218143717115876)
XLA Ops:
  0.6 3.1 %y_pack.1 = bf16[8,2,336,128]{3,2,1,0:T(8,128)(2,1)} custom-call(bf16[5,12,24,384]{3,2,1,0:T(8,128)(2,1)} %bitcast.6, bf16[12,24,384]{2,1,0:T(8,128)(2,1)} %adv.5), custom_call_target="tpu_custom_call" | custom-call | tf_op jit(solution)/shard_map/y_pack/pallas_call | solution.py:329
  3.7 8.4 %all-to-all-start.2 = ((bf16[16,336,128]{2,1,0:T(8,128)(2,1)}), bf16[16,336,128]{2,1,0:T(8,128)(2,1)S(1)}, u32[]{:S(2)}, u32[]{:S(2)}) async-start(bf16[16,336,128]{2,1,0:T(8,128)(2,1)} %bitcast.10), calls=%async_computation.2 | async-start | bytes 2752512 | tf_op jit(solution)/shard_map/all_to_all | solution.py:330
  12.1 2.8 %z_pack.1 = bf16[8,648,128]{2,1,0:T(8,128)(2,1)} custom-call(bf16[5,12,24,384]{3,2,1,0:T(8,128)(2,1)} %bitcast.7, bf16[12,24,384]{2,1,0:T(8,128)(2,1)} %adv.4), custom_call_target="tpu_custom_call" | custom-call | tf_op jit(solution)/shard_map/z_pack/pallas_call | solution.py:327
  14.9 17.9 %all-to-all-done.2.recv = bf16[16,336,128]{2,1,0:T(8,128)(2,1)S(1)} async-done(((bf16[16,336,128]{2,1,0:T(8,128)(2,1)}), bf16[16,336,128]{2,1,0:T(8,128)(2,1)S(1)}, u32[]{:S(2)}, u32[]{:S(2)}) %all-to-all-start.2) | async-done | bytes 1376288 | tf_op jit(solution)/shard_map/all_to_all | solution.py:330
  32.8 0.0 copy-start.1
  32.8 1.1 copy-done.1
  33.8 8.2 %all-to-all-start = ((bf16[8,648,128]{2,1,0:T(8,128)(2,1)}), bf16[8,648,128]{2,1,0:T(8,128)(2,1)S(1)}, u32[]{:S(2)}, u32[]{:S(2)}) async-start(bf16[8,648,128]{2,1,0:T(8,128)(2,1)} %z_pack.1), calls=%async_computation | async-start | bytes 2654208 | tf_op jit(solution)/shard_map/all_to_all | solution.py:328
  42.0 6.1 %y_term.1 = bf16[16,336,128]{2,1,0:T(8,128)(2,1)} custom-call(f32[5]{0:T(128)} %coef.5, bf16[16,336,128]{2,1,0:T(8,128)(2,1)} %copy-done.1, bf16[2,192,192]{2,1,0:T(8,128)(2,1)} %mat.5, bf16[2,384,192]{2,1,0:T(8,128)(2,1)} %constant.10.clone.spread, bf16[384,384]{1,0:T(8,128)(2,1)} %constant.11.clone.gather), custom_call_target="tpu_custom_call" | custom-call | tf_op jit(solution)/shard_map/y_term/pallas_call | solution.py:340
  48.1 29.1 %all-to-all-done.recv = bf16[8,648,128]{2,1,0:T(8,128)(2,1)S(1)} async-done(((bf16[8,648,128]{2,1,0:T(8,128)(2,1)}), bf16[8,648,128]{2,1,0:T(8,128)(2,1)S(1)}, u32[]{:S(2)}, u32[]{:S(2)}) %all-to-all-start) | async-done | bytes 1327136 | tf_op jit(solution)/shard_map/all_to_all | solution.py:328
  77.2 0.0 copy-start.2
  77.2 1.1 copy-done.2
  78.2 4.5 %all-to-all-start.3 = ((bf16[16,336,128]{2,1,0:T(8,128)(2,1)}), bf16[16,336,128]{2,1,0:T(8,128)(2,1)S(1)}, u32[]{:S(2)}, u32[]{:S(2)}) async-start(bf16[16,336,128]{2,1,0:T(8,128)(2,1)} %y_term.1), calls=%async_computation.3 | async-start | bytes 2752512 | tf_op jit(solution)/shard_map/all_to_all | solution.py:347
  82.7 3.1 %z_term.1 = bf16[8,552,128]{2,1,0:T(8,128)(2,1)} custom-call(f32[5]{0:T(128)} %coef.5, bf16[8,648,128]{2,1,0:T(8,128)(2,1)} %copy-done.2, bf16[2,192,192]{2,1,0:T(8,128)(2,1)} %mat.4), custom_call_target="tpu_custom_call" | custom-call | tf_op jit(solution)/shard_map/z_term/pallas_call | solution.py:336
  85.8 17.5 %all-to-all-done.3 = bf16[16,336,128]{2,1,0:T(8,128)(2,1)S(1)} async-done(((bf16[16,336,128]{2,1,0:T(8,128)(2,1)}), bf16[16,336,128]{2,1,0:T(8,128)(2,1)S(1)}, u32[]{:S(2)}, u32[]{:S(2)}) %all-to-all-start.3) | async-done | bytes 1376288 | tf_op jit(solution)/shard_map/all_to_all | solution.py:347
  103.3 0.0 copy-start
  103.3 3.6 %all-to-all-start.1 = ((bf16[8,552,128]{2,1,0:T(8,128)(2,1)}), bf16[8,552,128]{2,1,0:T(8,128)(2,1)S(1)}, u32[]{:S(2)}, u32[]{:S(2)}) async-start(bf16[8,552,128]{2,1,0:T(8,128)(2,1)} %z_term.1), calls=%async_computation.1 | async-start | bytes 2260992 | tf_op jit(solution)/shard_map/all_to_all | solution.py:339
  106.9 5.3 %x_term.1.base = f32[5,12,24,384]{3,2,1,0:T(8,128)} custom-call(f32[5]{0:T(128)} %coef.5, bf16[5,12,24,384]{3,2,1,0:T(8,128)(2,1)} %bitcast.8, bf16[5,12,24,384]{3,2,1,0:T(8,128)(2,1)} %bitcast.11, bf16[12,24,384]{2,1,0:T(8,128)(2,1)} %adv.3, bf16[2,384,384]{2,1,0:T(8,128)(2,1)} %mat.3), custom_call_target="tpu_custom_call" | custom-call | tf_op jit(solution)/shard_map/x_term/pallas_call | solution.py:333
  112.2 0.0 copy-done
  112.2 25.6 %all-to-all-done.1.back_z = bf16[8,552,128]{2,1,0:T(8,128)(2,1)S(1)} async-done(((bf16[8,552,128]{2,1,0:T(8,128)(2,1)}), bf16[8,552,128]{2,1,0:T(8,128)(2,1)S(1)}, u32[]{:S(2)}, u32[]{:S(2)}) %all-to-all-start.1) | async-done | bytes 1130528 | tf_op jit(solution)/shard_map/all_to_all | solution.py:339
  137.8 0.0 copy-start.3
  137.8 1.0 copy-done.3
  138.8 6.2 %join.1 = (bf16[5,12,24,384]{3,2,1,0:T(8,128)(2,1)}, bf16[90,24,128]{2,1,0:T(8,128)(2,1)}, bf16[90,24,128]{2,1,0:T(8,128)(2,1)}) custom-call(s32[1]{0:T(128)} %bitcast.probe, f32[5,12,24,384]{3,2,1,0:T(8,128)} %x_term.1.base, bf16[8,552,128]{2,1,0:T(8,128)(2,1)} %copy-done.3, bf16[8,2,336,128]{3,2,1,0:T(8,128)(2,1)} %bitcast.9), custom_call_target="tpu_custom_call" | custom-call | tf_op jit(solution)/shard_map/join/pallas_call | solution.py:348
  144.9 0.4 collective-permute-start
  145.3 13.4 %collective-permute-done.recv = bf16[90,24,128]{2,1,0:T(8,128)(2,1)S(1)} collective-permute-done((bf16[90,24,128]{2,1,0:T(8,128)(2,1)}, bf16[90,24,128]{2,1,0:T(8,128)(2,1)S(1)}, u32[]{:S(2)}, u32[]{:S(2)}) %collective-permute-start) | collective-permute-done | bytes 552992 | tf_op jit(solution)/shard_map/ppermute | solution.py:355
  158.7 0.0 copy-start.4
  158.8 0.8 copy-done.4
  159.6 5.4 %sketch.1 = bf16[2,5,12,24,192]{4,3,2,1,0:T(8,128)(2,1)} custom-call(s32[1]{0:T(128)} %bitcast.probe, f32[2,2]{1,0:T(2,128)} %mix.1, bf16[90,24,128]{2,1,0:T(8,128)(2,1)} %get-tuple-element.6.own, bf16[90,24,128]{2,1,0:T(8,128)(2,1)} %copy-done.4), custom_call_target="tpu_custom_call" | custom-call | tf_op jit(solution)/shard_map/sketch/pallas_call | solution.py:356
Async XLA Ops:
  3.7 29.1 %all-to-all-start.2 = ((bf16[16,336,128]{2,1,0:T(8,128)(2,1)}), bf16[16,336,128]{2,1,0:T(8,128)(2,1)S(1)}, u32[]{:S(2)}, u32[]{:S(2)}) async-start(bf16[16,336,128]{2,1,0:T(8,128)(2,1)} %bitcast.10), calls=%async_computation.2 | async-start | bytes 2752512 | tf_op jit(solution)/shard_map/all_to_all | solution.py:330
  32.8 1.1 copy-start.1
  33.8 43.3 %all-to-all-start = ((bf16[8,648,128]{2,1,0:T(8,128)(2,1)}), bf16[8,648,128]{2,1,0:T(8,128)(2,1)S(1)}, u32[]{:S(2)}, u32[]{:S(2)}) async-start(bf16[8,648,128]{2,1,0:T(8,128)(2,1)} %z_pack.1), calls=%async_computation | async-start | bytes 2654208 | tf_op jit(solution)/shard_map/all_to_all | solution.py:328
  77.2 1.1 copy-start.2
  78.2 25.1 %all-to-all-start.3 = ((bf16[16,336,128]{2,1,0:T(8,128)(2,1)}), bf16[16,336,128]{2,1,0:T(8,128)(2,1)S(1)}, u32[]{:S(2)}, u32[]{:S(2)}) async-start(bf16[16,336,128]{2,1,0:T(8,128)(2,1)} %y_term.1), calls=%async_computation.3 | async-start | bytes 2752512 | tf_op jit(solution)/shard_map/all_to_all | solution.py:347
  103.3 8.8 %copy-start = (bf16[16,336,128]{2,1,0:T(8,128)(2,1)}, bf16[16,336,128]{2,1,0:T(8,128)(2,1)S(1)}, u32[]{:S(2)}) copy-start(bf16[16,336,128]{2,1,0:T(8,128)(2,1)S(1)} %all-to-all-done.3) | copy-start | bytes 4128772
  103.3 34.4 %all-to-all-start.1 = ((bf16[8,552,128]{2,1,0:T(8,128)(2,1)}), bf16[8,552,128]{2,1,0:T(8,128)(2,1)S(1)}, u32[]{:S(2)}, u32[]{:S(2)}) async-start(bf16[8,552,128]{2,1,0:T(8,128)(2,1)} %z_term.1), calls=%async_computation.1 | async-start | bytes 2260992 | tf_op jit(solution)/shard_map/all_to_all | solution.py:339
  137.8 1.0 copy-start.3
  144.9 13.8 %collective-permute-start = (bf16[90,24,128]{2,1,0:T(8,128)(2,1)}, bf16[90,24,128]{2,1,0:T(8,128)(2,1)S(1)}, u32[]{:S(2)}, u32[]{:S(2)}) collective-permute-start(bf16[90,24,128]{2,1,0:T(8,128)(2,1)} %get-tuple-element.7), channel_id=1, source_target_pairs={{0,128},{128,0},{1,129},{129,1},{2,130},{130,2},{3,131},{131,3},{4... | collective-permute-start | bytes 1658888 | tf_op jit(solution)/shard_map/ppermute | solution.py:355
  158.7 0.8 copy-start.4
where the time goes:
time: 165 us
  waiting for transfers between devices  103 us (62%)
  Pallas kernels  31.9 us (19%)
  starting transfers between devices  25 us (15%)
  local copies, waits for them, and re-layouts  3.95 us (2%)
    all_to_all x1, waiting for transfers between devices, on_device(): at_z = lax.all_to_all(to_z, 'col', split_axis=0, concat_axis=0, tiled=True)  29.1 us
    all_to_all x1, waiting for transfers between devices, on_device(): lax.all_to_all(term_z, 'col', split_axis=0, concat_axis=0, tiled=True)  25.6 us
    all_to_all x1, waiting for transfers between devices, on_device(): lax.all_to_all(to_y.reshape(16, 336, 128), 'row', split_axis=0, concat_ax...  17.9 us
    all_to_all x1, waiting for transfers between devices, on_device(): lax.all_to_all(term_y, 'row', split_axis=0, concat_axis=0, tiled=True)  17.5 us
    ppermute x1, waiting for transfers between devices, on_device(): recv = lax.ppermute(send, 'probe', [(0, 1), (1, 0)])  13.4 us
    all_to_all x1, starting transfers between devices, on_device(): lax.all_to_all(to_y.reshape(16, 336, 128), 'row', split_axis=0, concat_ax...  8.44 us
    all_to_all x1, starting transfers between devices, on_device(): at_z = lax.all_to_all(to_z, 'col', split_axis=0, concat_axis=0, tiled=True)  8.19 us
    pallas_call x1, Pallas kernels, on_device(): call(join_kernel, [shape((5, 12, 24, 384)), shape((90, 24, 128)), shape((...  6.15 us
  transfers between devices with their start and end apart: 5, of which 5 were waited for; matrix products, arithmetic and copies ran while one was open for 0% of the time, Pallas kernels for 10%

commit v1 on v0

--- a/solution.py
+++ b/solution.py
@@ -6,9 +6,10 @@
 from jax.experimental.pallas import tpu as pltpu
 from jax.sharding import PartitionSpec as P
 
+
 step_size = 0.25
 
-VMEM = pltpu.VMEM
+
 F32 = jnp.float32
 BF16 = jnp.bfloat16
 
@@ -36,22 +37,36 @@
     return jnp.where(low, swap(first), second)
 
 
-def z_pack_kernel(state, adv, out):
-    def body(a, carry):
-        for yl in range(3):
-            y = 3 * a + yl
-            rows = [state[v, y].astype(F32) for v in range(5)] + [adv[y].astype(F32)]
-            for b in range(2):
+def z_pack_kernel(col, state, adv, *outs):
+    me = col[0]
+    for r in range(8):
+        dest = lax.rem(me + r, 8)
+        a = dest // 2
+
+        def fill(b, r=r, a=a):
+            def body(yl, carry):
+                y = 3 * a + yl
+                base = pl.multiple_of(yl * 216, 8)
+                full = slice(256 * b, 256 * b + 128)
                 for u in range(6):
-                    at = yl * 216 + 24 * u
-                    out[2 * a + b, at : at + 24, :] = rows[u][:, 256 * b : 256 * b + 128].astype(BF16)
+                    src = state[u, y, :, full] if u < 5 else adv[y, :, full]
+                    outs[r][pl.ds(base + 24 * u, 24), :] = src
+                mid = [state[u, y, :, 128:256].astype(F32) for u in range(5)]
+                mid.append(adv[y, :, 128:256].astype(F32))
                 for q in range(3):
-                    at = yl * 216 + 144 + 24 * q
-                    tile = merge(b, rows[2 * q][:, 128:256], rows[2 * q + 1][:, 128:256])
-                    out[2 * a + b, at : at + 24, :] = tile.astype(BF16)
-        return carry
-
-    lax.fori_loop(0, 4, body, 0)
+                    tile = merge(b, mid[2 * q], mid[2 * q + 1])
+                    outs[r][pl.ds(base + 144 + 24 * q, 24), :] = tile.astype(BF16)
+                return carry
+
+            lax.fori_loop(0, 3, body, 0)
+
+        @pl.when(lax.rem(dest, 2) == 0)
+        def _():
+            fill(0)
+
+        @pl.when(lax.rem(dest, 2) == 1)
+        def _():
+            fill(1)
 
 
 def y_pack_kernel(state, adv, out):
@@ -92,16 +107,31 @@
             out[v, ys] = (field + step_size * (term + frc)).reshape(6, 24, 384)
 
 
-def z_kernel(coef, recv, mat, out):
-    lhs = mat[...].reshape(384, 192)
+def z_kernel(col, coef, *refs):
+    recv, mat, outs = refs[:8], refs[8], refs[9:]
+    me = col[0]
     low = low_lanes((192, 128))
+    point = lax.broadcasted_iota(jnp.int32, (192, 192), 0)
+    place = lax.broadcasted_iota(jnp.int32, (192, 192), 1)
+    block = jnp.zeros((192, 192), jnp.int32)
+    for r in range(8):
+        inside = (place >= 24 * r) & (place < 24 * r + 24)
+        block = jnp.where(inside, 24 * lax.rem(me - r + 8, 8) - 24 * r, block)
+    order = jnp.where(point == place + block, 1.0, 0.0).astype(BF16)
+    parts = []
+    for k in range(2):
+        cols = jnp.dot(mat[k], order, preferred_element_type=F32).astype(BF16)
+        rows = lax.dot_general(order, cols, (((0,), (0,)), ((), ())), preferred_element_type=F32)
+        parts.append(rows.astype(BF16))
+    lhs = jnp.concatenate(parts, axis=0)
 
     def tile(yl, t):
         at = yl * 216 + 24 * t
-        return recv[:, at : at + 24, :].astype(F32).reshape(192, 128)
+        return jnp.concatenate([ref[at : at + 24, :].astype(F32) for ref in recv], axis=0)
 
     def put(t, term):
-        out[:, 24 * t : 24 * t + 24, :] = term.reshape(8, 24, 128).astype(BF16)
+        for r in range(8):
+            outs[r][24 * t : 24 * t + 24, :] = term[24 * r : 24 * r + 24].astype(BF16)
 
     tails = []
     for yl in range(3):
@@ -177,8 +207,11 @@
         terms(12 + j, tail[j], coef_of(2))
 
 
-def join_kernel(probe, base, back_z, back_y, out, send, own, work):
+def join_kernel(probe, col, base, back_y, *refs):
+    arrivals, (out, send, own, work, back_z) = refs[:8], refs[8:]
     first = probe[0] == 0
+    for r in range(8):
+        back_z[lax.rem(col[0] + r, 8)] = arrivals[r][...]
 
     def put_lines(c, block):
         work[:, :, 128 * c : 128 * c + 128] = jnp.swapaxes(block, 0, 1)
@@ -280,16 +313,27 @@
     lax.fori_loop(0, 30, body, 0)
 
 
-def call(kernel, out_shapes, specs, scratch=(), name=None):
+def call(kernel, out_shapes, scalars, arrays, scratch=()):
     many = isinstance(out_shapes, (list, tuple))
     return pl.pallas_call(
         kernel,
         out_shape=out_shapes,
-        in_specs=specs,
+        in_specs=[sspec()] * len(scalars) + [vspec()] * len(arrays),
         out_specs=[vspec() for _ in out_shapes] if many else vspec(),
         scratch_shapes=scratch,
-        name=name,
-    )
+        compiler_params=pltpu.CompilerParams(vmem_limit_bytes=24 << 20),
+    )(*scalars, *arrays)
+
+
+def near(x):
+    return pltpu.with_memory_space_constraint(x, pltpu.VMEM)
+
+
+def shift(x, distance):
+    return lax.ppermute(x, "col", [(i, (i + distance) % 8) for i in range(8)])
+
+
+ROUTES = (3, 5, 4, 2, 6, 1, 7)
 
 
 def row_tables():
@@ -317,6 +361,7 @@
     state = flow_state.reshape(5, 12, 24, 384)
     forced = forcing.reshape(5, 12, 24, 384)
     probe = lax.axis_index("probe").astype(jnp.int32).reshape(1)
+    col = lax.axis_index("col").astype(jnp.int32).reshape(1)
     spread, gather = row_tables()
     spread = jnp.asarray(spread, BF16)
     gather = jnp.asarray(gather, BF16)
@@ -324,38 +369,45 @@
     def shape(s, t=BF16):
         return jax.ShapeDtypeStruct(s, t)
 
-    to_z = call(z_pack_kernel, shape((8, 648, 128)), [vspec()] * 2, name="z_pack")(state, advect_z)
-    at_z = lax.all_to_all(to_z, "col", split_axis=0, concat_axis=0, tiled=True)
-    to_y = call(y_pack_kernel, shape((8, 2, 336, 128)), [vspec()] * 2, name="y_pack")(state, advect_y)
+    def held(s, t=BF16):
+        return pltpu.VMEM(s, t)
+
+    to_y = call(y_pack_kernel, held((8, 2, 336, 128)), [], [state, advect_y])
     at_y = lax.all_to_all(
         to_y.reshape(16, 336, 128), "row", split_axis=0, concat_axis=0, tiled=True
     )
+    to_z = call(z_pack_kernel, [held((648, 128))] * 8, [col], [state, advect_z])
+    at_z = list(to_z)
+    for r in ROUTES:
+        at_z[r] = shift(to_z[r], r)
     base = call(
-        x_kernel, shape((5, 12, 24, 384), F32), [sspec()] + [vspec()] * 4, name="x_term"
-    )(diffusivity, state, forced, advect_x, deriv_x)
-    term_z = call(z_kernel, shape((8, 552, 128)), [sspec()] + [vspec()] * 2, name="z_term")(
-        diffusivity, at_z, deriv_z
-    )
-    back_z = lax.all_to_all(term_z, "col", split_axis=0, concat_axis=0, tiled=True)
+        x_kernel, held((5, 12, 24, 384), F32), [diffusivity], [state, forced, advect_x, deriv_x]
+    )
     term_y = call(
         y_terms_kernel,
-        shape((16, 336, 128)),
-        [sspec()] + [vspec()] * 4,
+        held((16, 336, 128)),
+        [diffusivity],
+        [near(at_y), deriv_y, spread, gather],
         [pltpu.VMEM((768, 384), BF16)],
-        name="y_term",
-    )(diffusivity, at_y, deriv_y, spread, gather)
+    )
     back_y = lax.all_to_all(term_y, "row", split_axis=0, concat_axis=0, tiled=True)
+    term_z = call(
+        z_kernel, [held((552, 128))] * 8, [col, diffusivity], [near(x) for x in at_z] + [deriv_z]
+    )
+    back_z = list(term_z)
+    for r in ROUTES:
+        back_z[r] = shift(term_z[r], -r)
     section, send, own = call(
         join_kernel,
-        [shape((5, 12, 24, 384)), shape((90, 24, 128)), shape((90, 24, 128))],
-        [sspec()] + [vspec()] * 3,
-        [pltpu.VMEM((24, 24, 384), F32)],
-        name="join",
-    )(probe, base, back_z, back_y.reshape(8, 2, 336, 128))
+        [shape((5, 12, 24, 384)), held((90, 24, 128)), held((90, 24, 128))],
+        [probe, col],
+        [near(base), near(back_y.reshape(8, 2, 336, 128))] + [near(x) for x in back_z],
+        [pltpu.VMEM((24, 24, 384), F32), pltpu.VMEM((8, 552, 128), BF16)],
+    )
     recv = lax.ppermute(send, "probe", [(0, 1), (1, 0)])
     sketch = call(
-        sketch_kernel, shape((2, 5, 12, 24, 192)), [sspec()] * 2 + [vspec()] * 2, name="sketch"
-    )(probe, test_mix, own, recv)
+        sketch_kernel, shape((2, 5, 12, 24, 192)), [probe, test_mix], [near(own), near(recv)]
+    )
     return (section[None], sketch)
 
 
@@ -372,6 +424,7 @@
         P(),
         P(),
     )
+
     return jax.shard_map(
         on_device,
         mesh=mesh,

time: 165 us -> 150 us (0.909)
  waiting for transfers between devices: 103 us -> 48.4 us
  blocking collectives: 0 us -> 28.8 us
  starting transfers between devices: 25 us -> 38.8 us
  Pallas kernels: 31.9 us -> 22.8 us
  local copies, waits for them, and re-layouts: 3.95 us -> 9.2 us
    all_to_all x3 -> x0, waiting for transfers between devices: 72.5 us -> none  [the longest x1 29.1 us: on_device(): at_z = lax.all_to_all(to_z, 'col', split_axis=0, concat_axis=0, tiled=True)]
    ppermute x0 -> x14, waiting for transfers between devices: none -> 35.7 us  [shift(): return lax.ppermute(x, 'col', [(i, (i + distance) % 8) for i in range(8)])]
    ppermute x0 -> x14, starting transfers between devices: none -> 33.1 us  [shift(): return lax.ppermute(x, 'col', [(i, (i + distance) % 8) for i in range(8)])]
    all_to_all x0 -> x1, blocking collectives: none -> 28.8 us  [on_device(): lax.all_to_all(to_y.reshape(16, 336, 128), 'row', split_axis=0, concat_ax...]
    all_to_all x3 -> x0, starting transfers between devices: 20.2 us -> none  [the longest x1 8.44 us: on_device(): lax.all_to_all(to_y.reshape(16, 336, 128), 'row', split_axis=0, concat_ax...]
    all_to_all x1, waiting for transfers between devices: 17.5 us -> 0.01 us  [on_device(): lax.all_to_all(term_y, 'row', split_axis=0, concat_axis=0, tiled=True)]
    pallas_call x7, Pallas kernels: 31.9 us -> 22.8 us  [call(): pl.pallas_call(kernel, out_shape=out_shapes, in_specs=[sspec()] * len(sca...]
    unnamed x10 -> x38, local copies, waits for them, and re-layouts: 3.95 us -> 9.2 us
  transfers between devices with their start and end apart: 5 -> 16, of which waited for: 5 -> 8; matrix products, arithmetic and copies ran while one was open for 0% -> 0% of each run, Pallas kernels for 10% -> 5%
where the time goes in v1:
time: 150 us; the launch traced here: 149 us
  waiting for transfers between devices  48.4 us (32%)
  starting transfers between devices  38.8 us (26%)
  blocking collectives  28.8 us (19%)
  Pallas kernels  22.8 us (15%)
  local copies, waits for them, and re-layouts  9.2 us (6%)
    ppermute x14, waiting for transfers between devices, shift(): return lax.ppermute(x, 'col', [(i, (i + distance) % 8) for i in range(8)])  35.7 us
    ppermute x14, starting transfers between devices, shift(): return lax.ppermute(x, 'col', [(i, (i + distance) % 8) for i in range(8)])  33.1 us
    all_to_all x1, blocking collectives, on_device(): lax.all_to_all(to_y.reshape(16, 336, 128), 'row', split_axis=0, concat_ax...  28.8 us
    pallas_call x7, Pallas kernels, call(): pl.pallas_call(kernel, out_shape=out_shapes, in_specs=[sspec()] * len(sca...  22.8 us
    ppermute x1, waiting for transfers between devices, on_device(): recv = lax.ppermute(send, 'probe', [(0, 1), (1, 0)])  12.7 us
    unnamed x38, local copies, waits for them, and re-layouts  9.2 us
    all_to_all x1, starting transfers between devices, on_device(): lax.all_to_all(term_y, 'row', split_axis=0, concat_axis=0, tiled=True)  5.4 us
  transfers between devices with their start and end apart: 16, of which 8 were waited for; matrix products, arithmetic and copies ran while one was open for 0% of the time, Pallas kernels for 5%

profile of v1, /device:TPU:1, one launch (start us, length us, event | category | flops | bytes accessed | tf_op | source)
XLA Modules:
  0.0 148.7 jit_solution(1124087219740781571)
XLA Ops:
  0.6 0.0 copy-start
  0.6 1.2 copy-done
  1.9 0.9 copy-done.7
  2.8 0.7 shard_map.132
  3.6 0.0 copy-start.4
  3.6 0.0 copy-start.5
  3.6 0.0 copy-start.10
  3.6 0.0 copy-start.17
  3.6 28.8 %all_to_all.10.recv = bf16[16,336,128]{2,1,0:T(8,128)(2,1)S(1)} all-to-all(bf16[16,336,128]{2,1,0:T(8,128)(2,1)S(1)} %bitcast.10), channel_id=1, replica_groups=mesh['probe'=2,'row'=16,'col'=8] {'row'}, dimensions={0} | all-to-all | bytes 2752512 | tf_op jit(solution)/shard_map/all_to_all | solution.py:376
  32.4 5.0 %shard_map.133 = bf16[16,336,128]{2,1,0:T(8,128)(2,1)} custom-call(f32[5]{0:T(128)S(1)} %copy-done.17, bf16[16,336,128]{2,1,0:T(8,128)(2,1)S(1)} %all_to_all.10.recv, bf16[2,192,192]{2,1,0:T(8,128)(2,1)S(1)} %copy-done.10, bf16[2,384,192]{2,1,0:T(8,128)(2,1)S(1)} %copy-done.4, bf16[384,384]{1,0:T(8,128)(2,1)S(1)} %copy-done.5), custom_call_target="tpu_custom_call" | custom-call | tf_op jit(solution)/shard_map/pallas_call | solution.py:318
  37.4 5.4 %all-to-all-start.1 = ((bf16[16,336,128]{2,1,0:T(8,128)(2,1)}), bf16[16,336,128]{2,1,0:T(8,128)(2,1)}, u32[]{:S(2)}, u32[]{:S(2)}) async-start(bf16[16,336,128]{2,1,0:T(8,128)(2,1)} %shard_map.133), calls=%async_computation.1 | async-start | bytes 2752512 | tf_op jit(solution)/shard_map/all_to_all | solution.py:393
  42.8 0.0 copy-start.8
  42.9 1.9 %shard_map.134 = (bf16[648,128]{1,0:T(8,128)(2,1)S(1)}, bf16[648,128]{1,0:T(8,128)(2,1)S(1)}, bf16[648,128]{1,0:T(8,128)(2,1)S(1)}, bf16[648,128]{1,0:T(8,128)(2...) custom-call(s32[1]{0:T(128)} %bitcast.1.col, ...), custom_call_target="tpu_custom_call" | custom-call | tf_op jit(solution)/shard_map/pallas_call | solution.py:318
  44.8 1.7 %collective-permute-start = (bf16[648,128]{1,0:T(8,128)(2,1)S(1)}, bf16[648,128]{1,0:T(8,128)(2,1)S(1)}, u32[]{:S(2)}, u32[]{:S(2)}) collective-permute-start(bf16[648,128]{1,0:T(8,128)(2,1)S(1)} %get-tuple-element.22), channel_id=1, source_target_pairs={{0,1},{1,2},{2,3},{3,4},{4,5},{5,6},{6,7},{7,0},{8,9},{9,10},{10,1... | collective-permute-start | bytes 497672 | tf_op jit(solution)/shard_map/ppermute | solution.py:333
  46.5 3.0 %collective-permute-start.1 = (bf16[648,128]{1,0:T(8,128)(2,1)S(1)}, bf16[648,128]{1,0:T(8,128)(2,1)S(1)}, u32[]{:S(2)}, u32[]{:S(2)}) collective-permute-start(bf16[648,128]{1,0:T(8,128)(2,1)S(1)} %get-tuple-element.23), channel_id=1, source_target_pairs={{0,2},{1,3},{2,4},{3,5},{4,6},{5,7},{6,0},{7,1},{8,10},{9,11},{10,... | collective-permute-start | bytes 497672 | tf_op jit(solution)/shard_map/ppermute | solution.py:333
  49.5 3.7 %collective-permute-start.2 = (bf16[648,128]{1,0:T(8,128)(2,1)S(1)}, bf16[648,128]{1,0:T(8,128)(2,1)S(1)}, u32[]{:S(2)}, u32[]{:S(2)}) collective-permute-start(bf16[648,128]{1,0:T(8,128)(2,1)S(1)} %get-tuple-element.24), channel_id=1, source_target_pairs={{0,3},{1,4},{2,5},{3,6},{4,7},{5,0},{6,1},{7,2},{8,11},{9,12},{10,... | collective-permute-start | bytes 497672 | tf_op jit(solution)/shard_map/ppermute | solution.py:333
  53.2 0.5 collective-permute-start.3
  53.7 4.5 %collective-permute-start.4 = (bf16[648,128]{1,0:T(8,128)(2,1)S(1)}, bf16[648,128]{1,0:T(8,128)(2,1)S(1)}, u32[]{:S(2)}, u32[]{:S(2)}) collective-permute-start(bf16[648,128]{1,0:T(8,128)(2,1)S(1)} %get-tuple-element.26), channel_id=1, source_target_pairs={{0,5},{1,6},{2,7},{3,0},{4,1},{5,2},{6,3},{7,4},{8,13},{9,14},{10,... | collective-permute-start | bytes 497672 | tf_op jit(solution)/shard_map/ppermute | solution.py:333
  58.2 0.0 collective-permute-done.refs_1_
  58.2 2.4 %collective-permute-start.5 = (bf16[648,128]{1,0:T(8,128)(2,1)S(1)}, bf16[648,128]{1,0:T(8,128)(2,1)S(1)}, u32[]{:S(2)}, u32[]{:S(2)}) collective-permute-start(bf16[648,128]{1,0:T(8,128)(2,1)S(1)} %get-tuple-element.27), channel_id=1, source_target_pairs={{0,6},{1,7},{2,0},{3,1},{4,2},{5,3},{6,4},{7,5},{8,14},{9,15},{10,... | collective-permute-start | bytes 497672 | tf_op jit(solution)/shard_map/ppermute | solution.py:333
  60.6 3.9 %collective-permute-start.6 = (bf16[648,128]{1,0:T(8,128)(2,1)S(1)}, bf16[648,128]{1,0:T(8,128)(2,1)S(1)}, u32[]{:S(2)}, u32[]{:S(2)}) collective-permute-start(bf16[648,128]{1,0:T(8,128)(2,1)S(1)} %get-tuple-element.28), channel_id=1, source_target_pairs={{0,7},{1,0},{2,1},{3,2},{4,3},{5,4},{6,5},{7,6},{8,15},{9,8},{10,9... | collective-permute-start | bytes 497672 | tf_op jit(solution)/shard_map/ppermute | solution.py:333
  64.5 8.5 %collective-permute-done.2.refs_3_ = bf16[648,128]{1,0:T(8,128)(2,1)S(1)} collective-permute-done((bf16[648,128]{1,0:T(8,128)(2,1)S(1)}, bf16[648,128]{1,0:T(8,128)(2,1)S(1)}, u32[]{:S(2)}, u32[]{:S(2)}) %collective-permute-start.2) | collective-permute-done | bytes 165920 | tf_op jit(solution)/shard_map/ppermute | solution.py:333
  73.0 2.9 %collective-permute-done.3.refs_4_ = bf16[648,128]{1,0:T(8,128)(2,1)S(1)} collective-permute-done((bf16[648,128]{1,0:T(8,128)(2,1)S(1)}, bf16[648,128]{1,0:T(8,128)(2,1)S(1)}, u32[]{:S(2)}, u32[]{:S(2)}) %collective-permute-start.3) | collective-permute-done | bytes 165920 | tf_op jit(solution)/shard_map/ppermute | solution.py:333
  75.8 7.8 %collective-permute-done.5.refs_6_ = bf16[648,128]{1,0:T(8,128)(2,1)S(1)} collective-permute-done((bf16[648,128]{1,0:T(8,128)(2,1)S(1)}, bf16[648,128]{1,0:T(8,128)(2,1)S(1)}, u32[]{:S(2)}, u32[]{:S(2)}) %collective-permute-start.5) | collective-permute-done | bytes 165920 | tf_op jit(solution)/shard_map/ppermute | solution.py:333
  83.7 0.8 collective-permute-done.6.refs_7_
  84.5 2.5 %shard_map.135 = (bf16[552,128]{1,0:T(8,128)(2,1)S(1)}, bf16[552,128]{1,0:T(8,128)(2,1)S(1)}, bf16[552,128]{1,0:T(8,128)(2,1)S(1)}, bf16[552,128]{1,0:T(8,128)(2...) custom-call(s32[1]{0:T(128)} %bitcast.1.col, ...), custom_call_target="tpu_custom_call" | custom-call | tf_op jit(solution)/shard_map/pallas_call | solution.py:318
  87.0 0.6 copy-done.11
  87.6 2.7 %collective-permute-start.7 = (bf16[552,128]{1,0:T(8,128)(2,1)S(1)}, bf16[552,128]{1,0:T(8,128)(2,1)S(1)}, u32[]{:S(2)}, u32[]{:S(2)}) collective-permute-start(bf16[552,128]{1,0:T(8,128)(2,1)S(1)} %get-tuple-element.30), channel_id=1, source_target_pairs={{0,7},{1,0},{2,1},{3,2},{4,3},{5,4},{6,5},{7,6},{8,15},{9,8},{10,9... | collective-permute-start | bytes 423944 | tf_op jit(solution)/shard_map/ppermute | solution.py:333
  90.3 0.9 collective-permute-start.8
  91.2 3.0 %collective-permute-start.9 = (bf16[552,128]{1,0:T(8,128)(2,1)}, bf16[552,128]{1,0:T(8,128)(2,1)}, u32[]{:S(2)}, u32[]{:S(2)}) collective-permute-start(bf16[552,128]{1,0:T(8,128)(2,1)} %get-tuple-element.32), channel_id=1, source_target_pairs={{0,5},{1,6},{2,7},{3,0},{4,1},{5,2},{6,3},{7,4},{8,13},{9,14},{10,... | collective-permute-start | bytes 423944 | tf_op jit(solution)/shard_map/ppermute | solution.py:333
  94.2 1.5 %collective-permute-start.10 = (bf16[552,128]{1,0:T(8,128)(2,1)}, bf16[552,128]{1,0:T(8,128)(2,1)}, u32[]{:S(2)}, u32[]{:S(2)}) collective-permute-start(bf16[552,128]{1,0:T(8,128)(2,1)} %get-tuple-element.33), channel_id=1, source_target_pairs={{0,4},{1,5},{2,6},{3,7},{4,0},{5,1},{6,2},{7,3},{8,12},{9,13},{10,... | collective-permute-start | bytes 423944 | tf_op jit(solution)/shard_map/ppermute | solution.py:333
  95.8 3.3 %collective-permute-start.11 = (bf16[552,128]{1,0:T(8,128)(2,1)}, bf16[552,128]{1,0:T(8,128)(2,1)}, u32[]{:S(2)}, u32[]{:S(2)}) collective-permute-start(bf16[552,128]{1,0:T(8,128)(2,1)} %get-tuple-element.34), channel_id=1, source_target_pairs={{0,3},{1,4},{2,5},{3,6},{4,7},{5,0},{6,1},{7,2},{8,11},{9,12},{10,... | collective-permute-start | bytes 423944 | tf_op jit(solution)/shard_map/ppermute | solution.py:333
  99.0 0.6 copy-done.13
  99.7 2.0 %collective-permute-start.12 = (bf16[552,128]{1,0:T(8,128)(2,1)}, bf16[552,128]{1,0:T(8,128)(2,1)}, u32[]{:S(2)}, u32[]{:S(2)}) collective-permute-start(bf16[552,128]{1,0:T(8,128)(2,1)} %get-tuple-element.35), channel_id=1, source_target_pairs={{0,2},{1,3},{2,4},{3,5},{4,6},{5,7},{6,0},{7,1},{8,10},{9,11},{10,... | collective-permute-start | bytes 423944 | tf_op jit(solution)/shard_map/ppermute | solution.py:333
  101.7 2.2 %collective-permute-done.8.refs_2_ = bf16[552,128]{1,0:T(8,128)(2,1)S(1)} collective-permute-done((bf16[552,128]{1,0:T(8,128)(2,1)S(1)}, bf16[552,128]{1,0:T(8,128)(2,1)S(1)}, u32[]{:S(2)}, u32[]{:S(2)}) %collective-permute-start.8) | collective-permute-done | bytes 141344 | tf_op jit(solution)/shard_map/ppermute | solution.py:333
  104.0 0.6 copy-done.15
  104.6 1.2 copy-done.2
  105.8 1.1 copy-done.3
  106.9 2.8 %shard_map.131.base = f32[5,12,24,384]{3,2,1,0:T(8,128)S(1)} custom-call(f32[5]{0:T(128)S(1)} %copy-done.17, bf16[5,12,24,384]{3,2,1,0:T(8,128)(2,1)S(1)} %bitcast.9, bf16[5,12,24,384]{3,2,1,0:T(8,128)(2,1)S(1)} %bitcast.11, bf16[12,24,384]{2,1,0:T(8,128)(2,1)S(1)} %copy-done.8, bf16[2,384,384]{2,1,0:T(8,128)(2,1)S(1)} %copy-done.3), custom_call_target="tpu_custom_call" | custom-call | tf_op jit(solution)/shard_map/pallas_call | solution.py:318
  109.7 7.3 %collective-permute-done.11.refs_5_ = bf16[552,128]{1,0:T(8,128)(2,1)} collective-permute-done((bf16[552,128]{1,0:T(8,128)(2,1)}, bf16[552,128]{1,0:T(8,128)(2,1)}, u32[]{:S(2)}, u32[]{:S(2)}) %collective-permute-start.11) | collective-permute-done | bytes 141344 | tf_op jit(solution)/shard_map/ppermute | solution.py:333
  117.0 6.2 %collective-permute-done.13.refs_7_ = bf16[552,128]{1,0:T(8,128)(2,1)} collective-permute-done((bf16[552,128]{1,0:T(8,128)(2,1)}, bf16[552,128]{1,0:T(8,128)(2,1)}, u32[]{:S(2)}, u32[]{:S(2)}) %collective-permute-start.13) | collective-permute-done | bytes 141344 | tf_op jit(solution)/shard_map/ppermute | solution.py:333
  123.2 0.9 copy-done.12
  124.1 0.9 copy-done.14
  125.0 0.9 copy-done.16
  125.9 5.1 %shard_map.136 = (bf16[5,12,24,384]{3,2,1,0:T(8,128)(2,1)}, bf16[90,24,128]{2,1,0:T(8,128)(2,1)S(1)}, bf16[90,24,128]{2,1,0:T(8,128)(2,1)S(1)}) custom-call(s32[1]{0:T(128)} %bitcast.probe, s32[1]{0:T(128)} %bitcast.1.col, f32[5,12,24,384]{3,2,1,0:T(8,128)S(1)} %shard_map.131.base, bf16[8,2,336,128]{3,2,1,0:T(8,128)(2,1)} %bitcast.5.back_y, ...), custom_call_target="tpu_custom_call" | custom-call | tf_op jit(solution)/shard_map/pallas_call | solution.py:318
  131.0 0.3 collective-permute-start.14
  131.3 12.7 %collective-permute-done.14.recv = bf16[90,24,128]{2,1,0:T(8,128)(2,1)S(1)} collective-permute-done((bf16[90,24,128]{2,1,0:T(8,128)(2,1)S(1)}, bf16[90,24,128]{2,1,0:T(8,128)(2,1)S(1)}, u32[]{:S(2)}, u32[]{:S(2)}) %collective-permute-start.14) | collective-permute-done | bytes 552992 | tf_op jit(solution)/shard_map/ppermute | solution.py:407
  144.0 4.7 %shard_map.137 = bf16[2,5,12,24,192]{4,3,2,1,0:T(8,128)(2,1)} custom-call(s32[1]{0:T(128)} %bitcast.probe, f32[2,2]{1,0:T(2,128)S(1)} %copy-done.18, bf16[90,24,128]{2,1,0:T(8,128)(2,1)S(1)} %get-tuple-element.38.own, bf16[90,24,128]{2,1,0:T(8,128)(2,1)S(1)} %collective-permute-done.14.recv), custom_call_target="tpu_custom_call" | custom-call | tf_op jit(solution)/shard_map/pallas_call | solution.py:318
  (30 shorter events, 0.1 us)
Async XLA Ops:
  0.6 1.2 copy-start
  1.9 0.9 copy-start.7
  3.6 28.8 %copy-start.4 = (bf16[2,384,192]{2,1,0:T(8,128)(2,1)S(1)}, bf16[2,384,192]{2,1,0:T(8,128)(2,1)}, u32[]{:S(2)}) copy-start(bf16[2,384,192]{2,1,0:T(8,128)(2,1)} %constant.13.clone.spread) | copy-start | bytes 884740
  3.6 28.8 %copy-start.5 = (bf16[384,384]{1,0:T(8,128)(2,1)S(1)}, bf16[384,384]{1,0:T(8,128)(2,1)}, u32[]{:S(2)}) copy-start(bf16[384,384]{1,0:T(8,128)(2,1)} %constant.14.clone.gather) | copy-start | bytes 884740
  3.6 28.8 %copy-start.10 = (bf16[2,192,192]{2,1,0:T(8,128)(2,1)S(1)}, bf16[2,192,192]{2,1,0:T(8,128)(2,1)}, u32[]{:S(2)}) copy-start(bf16[2,192,192]{2,1,0:T(8,128)(2,1)} %mat.3) | copy-start | bytes 442372
  3.6 28.8 %copy-start.17 = (f32[5]{0:T(128)S(1)}, f32[5]{0:T(128)}, u32[]{:S(2)}) copy-start(f32[5]{0:T(128)} %coef.5) | copy-start | bytes 64
  37.4 5.4 %copy-start.1 = (bf16[1,5,12,24,384]{4,3,2,1,0:T(8,128)(2,1)S(1)}, bf16[1,5,12,24,384]{4,3,2,1,0:T(8,128)(2,1)}, u32[]{:S(2)}) copy-start(bf16[1,5,12,24,384]{4,3,2,1,0:T(8,128)(2,1)} %param.12) | copy-start | bytes 3317764
  37.4 5.4 %copy-start.6 = (bf16[12,24,384]{2,1,0:T(8,128)(2,1)S(1)}, bf16[12,24,384]{2,1,0:T(8,128)(2,1)}, u32[]{:S(2)}) copy-start(bf16[12,24,384]{2,1,0:T(8,128)(2,1)} %adv.5) | copy-start | bytes 663556
  37.4 47.0 %copy-start.9 = (bf16[2,192,192]{2,1,0:T(8,128)(2,1)S(1)}, bf16[2,192,192]{2,1,0:T(8,128)(2,1)}, u32[]{:S(2)}) copy-start(bf16[2,192,192]{2,1,0:T(8,128)(2,1)} %refs_8_.1) | copy-start | bytes 442372
  37.4 85.7 %all-to-all-start.1 = ((bf16[16,336,128]{2,1,0:T(8,128)(2,1)}), bf16[16,336,128]{2,1,0:T(8,128)(2,1)}, u32[]{:S(2)}, u32[]{:S(2)}) async-start(bf16[16,336,128]{2,1,0:T(8,128)(2,1)} %shard_map.133), calls=%async_computation.1 | async-start | bytes 2752512 | tf_op jit(solution)/shard_map/all_to_all | solution.py:393
  42.8 61.8 %copy-start.8 = (bf16[12,24,384]{2,1,0:T(8,128)(2,1)S(1)}, bf16[12,24,384]{2,1,0:T(8,128)(2,1)}, u32[]{:S(2)}) copy-start(bf16[12,24,384]{2,1,0:T(8,128)(2,1)} %adv.3) | copy-start | bytes 663556
  44.8 13.4 %collective-permute-start = (bf16[648,128]{1,0:T(8,128)(2,1)S(1)}, bf16[648,128]{1,0:T(8,128)(2,1)S(1)}, u32[]{:S(2)}, u32[]{:S(2)}) collective-permute-start(bf16[648,128]{1,0:T(8,128)(2,1)S(1)} %get-tuple-element.22), channel_id=1, source_target_pairs={{0,1},{1,2},{2,3},{3,4},{4,5},{5,6},{6,7},{7,0},{8,9},{9,10},{10,1... | collective-permute-start | bytes 497672 | tf_op jit(solution)/shard_map/ppermute | solution.py:333
  46.5 14.1 %collective-permute-start.1 = (bf16[648,128]{1,0:T(8,128)(2,1)S(1)}, bf16[648,128]{1,0:T(8,128)(2,1)S(1)}, u32[]{:S(2)}, u32[]{:S(2)}) collective-permute-start(bf16[648,128]{1,0:T(8,128)(2,1)S(1)} %get-tuple-element.23), channel_id=1, source_target_pairs={{0,2},{1,3},{2,4},{3,5},{4,6},{5,7},{6,0},{7,1},{8,10},{9,11},{10,... | collective-permute-start | bytes 497672 | tf_op jit(solution)/shard_map/ppermute | solution.py:333
  49.5 23.5 %collective-permute-start.2 = (bf16[648,128]{1,0:T(8,128)(2,1)S(1)}, bf16[648,128]{1,0:T(8,128)(2,1)S(1)}, u32[]{:S(2)}, u32[]{:S(2)}) collective-permute-start(bf16[648,128]{1,0:T(8,128)(2,1)S(1)} %get-tuple-element.24), channel_id=1, source_target_pairs={{0,3},{1,4},{2,5},{3,6},{4,7},{5,0},{6,1},{7,2},{8,11},{9,12},{10,... | collective-permute-start | bytes 497672 | tf_op jit(solution)/shard_map/ppermute | solution.py:333
  53.2 22.6 %collective-permute-start.3 = (bf16[648,128]{1,0:T(8,128)(2,1)S(1)}, bf16[648,128]{1,0:T(8,128)(2,1)S(1)}, u32[]{:S(2)}, u32[]{:S(2)}) collective-permute-start(bf16[648,128]{1,0:T(8,128)(2,1)S(1)} %get-tuple-element.25), channel_id=1, source_target_pairs={{0,4},{1,5},{2,6},{3,7},{4,0},{5,1},{6,2},{7,3},{8,12},{9,13},{10,... | collective-permute-start | bytes 497672 | tf_op jit(solution)/shard_map/ppermute | solution.py:333
  53.7 22.1 %collective-permute-start.4 = (bf16[648,128]{1,0:T(8,128)(2,1)S(1)}, bf16[648,128]{1,0:T(8,128)(2,1)S(1)}, u32[]{:S(2)}, u32[]{:S(2)}) collective-permute-start(bf16[648,128]{1,0:T(8,128)(2,1)S(1)} %get-tuple-element.26), channel_id=1, source_target_pairs={{0,5},{1,6},{2,7},{3,0},{4,1},{5,2},{6,3},{7,4},{8,13},{9,14},{10,... | collective-permute-start | bytes 497672 | tf_op jit(solution)/shard_map/ppermute | solution.py:333
  58.2 25.5 %collective-permute-start.5 = (bf16[648,128]{1,0:T(8,128)(2,1)S(1)}, bf16[648,128]{1,0:T(8,128)(2,1)S(1)}, u32[]{:S(2)}, u32[]{:S(2)}) collective-permute-start(bf16[648,128]{1,0:T(8,128)(2,1)S(1)} %get-tuple-element.27), channel_id=1, source_target_pairs={{0,6},{1,7},{2,0},{3,1},{4,2},{5,3},{6,4},{7,5},{8,14},{9,15},{10,... | collective-permute-start | bytes 497672 | tf_op jit(solution)/shard_map/ppermute | solution.py:333
  60.6 23.9 %collective-permute-start.6 = (bf16[648,128]{1,0:T(8,128)(2,1)S(1)}, bf16[648,128]{1,0:T(8,128)(2,1)S(1)}, u32[]{:S(2)}, u32[]{:S(2)}) collective-permute-start(bf16[648,128]{1,0:T(8,128)(2,1)S(1)} %get-tuple-element.28), channel_id=1, source_target_pairs={{0,7},{1,0},{2,1},{3,2},{4,3},{5,4},{6,5},{7,6},{8,15},{9,8},{10,9... | collective-permute-start | bytes 497672 | tf_op jit(solution)/shard_map/ppermute | solution.py:333
  87.0 0.7 copy-start.11
  87.6 11.4 %collective-permute-start.7 = (bf16[552,128]{1,0:T(8,128)(2,1)S(1)}, bf16[552,128]{1,0:T(8,128)(2,1)S(1)}, u32[]{:S(2)}, u32[]{:S(2)}) collective-permute-start(bf16[552,128]{1,0:T(8,128)(2,1)S(1)} %get-tuple-element.30), channel_id=1, source_target_pairs={{0,7},{1,0},{2,1},{3,2},{4,3},{5,4},{6,5},{7,6},{8,15},{9,8},{10,9... | collective-permute-start | bytes 423944 | tf_op jit(solution)/shard_map/ppermute | solution.py:333
  90.3 13.6 %collective-permute-start.8 = (bf16[552,128]{1,0:T(8,128)(2,1)S(1)}, bf16[552,128]{1,0:T(8,128)(2,1)S(1)}, u32[]{:S(2)}, u32[]{:S(2)}) collective-permute-start(bf16[552,128]{1,0:T(8,128)(2,1)S(1)} %get-tuple-element.31), channel_id=1, source_target_pairs={{0,6},{1,7},{2,0},{3,1},{4,2},{5,3},{6,4},{7,5},{8,14},{9,15},{10,... | collective-permute-start | bytes 423944 | tf_op jit(solution)/shard_map/ppermute | solution.py:333
  91.2 18.5 %collective-permute-start.9 = (bf16[552,128]{1,0:T(8,128)(2,1)}, bf16[552,128]{1,0:T(8,128)(2,1)}, u32[]{:S(2)}, u32[]{:S(2)}) collective-permute-start(bf16[552,128]{1,0:T(8,128)(2,1)} %get-tuple-element.32), channel_id=1, source_target_pairs={{0,5},{1,6},{2,7},{3,0},{4,1},{5,2},{6,3},{7,4},{8,13},{9,14},{10,... | collective-permute-start | bytes 423944 | tf_op jit(solution)/shard_map/ppermute | solution.py:333
  94.2 15.5 %collective-permute-start.10 = (bf16[552,128]{1,0:T(8,128)(2,1)}, bf16[552,128]{1,0:T(8,128)(2,1)}, u32[]{:S(2)}, u32[]{:S(2)}) collective-permute-start(bf16[552,128]{1,0:T(8,128)(2,1)} %get-tuple-element.33), channel_id=1, source_target_pairs={{0,4},{1,5},{2,6},{3,7},{4,0},{5,1},{6,2},{7,3},{8,12},{9,13},{10,... | collective-permute-start | bytes 423944 | tf_op jit(solution)/shard_map/ppermute | solution.py:333
  95.8 21.3 %collective-permute-start.11 = (bf16[552,128]{1,0:T(8,128)(2,1)}, bf16[552,128]{1,0:T(8,128)(2,1)}, u32[]{:S(2)}, u32[]{:S(2)}) collective-permute-start(bf16[552,128]{1,0:T(8,128)(2,1)} %get-tuple-element.34), channel_id=1, source_target_pairs={{0,3},{1,4},{2,5},{3,6},{4,7},{5,0},{6,1},{7,2},{8,11},{9,12},{10,... | collective-permute-start | bytes 423944 | tf_op jit(solution)/shard_map/ppermute | solution.py:333
  99.0 0.7 copy-start.13
  99.7 17.3 %collective-permute-start.12 = (bf16[552,128]{1,0:T(8,128)(2,1)}, bf16[552,128]{1,0:T(8,128)(2,1)}, u32[]{:S(2)}, u32[]{:S(2)}) collective-permute-start(bf16[552,128]{1,0:T(8,128)(2,1)} %get-tuple-element.35), channel_id=1, source_target_pairs={{0,2},{1,3},{2,4},{3,5},{4,6},{5,7},{6,0},{7,1},{8,10},{9,11},{10,... | collective-permute-start | bytes 423944 | tf_op jit(solution)/shard_map/ppermute | solution.py:333
  104.0 0.6 copy-start.15
  104.6 18.6 %collective-permute-start.13 = (bf16[552,128]{1,0:T(8,128)(2,1)}, bf16[552,128]{1,0:T(8,128)(2,1)}, u32[]{:S(2)}, u32[]{:S(2)}) collective-permute-start(bf16[552,128]{1,0:T(8,128)(2,1)} %get-tuple-element.36), channel_id=1, source_target_pairs={{0,1},{1,2},{2,3},{3,4},{4,5},{5,6},{6,7},{7,0},{8,9},{9,10},{10,1... | collective-permute-start | bytes 423944 | tf_op jit(solution)/shard_map/ppermute | solution.py:333
  104.6 1.2 copy-start.2
  105.8 1.1 copy-start.3
  123.2 0.9 copy-start.12
  124.1 0.9 copy-start.14
  125.0 0.9 copy-start.16
  125.9 18.1 %copy-start.18 = (f32[2,2]{1,0:T(2,128)S(1)}, f32[2,2]{1,0:T(2,128)}, u32[]{:S(2)}) copy-start(f32[2,2]{1,0:T(2,128)} %mix.1) | copy-start | bytes 52
  131.0 13.0 %collective-permute-start.14 = (bf16[90,24,128]{2,1,0:T(8,128)(2,1)S(1)}, bf16[90,24,128]{2,1,0:T(8,128)(2,1)S(1)}, u32[]{:S(2)}, u32[]{:S(2)}) collective-permute-start(bf16[90,24,128]{2,1,0:T(8,128)(2,1)S(1)} %get-tuple-element.39), channel_id=1, source_target_pairs={{0,128},{128,0},{1,129},{129,1},{2,130},{130,2},{3,131},{131,3},{4... | collective-permute-start | bytes 1658888 | tf_op jit(solution)/shard_map/ppermute | solution.py:407

commit v2 on v1

v2 whole, which is shorter than its diff:
```python
import functools

import jax
import jax.numpy as jnp
from jax import lax
from jax.experimental import pallas as pl
from jax.experimental.pallas import tpu as pltpu
from jax.sharding import PartitionSpec as P


step_size = 0.25


F32 = jnp.float32
BF16 = jnp.bfloat16


def vspec():
    return pl.BlockSpec(memory_space=pltpu.VMEM)


def sspec():
    return pl.BlockSpec(memory_space=pltpu.SMEM)


def swap(x):
    return pltpu.roll(x, 64, x.ndim - 1)


def low_lanes(shape):
    return lax.broadcasted_iota(jnp.int32, shape, len(shape) - 1) < 64


def merge(half, first, second):
    low = low_lanes(first.shape)
    if half == 0:
        return jnp.where(low, first, swap(second))
    return jnp.where(low, swap(first), second)


def z_pack_kernel(col, state, adv, *outs):
    me = col[0]
    for r in range(8):
        dest = lax.rem(me + r, 8)
        a = dest // 2

        def fill(b, r=r, a=a):
            def body(yl, carry):
                y = 3 * a + yl
                base = pl.multiple_of(yl * 216, 8)
                full = slice(256 * b, 256 * b + 128)
                for u in range(6):
                    src = state[u, y, :, full] if u < 5 else adv[y, :, full]
                    outs[r][pl.ds(base + 24 * u, 24), :] = src
                mid = [state[u, y, :, 128:256].astype(F32) for u in range(5)]
                mid.append(adv[y, :, 128:256].astype(F32))
                for q in range(3):
                    tile = merge(b, mid[2 * q], mid[2 * q + 1])
                    outs[r][pl.ds(base + 144 + 24 * q, 24), :] = tile.astype(BF16)
                return carry

            lax.fori_loop(0, 3, body, 0)

        @pl.when(lax.rem(dest, 2) == 0)
        def _():
            fill(0)

        @pl.when(lax.rem(dest, 2) == 1)
        def _():
            fill(1)


def y_pack_kernel(state_far, adv_far, out, state, adv, sem):
    copies = [
        pltpu.make_async_copy(state_far.at[0:2], state.at[0:2], sem.at[0]),
        pltpu.make_async_copy(state_far.at[2:4], state.at[2:4], sem.at[1]),
        pltpu.make_async_copy(state_far.at[4], state.at[4], sem.at[2]),
        pltpu.make_async_copy(adv_far, adv, sem.at[3]),
    ]
    for copy in copies:
        copy.start()

    def lines(p, c):
        lanes = slice(128 * c, 128 * c + 128)
        if p < 2:
            block = state[2 * p : 2 * p + 2, :, :, lanes].astype(F32).reshape(24, 24, 128)
        else:
            block = jnp.concatenate([state[4, :, :, lanes], adv[:, :, lanes]], axis=0).astype(F32)
        return jnp.swapaxes(block, 0, 1)

    for p in range(3):
        for copy in copies[p : p + 1 if p < 2 else 4]:
            copy.wait()
        for b in range(2):
            out[:, b, 72 * p : 72 * p + 72, :] = lines(p, 2 * b).reshape(8, 72, 128).astype(BF16)
    mid = [lines(p, 1) for p in range(2)]
    for b in range(2):
        tile = merge(b, mid[0], mid[1])
        out[:, b, 216:288, :] = tile.reshape(8, 72, 128).astype(BF16)
    last = lines(2, 1).reshape(8, 3, 24, 128)
    none = jnp.zeros((8, 24, 128), F32)
    for b in range(2):
        out[:, b, 288:312, :] = merge(b, last[:, 0], last[:, 1]).astype(BF16)
        out[:, b, 312:336, :] = merge(b, last[:, 2], none).astype(BF16)


def xy_kernel(coef, state, forcing, adv, mat, back_y, out, work):
    lhs_mat = mat[...].reshape(768, 384)
    low3 = low_lanes((24, 24, 128))
    low8 = low_lanes((8, 24, 128))

    def put_lines(c, block):
        work[:, :, 128 * c : 128 * c + 128] = jnp.swapaxes(block, 0, 1)

    def y_tile(b, at, n):
        return back_y[:, b, at : at + 24 * n, :].astype(F32)

    for p in range(3):
        for b in range(2):
            put_lines(2 * b, y_tile(b, 72 * p, 3).reshape(24, 24, 128))
        if p < 2:
            m = [y_tile(b, 216, 3).reshape(24, 24, 128) for b in range(2)]
            if p == 0:
                put_lines(1, jnp.where(low3, m[0], swap(m[1])))
            else:
                put_lines(1, jnp.where(low3, swap(m[0]), m[1]))
        else:
            m = [[y_tile(b, 288 + 24 * j, 1) for j in range(2)] for b in range(2)]
            parts = [
                jnp.where(low8, m[0][0], swap(m[1][0])),
                jnp.where(low8, swap(m[0][0]), m[1][0]),
                jnp.where(low8, m[0][1], swap(m[1][1])),
            ]
            put_lines(1, jnp.stack(parts, axis=1).reshape(24, 24, 128))
        for i in range(2 if p < 2 else 1):
            v = 2 * p + i
            for h in range(2):
                ys = slice(6 * h, 6 * h + 6)
                field = state[v, ys].astype(F32).reshape(144, 384)
                grad = lax.dot_general(
                    field.astype(BF16),
                    lhs_mat,
                    (((1,), (1,)), ((), ())),
                    preferred_element_type=F32,
                )
                vel = adv[ys].astype(F32).reshape(144, 384)
                frc = forcing[v, ys].astype(F32).reshape(144, 384)
                term = coef[v] * grad[:, 384:] - vel * grad[:, :384]
                term = term + work[12 * i + 6 * h : 12 * i + 6 * h + 6].reshape(144, 384)
                out[v, ys] = (field + step_size * (term + frc)).reshape(6, 24, 384)


def matrices_kernel(col, mat_y, mat_z, lines_y, lines_z):
    me = col[0]
    point = lax.broadcasted_iota(jnp.int32, (192, 192), 0)
    place = lax.broadcasted_iota(jnp.int32, (192, 192), 1)
    block = jnp.zeros((192, 192), jnp.int32)
    for r in range(8):
        inside = (place >= 24 * r) & (place < 24 * r + 24)
        block = jnp.where(inside, 24 * lax.rem(me - r + 8, 8) - 24 * r, block)
    order = jnp.where(point == place + block, 1.0, 0.0).astype(BF16)
    for k in range(2):
        cols = jnp.dot(mat_z[k], order, preferred_element_type=F32).astype(BF16)
        rows = lax.dot_general(order, cols, (((0,), (0,)), ((), ())), preferred_element_type=F32)
        lines_z[192 * k : 192 * k + 192, :] = rows.astype(BF16)

    def spots(index):
        q = lax.shift_right_logical(index * 5462, 16)
        return lax.rem(q, 2), 12 * lax.shift_right_logical(q, 1) + index - 12 * q

    member, line = spots(lax.broadcasted_iota(jnp.int32, (384, 192), 0))
    same = line == lax.broadcasted_iota(jnp.int32, (384, 192), 1)
    spread = [jnp.where(same & (member == m), 1.0, 0.0).astype(BF16) for m in range(2)]
    for k in range(2):
        acc = jnp.zeros((384, 384), F32)
        for m in range(2):
            left = jnp.dot(spread[m], mat_y[k], preferred_element_type=F32).astype(BF16)
            acc = acc + lax.dot_general(
                left, spread[m], (((1,), (1,)), ((), ())), preferred_element_type=F32
            )
        lines_y[384 * k : 384 * k + 384, :] = acc.astype(BF16)
    line_to = spots(lax.broadcasted_iota(jnp.int32, (384, 384), 0))[1]
    member_from, line_from = spots(lax.broadcasted_iota(jnp.int32, (384, 384), 1))
    pick = (line_to == line_from) & (member_from == 1)
    lines_y[768:1152, :] = jnp.where(pick, 1.0, 0.0).astype(BF16)


def z_kernel(coef, *refs):
    recv, lines, outs = refs[:8], refs[8], refs[9:]
    low = low_lanes((192, 128))
    lhs = lines[...]

    def tile(yl, t):
        at = yl * 216 + 24 * t
        return jnp.concatenate([ref[at : at + 24, :].astype(F32) for ref in recv], axis=0)

    def put(t, term):
        for r in range(8):
            outs[r][24 * t : 24 * t + 24, :] = term[24 * r : 24 * r + 24].astype(BF16)

    tails = []
    for yl in range(3):
        tiles = [tile(yl, t) for t in range(9)]
        vel = tiles[5]
        vel_half = jnp.where(low, swap(tiles[8]), tiles[8])
        names = [0, 1, 2, 3, 4, 6, 7, 8]
        for n in range(0, 8, 2):
            rhs = jnp.concatenate([tiles[names[n]], tiles[names[n + 1]]], axis=1).astype(BF16)
            grad = jnp.dot(lhs, rhs, preferred_element_type=F32)
            for j in range(2):
                t = names[n + j]
                g0 = grad[:192, 128 * j : 128 * j + 128]
                g1 = grad[192:, 128 * j : 128 * j + 128]
                if t < 5:
                    put(yl * 7 + t, coef[t] * g1 - vel * g0)
                elif t < 8:
                    q = t - 6
                    c = jnp.where(low, coef[2 * q], coef[2 * q + 1])
                    put(yl * 7 + 5 + q, c * g1 - vel_half * g0)
                else:
                    tails.append(coef[4] * g1 - vel_half * g0)
    put(21, jnp.where(low, tails[0], swap(tails[1])))
    put(22, jnp.where(low, tails[2], 0.0))


def y_kernel(coef, recv, lines, out):
    lhs = lines[0:768, :]
    take = lines[768:1152, :]
    low = low_lanes((384, 128))
    member = lax.broadcasted_iota(jnp.int32, (16, 24, 128), 1).reshape(384, 128) >= 12

    def tile(t):
        return recv[:, 24 * t : 24 * t + 24, :].astype(F32).reshape(384, 128).astype(BF16)

    def put(t, term):
        out[:, 24 * t : 24 * t + 24, :] = term.reshape(16, 24, 128).astype(BF16)

    def coef_of(p):
        if p == 2:
            return jnp.where(member, 0.0, coef[4])
        return jnp.where(member, coef[2 * p + 1], coef[2 * p])

    vel_tail = jnp.dot(
        take, jnp.concatenate([tile(12), tile(13)], axis=1), preferred_element_type=F32
    )
    tail = [vel_tail[:, :128], vel_tail[:, 128:]]
    vel_half = [
        jnp.where(low, tail[0], swap(tail[0])),
        jnp.where(low, swap(tail[0]), tail[0]),
        jnp.where(low, tail[1], swap(tail[1])),
    ]

    work = [(12, tail[0], coef_of(2)), (13, tail[1], coef_of(2))]
    vel_full = jnp.dot(
        take, jnp.concatenate([tile(6), tile(7)], axis=1), preferred_element_type=F32
    )
    vels = [vel_full[:, :128], vel_full[:, 128:]]
    vels.append(jnp.dot(take, tile(8), preferred_element_type=F32))
    for zl in range(3):
        work += [(3 * p + zl, vels[zl], coef_of(p)) for p in range(3)]
        work.append((9 + zl, vel_half[zl], jnp.where(low, coef_of(0), coef_of(1))))
    for n in range(0, 14, 2):
        pair = work[n : n + 2]
        rhs = jnp.concatenate([tile(t) for t, _, _ in pair], axis=1)
        grad = jnp.dot(lhs, rhs, preferred_element_type=F32)
        for k, (t, vel, c) in enumerate(pair):
            lanes = slice(128 * k, 128 * k + 128)
            put(t, c * grad[384:, lanes] - vel * grad[:384, lanes])


def tiles_of(p):
    return 36 if p < 2 else 20


def join_kernel(p, probe, col, *refs):
    count = 2 if p < 2 else 1
    base, arrivals = refs[0], refs[1:9]
    out, send, own, rows, sem = refs[-5:]
    first = probe[0] == 0
    me = col[0]
    low = low_lanes((24, 128))

    def give(n, half0, half1):
        send[n] = jnp.where(first, half1, half0).astype(BF16)
        own[n] = jnp.where(first, half0, half1).astype(BF16)

    def fill(odd_me):
        for k in range(4):
            r = [(2 * k - odd_me) % 8, (2 * k - odd_me + 1) % 8]
            a = lax.rem(me + r[0], 8) // 2

            def z_tile(b, t, r=r):
                return arrivals[r[b]][24 * t : 24 * t + 24, :].astype(F32)

            mids = []
            for yl in range(3):
                y = 3 * a + yl
                for i in range(count):
                    v = 2 * p + i
                    full = [z_tile(b, 7 * yl + v) for b in range(2)]
                    t, odd = (7 * yl + 5 + p, i) if p < 2 else (21 + yl // 2, yl % 2)
                    m = [z_tile(b, t) for b in range(2)]
                    if odd:
                        mid = jnp.where(low, swap(m[0]), m[1])
                    else:
                        mid = jnp.where(low, m[0], swap(m[1]))
                    res = []
                    for c, part in enumerate((full[0], mid, full[1])):
                        lanes = slice(128 * c, 128 * c + 128)
                        total = (base[v, y, :, lanes] + step_size * part).astype(BF16)
                        rows[i, y, :, lanes] = total
                        res.append(total.astype(F32))
                    give(12 * i + y, res[0], res[2])
                    mids.append(res[1])
                if p < 2:
                    pair = mids[-2:]
                    give(24 + y, merge(0, *pair), merge(1, *pair))
            if p == 2:
                none = jnp.zeros((24, 128), F32)
                give(12 + a, merge(0, mids[0], mids[1]), merge(1, mids[0], mids[1]))
                give(16 + a, merge(0, mids[2], none), merge(1, mids[2], none))

    for odd_me in range(2):

        @pl.when(lax.rem(me, 2) == odd_me)
        def _(odd_me=odd_me):
            fill(odd_me)

    copies = [
        pltpu.make_async_copy(rows.at[i], out.at[2 * p + i], sem.at[i]) for i in range(count)
    ]
    for copy in copies:
        copy.start()
    for copy in copies:
        copy.wait()


def sketch_kernel(q, probe, mix, *refs):
    count = 2 if q < 2 else 1
    own, recv = refs[:2]
    out, rows, sem = refs[-3:]
    p = probe[0]
    low = low_lanes((24, 128))

    def mixed(n, g):
        a = (own[n].astype(F32) * mix[p, g]).astype(BF16).astype(F32)
        b = (recv[n].astype(F32) * mix[1 - p, g]).astype(BF16).astype(F32)
        return a + b

    def put(i, g, y, full, piece):
        turned = swap(full)
        head = jnp.where(p == 0, full, jnp.where(low, piece, turned))
        tail = jnp.where(p == 0, piece, turned)
        rows[i, g, y, :, 0:128] = head.astype(BF16)
        rows[i, g, y, :, 128:192] = tail[:, :64].astype(BF16)

    def body(a, carry):
        for g in range(2):
            for yl in range(3):
                y = 3 * a + yl
                if q < 2:
                    half = mixed(24 + y, g)
                    put(0, g, y, mixed(y, g), half)
                    put(1, g, y, mixed(12 + y, g), swap(half))
                else:
                    half = mixed(12 + a if yl < 2 else 16 + a, g)
                    put(0, g, y, mixed(y, g), swap(half) if yl == 1 else half)
        return carry

    lax.fori_loop(0, 4, body, 0)
    copies = [
        pltpu.make_async_copy(rows.at[i, g], out.at[g, 2 * q + i], sem.at[i, g])
        for i in range(count)
        for g in range(2)
    ]
    for copy in copies:
        copy.start()
    for copy in copies:
        copy.wait()


def call(kernel, out_shapes, scalars, arrays, scratch=(), kept=(), spaces=None, stay=False):
    many = isinstance(out_shapes, (list, tuple))
    specs = spaces or [vspec() for _ in (out_shapes if many else [0])]
    before = len(scalars) + len(arrays)
    return pl.pallas_call(
        kernel,
        out_shape=out_shapes,
        in_specs=[sspec()] * len(scalars)
        + [pl.BlockSpec(memory_space=pl.ANY) if stay else vspec()] * len(arrays)
        + [pl.BlockSpec(memory_space=pl.ANY)] * len(kept),
        out_specs=specs if many else specs[0],
        scratch_shapes=scratch,
        input_output_aliases={before + n: n for n in range(len(kept))},
        compiler_params=pltpu.CompilerParams(vmem_limit_bytes=16 << 20),
    )(*scalars, *arrays, *kept)


def far(x):
    return pltpu.with_memory_space_constraint(x, pltpu.HBM)


def near(x):
    return pltpu.with_memory_space_constraint(x, pltpu.VMEM)


def shift(x, distance):
    return lax.ppermute(x, "col", [(i, (i + distance) % 8) for i in range(8)])


ROUTES = (3, 5, 4, 2, 6, 1, 7)


def on_device(
    flow_state,
    forcing,
    advect_x,
    advect_y,
    advect_z,
    diffusivity,
    deriv_x,
    deriv_y,
    deriv_z,
    test_mix,
):
    state = flow_state.reshape(5, 12, 24, 384)
    forced = forcing.reshape(5, 12, 24, 384)
    probe = lax.axis_index("probe").astype(jnp.int32).reshape(1)
    col = lax.axis_index("col").astype(jnp.int32).reshape(1)

    def shape(s, t=BF16):
        return jax.ShapeDtypeStruct(s, t)

    def held(s, t=BF16):
        return pltpu.VMEM(s, t)

    def stored(s, t=BF16):
        return pltpu.HBM(s, t)

    any_space = pl.BlockSpec(memory_space=pl.ANY)
    to_y = call(y_pack_kernel, held((8, 2, 336, 128)), [], [far(state), far(advect_y)],
        [
            pltpu.VMEM((5, 12, 24, 384), BF16),
            pltpu.VMEM((12, 24, 384), BF16),
            pltpu.SemaphoreType.DMA((4,)),
        ],
        stay=True,
    )
    at_y = lax.all_to_all(
        to_y.reshape(16, 336, 128), "row", split_axis=0, concat_axis=0, tiled=True
    )
    to_z = call(z_pack_kernel, [stored((648, 128))] + [held((648, 128))] * 7, [col], [state, advect_z])
    at_z = list(to_z)
    for r in ROUTES:
        at_z[r] = shift(to_z[r], r)
    lines_y, lines_z = call(
        matrices_kernel,
        [stored((1152, 384)), stored((384, 192))],
        [col],
        [far(deriv_y), far(deriv_z)],
    )
    term_y = call(y_kernel, stored((16, 336, 128)), [diffusivity], [near(at_y), far(lines_y)])
    back_y = lax.all_to_all(term_y, "row", split_axis=0, concat_axis=0, tiled=True)
    term_z = call(
        z_kernel,
        [stored((552, 128))] + [held((552, 128))] * 7,
        [diffusivity],
        [far(at_z[0])] + [near(x) for x in at_z[1:]] + [far(lines_z)],
    )
    back_z = list(term_z)
    for r in ROUTES:
        back_z[r] = shift(term_z[r], -r)
    base = call(
        xy_kernel,
        held((5, 12, 24, 384), F32),
        [diffusivity],
        [state, forced, advect_x, deriv_x, near(back_y.reshape(8, 2, 336, 128))],
        [pltpu.VMEM((24, 24, 384), F32)],
    )
    pieces = [far(back_z[0])] + [near(x) for x in back_z[1:]]
    sections, sketches, halves = [], [], []
    for p in range(3):
        count = 2 if p < 2 else 1
        section, send, own = call(
            functools.partial(join_kernel, p),
            [shape((5, 12, 24, 384)), held((tiles_of(p), 24, 128)), held((tiles_of(p), 24, 128))],
            [probe, col],
            [near(base)] + pieces,
            [
                pltpu.VMEM((count, 12, 24, 384), BF16),
                pltpu.SemaphoreType.DMA((count,)),
            ],
            kept=sections[-1:],
            spaces=[any_space, vspec(), vspec()],
        )
        sections.append(section)
        halves.append((own, lax.ppermute(send, "probe", [(0, 1), (1, 0)])))
    for p in range(3):
        count = 2 if p < 2 else 1
        own, recv = halves[p]
        sketches.append(
            call(
                functools.partial(sketch_kernel, p),
                [shape((2, 5, 12, 24, 192))],
                [probe, test_mix],
                [near(own), near(recv)],
                [pltpu.VMEM((count, 2, 12, 24, 192), BF16), pltpu.SemaphoreType.DMA((count, 2))],
                kept=sketches[-1:],
                spaces=[any_space],
            )[0]
        )
    section, sketch = sections[-1], sketches[-1]
    return (section[None], sketch)


def solution(mesh):
    placed = (
        P("probe", None, "row", "col", None),
        P("probe", None, "row", "col", None),
        P("row", "col", None),
        P("row", "col", None),
        P("row", "col", None),
        P(),
        P(),
        P(),
        P(),
        P(),
    )

    return jax.shard_map(
        on_device,
        mesh=mesh,
        in_specs=placed,
        out_specs=(P("probe", None, "row", "col", None), P(None, None, "row", "col", "probe")),
        check_vma=False,
    )
```

time: 150 us -> 141 us (0.940)
  blocking collectives: 28.8 us -> 0 us
  starting transfers between devices: 38.8 us -> 48.3 us
  waiting for transfers between devices: 48.4 us -> 56.6 us
  Pallas kernels: 22.8 us -> 29.9 us
  local copies, waits for them, and re-layouts: 9.2 us -> 3.26 us
    all_to_all x1 -> x0, blocking collectives: 28.8 us -> none  [on_device(): lax.all_to_all(to_y.reshape(16, 336, 128), 'row', split_axis=0, concat_ax...]
    all_to_all x0 -> x1, waiting for transfers between devices: none -> 17.5 us  [on_device(): lax.all_to_all(to_y.reshape(16, 336, 128), 'row', split_axis=0, concat_ax...]
    ppermute x1 -> x3, waiting for transfers between devices: 12.7 us -> 3.59 us  [on_device(): halves.append((own, lax.ppermute(send, 'probe', [(0, 1), (1, 0)])))]
    all_to_all x0 -> x1, starting transfers between devices: none -> 8.45 us  [on_device(): lax.all_to_all(to_y.reshape(16, 336, 128), 'row', split_axis=0, concat_ax...]
    pallas_call x7 -> x12, Pallas kernels: 22.8 us -> 29.9 us  [call(): pl.pallas_call(kernel, out_shape=out_shapes, in_specs=[sspec()] * len(sca...]
    unnamed x38 -> x14, local copies, waits for them, and re-layouts: 9.2 us -> 3.26 us
    ppermute x1 -> x3, starting transfers between devices: 0.31 us -> 2.04 us  [on_device(): halves.append((own, lax.ppermute(send, 'probe', [(0, 1), (1, 0)])))]
  transfers between devices with their start and end apart: 16 -> 19, of which waited for: 8 -> 11; matrix products, arithmetic and copies ran while one was open for 0% -> 0% of each run, Pallas kernels for 5% -> 14%
where the time goes in v2:
time: 141 us; the launch traced here: 139 us
  waiting for transfers between devices  56.6 us (40%)
  starting transfers between devices  48.3 us (34%)
  Pallas kernels  29.9 us (21%)
  local copies, waits for them, and re-layouts  3.26 us (2%)
    ppermute x14, waiting for transfers between devices, shift(): return lax.ppermute(x, 'col', [(i, (i + distance) % 8) for i in range(8)])  35.5 us
    ppermute x14, starting transfers between devices, shift(): return lax.ppermute(x, 'col', [(i, (i + distance) % 8) for i in range(8)])  33.2 us
    pallas_call x12, Pallas kernels, call(): pl.pallas_call(kernel, out_shape=out_shapes, in_specs=[sspec()] * len(sca...  29.9 us
    all_to_all x1, waiting for transfers between devices, on_device(): lax.all_to_all(to_y.reshape(16, 336, 128), 'row', split_axis=0, concat_ax...  17.5 us
    all_to_all x1, starting transfers between devices, on_device(): lax.all_to_all(to_y.reshape(16, 336, 128), 'row', split_axis=0, concat_ax...  8.45 us
    all_to_all x1, starting transfers between devices, on_device(): lax.all_to_all(term_y, 'row', split_axis=0, concat_axis=0, tiled=True)  4.65 us
    ppermute x3, waiting for transfers between devices, on_device(): halves.append((own, lax.ppermute(send, 'probe', [(0, 1), (1, 0)])))  3.59 us
    unnamed x14, local copies, waits for them, and re-layouts  3.26 us
  transfers between devices with their start and end apart: 19, of which 11 were waited for; matrix products, arithmetic and copies ran while one was open for 0% of the time, Pallas kernels for 14%

profile of v2, /device:TPU:1, one launch (start us, length us, event | category | flops | bytes accessed | tf_op | source)
XLA Modules:
  0.0 139.0 jit_solution(8206160145504485180)
XLA Ops:
  0.6 2.8 %shard_map.113 = bf16[8,2,336,128]{3,2,1,0:T(8,128)(2,1)} custom-call(bf16[5,12,24,384]{3,2,1,0:T(8,128)(2,1)} %bitcast.7, bf16[12,24,384]{2,1,0:T(8,128)(2,1)} %adv_far.1), custom_call_target="tpu_custom_call" | custom-call | tf_op jit(solution)/shard_map/pallas_call | solution.py:386
  3.4 0.0 copy-start.6
  3.4 8.4 %all-to-all-start = ((bf16[16,336,128]{2,1,0:T(8,128)(2,1)}), bf16[16,336,128]{2,1,0:T(8,128)(2,1)S(1)}, u32[]{:S(2)}, u32[]{:S(2)}) async-start(bf16[16,336,128]{2,1,0:T(8,128)(2,1)} %bitcast.4), calls=%async_computation | async-start | bytes 2752512 | tf_op jit(solution)/shard_map/all_to_all | solution.py:449
  11.9 3.1 %shard_map.114 = (bf16[1152,384]{1,0:T(8,128)(2,1)}, bf16[384,192]{1,0:T(8,128)(2,1)}) custom-call(s32[1]{0:T(128)} %bitcast.1.col, bf16[2,192,192]{2,1,0:T(8,128)(2,1)} %mat_y.1, bf16[2,192,192]{2,1,0:T(8,128)(2,1)} %mat_z.1), custom_call_target="tpu_custom_call" | custom-call | tf_op jit(solution)/shard_map/pallas_call | solution.py:386
  15.0 17.5 %all-to-all-done.recv = bf16[16,336,128]{2,1,0:T(8,128)(2,1)S(1)} async-done(((bf16[16,336,128]{2,1,0:T(8,128)(2,1)}), bf16[16,336,128]{2,1,0:T(8,128)(2,1)S(1)}, u32[]{:S(2)}, u32[]{:S(2)}) %all-to-all-start) | async-done | bytes 1376288 | tf_op jit(solution)/shard_map/all_to_all | solution.py:449
  32.5 4.2 %shard_map.115 = bf16[16,336,128]{2,1,0:T(8,128)(2,1)} custom-call(f32[5]{0:T(128)S(1)} %copy-done.6, bf16[16,336,128]{2,1,0:T(8,128)(2,1)S(1)} %all-to-all-done.recv, bf16[1152,384]{1,0:T(8,128)(2,1)} %get-tuple-element.29.lines), custom_call_target="tpu_custom_call" | custom-call | tf_op jit(solution)/shard_map/pallas_call | solution.py:386
  36.7 4.6 %all-to-all-start.1 = ((bf16[16,336,128]{2,1,0:T(8,128)(2,1)}), bf16[16,336,128]{2,1,0:T(8,128)(2,1)S(1)}, u32[]{:S(2)}, u32[]{:S(2)}) async-start(bf16[16,336,128]{2,1,0:T(8,128)(2,1)} %shard_map.115), calls=%async_computation.1 | async-start | bytes 2752512 | tf_op jit(solution)/shard_map/all_to_all | solution.py:463
  41.3 2.6 %shard_map.117 = (bf16[648,128]{1,0:T(8,128)(2,1)}, bf16[648,128]{1,0:T(8,128)(2,1)S(1)}, bf16[648,128]{1,0:T(8,128)(2,1)S(1)}, bf16[648,128]{1,0:T(8,128)(2,1)S...) custom-call(s32[1]{0:T(128)} %bitcast.1.col, ...), custom_call_target="tpu_custom_call" | custom-call | tf_op jit(solution)/shard_map/pallas_call | solution.py:386
  43.9 1.6 %collective-permute-start = (bf16[648,128]{1,0:T(8,128)(2,1)S(1)}, bf16[648,128]{1,0:T(8,128)(2,1)S(1)}, u32[]{:S(2)}, u32[]{:S(2)}) collective-permute-start(bf16[648,128]{1,0:T(8,128)(2,1)S(1)} %get-tuple-element.31), channel_id=1, source_target_pairs={{0,1},{1,2},{2,3},{3,4},{4,5},{5,6},{6,7},{7,0},{8,9},{9,10},{10,1... | collective-permute-start | bytes 497672 | tf_op jit(solution)/shard_map/ppermute | solution.py:408
  45.6 3.0 %collective-permute-start.1 = (bf16[648,128]{1,0:T(8,128)(2,1)S(1)}, bf16[648,128]{1,0:T(8,128)(2,1)S(1)}, u32[]{:S(2)}, u32[]{:S(2)}) collective-permute-start(bf16[648,128]{1,0:T(8,128)(2,1)S(1)} %get-tuple-element.32), channel_id=1, source_target_pairs={{0,2},{1,3},{2,4},{3,5},{4,6},{5,7},{6,0},{7,1},{8,10},{9,11},{10,... | collective-permute-start | bytes 497672 | tf_op jit(solution)/shard_map/ppermute | solution.py:408
  48.6 3.7 %collective-permute-start.2 = (bf16[648,128]{1,0:T(8,128)(2,1)S(1)}, bf16[648,128]{1,0:T(8,128)(2,1)S(1)}, u32[]{:S(2)}, u32[]{:S(2)}) collective-permute-start(bf16[648,128]{1,0:T(8,128)(2,1)S(1)} %get-tuple-element.33), channel_id=1, source_target_pairs={{0,3},{1,4},{2,5},{3,6},{4,7},{5,0},{6,1},{7,2},{8,11},{9,12},{10,... | collective-permute-start | bytes 497672 | tf_op jit(solution)/shard_map/ppermute | solution.py:408
  52.3 0.5 collective-permute-start.3
  52.8 4.5 %collective-permute-start.4 = (bf16[648,128]{1,0:T(8,128)(2,1)S(1)}, bf16[648,128]{1,0:T(8,128)(2,1)S(1)}, u32[]{:S(2)}, u32[]{:S(2)}) collective-permute-start(bf16[648,128]{1,0:T(8,128)(2,1)S(1)} %get-tuple-element.35), channel_id=1, source_target_pairs={{0,5},{1,6},{2,7},{3,0},{4,1},{5,2},{6,3},{7,4},{8,13},{9,14},{10,... | collective-permute-start | bytes 497672 | tf_op jit(solution)/shard_map/ppermute | solution.py:408
  57.3 0.0 collective-permute-done.refs_1_
  57.3 2.4 %collective-permute-start.5 = (bf16[648,128]{1,0:T(8,128)(2,1)S(1)}, bf16[648,128]{1,0:T(8,128)(2,1)S(1)}, u32[]{:S(2)}, u32[]{:S(2)}) collective-permute-start(bf16[648,128]{1,0:T(8,128)(2,1)S(1)} %get-tuple-element.36), channel_id=1, source_target_pairs={{0,6},{1,7},{2,0},{3,1},{4,2},{5,3},{6,4},{7,5},{8,14},{9,15},{10,... | collective-permute-start | bytes 497672 | tf_op jit(solution)/shard_map/ppermute | solution.py:408
  59.7 4.0 %collective-permute-start.6 = (bf16[648,128]{1,0:T(8,128)(2,1)S(1)}, bf16[648,128]{1,0:T(8,128)(2,1)S(1)}, u32[]{:S(2)}, u32[]{:S(2)}) collective-permute-start(bf16[648,128]{1,0:T(8,128)(2,1)S(1)} %get-tuple-element.37), channel_id=1, source_target_pairs={{0,7},{1,0},{2,1},{3,2},{4,3},{5,4},{6,5},{7,6},{8,15},{9,8},{10,9... | collective-permute-start | bytes 497672 | tf_op jit(solution)/shard_map/ppermute | solution.py:408
  63.6 8.4 %collective-permute-done.2.refs_3_ = bf16[648,128]{1,0:T(8,128)(2,1)S(1)} collective-permute-done((bf16[648,128]{1,0:T(8,128)(2,1)S(1)}, bf16[648,128]{1,0:T(8,128)(2,1)S(1)}, u32[]{:S(2)}, u32[]{:S(2)}) %collective-permute-start.2) | collective-permute-done | bytes 165920 | tf_op jit(solution)/shard_map/ppermute | solution.py:408
  72.1 2.9 %collective-permute-done.3.refs_4_ = bf16[648,128]{1,0:T(8,128)(2,1)S(1)} collective-permute-done((bf16[648,128]{1,0:T(8,128)(2,1)S(1)}, bf16[648,128]{1,0:T(8,128)(2,1)S(1)}, u32[]{:S(2)}, u32[]{:S(2)}) %collective-permute-start.3) | collective-permute-done | bytes 165920 | tf_op jit(solution)/shard_map/ppermute | solution.py:408
  75.0 7.8 %collective-permute-done.5.refs_6_ = bf16[648,128]{1,0:T(8,128)(2,1)S(1)} collective-permute-done((bf16[648,128]{1,0:T(8,128)(2,1)S(1)}, bf16[648,128]{1,0:T(8,128)(2,1)S(1)}, u32[]{:S(2)}, u32[]{:S(2)}) %collective-permute-start.5) | collective-permute-done | bytes 165920 | tf_op jit(solution)/shard_map/ppermute | solution.py:408
  82.8 0.7 collective-permute-done.6.refs_7_
  83.5 2.7 %shard_map.118 = (bf16[552,128]{1,0:T(8,128)(2,1)}, bf16[552,128]{1,0:T(8,128)(2,1)S(1)}, bf16[552,128]{1,0:T(8,128)(2,1)S(1)}, bf16[552,128]{1,0:T(8,128)(2,1)}...) custom-call(f32[5]{0:T(128)S(1)} %copy-done.6, ...), custom_call_target="tpu_custom_call" | custom-call | tf_op jit(solution)/shard_map/pallas_call | solution.py:386
  86.2 2.8 %collective-permute-start.7 = (bf16[552,128]{1,0:T(8,128)(2,1)S(1)}, bf16[552,128]{1,0:T(8,128)(2,1)S(1)}, u32[]{:S(2)}, u32[]{:S(2)}) collective-permute-start(bf16[552,128]{1,0:T(8,128)(2,1)S(1)} %get-tuple-element.40), channel_id=1, source_target_pairs={{0,7},{1,0},{2,1},{3,2},{4,3},{5,4},{6,5},{7,6},{8,15},{9,8},{10,9... | collective-permute-start | bytes 423944 | tf_op jit(solution)/shard_map/ppermute | solution.py:408
  89.0 0.9 collective-permute-start.8
  89.9 3.0 %collective-permute-start.9 = (bf16[552,128]{1,0:T(8,128)(2,1)}, bf16[552,128]{1,0:T(8,128)(2,1)S(1)}, u32[]{:S(2)}, u32[]{:S(2)}) collective-permute-start(bf16[552,128]{1,0:T(8,128)(2,1)} %get-tuple-element.42), channel_id=1, source_target_pairs={{0,5},{1,6},{2,7},{3,0},{4,1},{5,2},{6,3},{7,4},{8,13},{9,14},{10,... | collective-permute-start | bytes 423944 | tf_op jit(solution)/shard_map/ppermute | solution.py:408
  92.9 1.5 %collective-permute-start.10 = (bf16[552,128]{1,0:T(8,128)(2,1)}, bf16[552,128]{1,0:T(8,128)(2,1)S(1)}, u32[]{:S(2)}, u32[]{:S(2)}) collective-permute-start(bf16[552,128]{1,0:T(8,128)(2,1)} %get-tuple-element.43), channel_id=1, source_target_pairs={{0,4},{1,5},{2,6},{3,7},{4,0},{5,1},{6,2},{7,3},{8,12},{9,13},{10,... | collective-permute-start | bytes 423944 | tf_op jit(solution)/shard_map/ppermute | solution.py:408
  94.4 3.3 %collective-permute-start.11 = (bf16[552,128]{1,0:T(8,128)(2,1)}, bf16[552,128]{1,0:T(8,128)(2,1)S(1)}, u32[]{:S(2)}, u32[]{:S(2)}) collective-permute-start(bf16[552,128]{1,0:T(8,128)(2,1)} %get-tuple-element.44), channel_id=1, source_target_pairs={{0,3},{1,4},{2,5},{3,6},{4,7},{5,0},{6,1},{7,2},{8,11},{9,12},{10,... | collective-permute-start | bytes 423944 | tf_op jit(solution)/shard_map/ppermute | solution.py:408
  97.7 2.0 %collective-permute-start.12 = (bf16[552,128]{1,0:T(8,128)(2,1)}, bf16[552,128]{1,0:T(8,128)(2,1)S(1)}, u32[]{:S(2)}, u32[]{:S(2)}) collective-permute-start(bf16[552,128]{1,0:T(8,128)(2,1)} %get-tuple-element.45), channel_id=1, source_target_pairs={{0,2},{1,3},{2,4},{3,5},{4,6},{5,7},{6,0},{7,1},{8,10},{9,11},{10,... | collective-permute-start | bytes 423944 | tf_op jit(solution)/shard_map/ppermute | solution.py:408
  99.7 2.8 %collective-permute-done.8.refs_3_ = bf16[552,128]{1,0:T(8,128)(2,1)S(1)} collective-permute-done((bf16[552,128]{1,0:T(8,128)(2,1)S(1)}, bf16[552,128]{1,0:T(8,128)(2,1)S(1)}, u32[]{:S(2)}, u32[]{:S(2)}) %collective-permute-start.8) | collective-permute-done | bytes 141344 | tf_op jit(solution)/shard_map/ppermute | solution.py:408
  102.5 1.2 copy-done.1
  103.7 1.1 copy-done.2
  104.8 0.9 copy-done.4
  105.7 3.1 %shard_map.116.refs_0_ = f32[5,12,24,384]{3,2,1,0:T(8,128)S(1)} custom-call(f32[5]{0:T(128)S(1)} %copy-done.6, bf16[5,12,24,384]{3,2,1,0:T(8,128)(2,1)S(1)} %bitcast.9, bf16[5,12,24,384]{3,2,1,0:T(8,128)(2,1)S(1)} %bitcast.11, bf16[12,24,384]{2,1,0:T(8,128)(2,1)S(1)} %copy-done.4, bf16[2,384,384]{2,1,0:T(8,128)(2,1)S(1)} %copy-done.2, ...), custom_call_target="tpu_custom_call" | custom-call | tf_op jit(solution)/shard_map/pallas_call | solution.py:386
  108.9 0.0 collective-permute-done.9.refs_4_
  108.9 0.0 collective-permute-done.10.refs_5_
  108.9 6.7 %collective-permute-done.11.refs_6_ = bf16[552,128]{1,0:T(8,128)(2,1)S(1)} collective-permute-done((bf16[552,128]{1,0:T(8,128)(2,1)}, bf16[552,128]{1,0:T(8,128)(2,1)S(1)}, u32[]{:S(2)}, u32[]{:S(2)}) %collective-permute-start.11) | collective-permute-done | bytes 141344 | tf_op jit(solution)/shard_map/ppermute | solution.py:408
  115.7 6.1 %collective-permute-done.13.refs_8_ = bf16[552,128]{1,0:T(8,128)(2,1)S(1)} collective-permute-done((bf16[552,128]{1,0:T(8,128)(2,1)}, bf16[552,128]{1,0:T(8,128)(2,1)S(1)}, u32[]{:S(2)}, u32[]{:S(2)}) %collective-permute-start.13) | collective-permute-done | bytes 141344 | tf_op jit(solution)/shard_map/ppermute | solution.py:408
  121.8 2.0 %shard_map.119 = (bf16[5,12,24,384]{3,2,1,0:T(8,128)(2,1)}, bf16[36,24,128]{2,1,0:T(8,128)(2,1)S(1)}, bf16[36,24,128]{2,1,0:T(8,128)(2,1)S(1)}) custom-call(s32[1]{0:T(128)} %bitcast.probe, s32[1]{0:T(128)} %bitcast.1.col, f32[5,12,24,384]{3,2,1,0:T(8,128)S(1)} %shard_map.116.refs_0_, bf16[552,128]{1,0:T(8,128)(2,1)} %get-tuple-element.39.refs_1_, ...), custom_call_target="tpu_custom_call" | custom-call | tf_op jit(solution)/shard_map/pallas_call | solution.py:386
  123.8 0.4 collective-permute-start.16
  124.2 2.0 %shard_map.120 = (bf16[5,12,24,384]{3,2,1,0:T(8,128)(2,1)}, bf16[36,24,128]{2,1,0:T(8,128)(2,1)S(1)}, bf16[36,24,128]{2,1,0:T(8,128)(2,1)S(1)}) custom-call(s32[1]{0:T(128)} %bitcast.probe, s32[1]{0:T(128)} %bitcast.1.col, f32[5,12,24,384]{3,2,1,0:T(8,128)S(1)} %shard_map.116.refs_0_, ...), custom_call_target="tpu_custom_call", output_to_operand_aliasing={{0}: (11, {})} | custom-call | tf_op jit(solution)/shard_map/pallas_call | solution.py:386
  126.2 1.2 collective-permute-start.15
  127.4 1.8 %shard_map.121 = (bf16[5,12,24,384]{3,2,1,0:T(8,128)(2,1)}, bf16[20,24,128]{2,1,0:T(8,128)(2,1)S(1)}, bf16[20,24,128]{2,1,0:T(8,128)(2,1)S(1)}) custom-call(s32[1]{0:T(128)} %bitcast.probe, s32[1]{0:T(128)} %bitcast.1.col, f32[5,12,24,384]{3,2,1,0:T(8,128)S(1)} %shard_map.116.refs_0_, ...), custom_call_target="tpu_custom_call", output_to_operand_aliasing={{0}: (11, {})} | custom-call | tf_op jit(solution)/shard_map/pallas_call | solution.py:386
  129.2 0.4 collective-permute-start.14
  129.6 0.2 collective-permute-done.16.refs_1_
  129.8 2.0 %shard_map.122.refs_2_ = bf16[2,5,12,24,192]{4,3,2,1,0:T(8,128)(2,1)} custom-call(s32[1]{0:T(128)} %bitcast.probe, f32[2,2]{1,0:T(2,128)S(1)} %copy-done.5, bf16[36,24,128]{2,1,0:T(8,128)(2,1)S(1)} %get-tuple-element.54.refs_0_, bf16[36,24,128]{2,1,0:T(8,128)(2,1)S(1)} %collective-permute-done.16.refs_1_), custom_call_target="tpu_custom_call" | custom-call | tf_op jit(solution)/shard_map/pallas_call | solution.py:386
  131.8 2.8 %collective-permute-done.15.refs_1_ = bf16[36,24,128]{2,1,0:T(8,128)(2,1)S(1)} collective-permute-done((bf16[36,24,128]{2,1,0:T(8,128)(2,1)S(1)}, bf16[36,24,128]{2,1,0:T(8,128)(2,1)S(1)}, u32[]{:S(2)}, u32[]{:S(2)}) %collective-permute-start.15) | collective-permute-done | bytes 221216 | tf_op jit(solution)/shard_map/ppermute | solution.py:497
  134.5 2.0 %shard_map.123.refs_2_ = bf16[2,5,12,24,192]{4,3,2,1,0:T(8,128)(2,1)} custom-call(s32[1]{0:T(128)} %bitcast.probe, f32[2,2]{1,0:T(2,128)S(1)} %copy-done.5, bf16[36,24,128]{2,1,0:T(8,128)(2,1)S(1)} %get-tuple-element.52.refs_0_, bf16[36,24,128]{2,1,0:T(8,128)(2,1)S(1)} %collective-permute-done.15.refs_1_, ...), custom_call_target="tpu_custom_call", output_to_operand_aliasing={{}: (4, {})} | custom-call | tf_op jit(solution)/shard_map/pallas_call | solution.py:386
  136.5 0.7 collective-permute-done.14.refs_1_
  137.2 1.7 %shard_map.124 = bf16[2,5,12,24,192]{4,3,2,1,0:T(8,128)(2,1)} custom-call(s32[1]{0:T(128)} %bitcast.probe, f32[2,2]{1,0:T(2,128)S(1)} %copy-done.5, bf16[20,24,128]{2,1,0:T(8,128)(2,1)S(1)} %get-tuple-element.50.refs_0_, bf16[20,24,128]{2,1,0:T(8,128)(2,1)S(1)} %collective-permute-done.14.refs_1_, ...), custom_call_target="tpu_custom_call", output_to_operand_aliasing={{}: (4, {})} | custom-call | tf_op jit(solution)/shard_map/pallas_call | solution.py:386
  (16 shorter events, 0.0 us)
Async XLA Ops:
  3.4 29.1 %copy-start.6 = (f32[5]{0:T(128)S(1)}, f32[5]{0:T(128)}, u32[]{:S(2)}) copy-start(f32[5]{0:T(128)} %coef.5) | copy-start | bytes 64
  3.4 29.1 %all-to-all-start = ((bf16[16,336,128]{2,1,0:T(8,128)(2,1)}), bf16[16,336,128]{2,1,0:T(8,128)(2,1)S(1)}, u32[]{:S(2)}, u32[]{:S(2)}) async-start(bf16[16,336,128]{2,1,0:T(8,128)(2,1)} %bitcast.4), calls=%async_computation | async-start | bytes 2752512 | tf_op jit(solution)/shard_map/all_to_all | solution.py:449
  36.7 4.7 %copy-start = (bf16[1,5,12,24,384]{4,3,2,1,0:T(8,128)(2,1)S(1)}, bf16[1,5,12,24,384]{4,3,2,1,0:T(8,128)(2,1)}, u32[]{:S(2)}) copy-start(bf16[1,5,12,24,384]{4,3,2,1,0:T(8,128)(2,1)} %param.10) | copy-start | bytes 3317764
  36.7 4.7 %copy-start.3 = (bf16[12,24,384]{2,1,0:T(8,128)(2,1)S(1)}, bf16[12,24,384]{2,1,0:T(8,128)(2,1)}, u32[]{:S(2)}) copy-start(bf16[12,24,384]{2,1,0:T(8,128)(2,1)} %adv.3) | copy-start | bytes 663556
  36.7 65.8 %all-to-all-start.1 = ((bf16[16,336,128]{2,1,0:T(8,128)(2,1)}), bf16[16,336,128]{2,1,0:T(8,128)(2,1)S(1)}, u32[]{:S(2)}, u32[]{:S(2)}) async-start(bf16[16,336,128]{2,1,0:T(8,128)(2,1)} %shard_map.115), calls=%async_computation.1 | async-start | bytes 2752512 | tf_op jit(solution)/shard_map/all_to_all | solution.py:463
  43.9 13.3 %collective-permute-start = (bf16[648,128]{1,0:T(8,128)(2,1)S(1)}, bf16[648,128]{1,0:T(8,128)(2,1)S(1)}, u32[]{:S(2)}, u32[]{:S(2)}) collective-permute-start(bf16[648,128]{1,0:T(8,128)(2,1)S(1)} %get-tuple-element.31), channel_id=1, source_target_pairs={{0,1},{1,2},{2,3},{3,4},{4,5},{5,6},{6,7},{7,0},{8,9},{9,10},{10,1... | collective-permute-start | bytes 497672 | tf_op jit(solution)/shard_map/ppermute | solution.py:408
  45.6 14.1 %collective-permute-start.1 = (bf16[648,128]{1,0:T(8,128)(2,1)S(1)}, bf16[648,128]{1,0:T(8,128)(2,1)S(1)}, u32[]{:S(2)}, u32[]{:S(2)}) collective-permute-start(bf16[648,128]{1,0:T(8,128)(2,1)S(1)} %get-tuple-element.32), channel_id=1, source_target_pairs={{0,2},{1,3},{2,4},{3,5},{4,6},{5,7},{6,0},{7,1},{8,10},{9,11},{10,... | collective-permute-start | bytes 497672 | tf_op jit(solution)/shard_map/ppermute | solution.py:408
  48.6 23.5 %collective-permute-start.2 = (bf16[648,128]{1,0:T(8,128)(2,1)S(1)}, bf16[648,128]{1,0:T(8,128)(2,1)S(1)}, u32[]{:S(2)}, u32[]{:S(2)}) collective-permute-start(bf16[648,128]{1,0:T(8,128)(2,1)S(1)} %get-tuple-element.33), channel_id=1, source_target_pairs={{0,3},{1,4},{2,5},{3,6},{4,7},{5,0},{6,1},{7,2},{8,11},{9,12},{10,... | collective-permute-start | bytes 497672 | tf_op jit(solution)/shard_map/ppermute | solution.py:408
  52.3 22.6 %collective-permute-start.3 = (bf16[648,128]{1,0:T(8,128)(2,1)S(1)}, bf16[648,128]{1,0:T(8,128)(2,1)S(1)}, u32[]{:S(2)}, u32[]{:S(2)}) collective-permute-start(bf16[648,128]{1,0:T(8,128)(2,1)S(1)} %get-tuple-element.34), channel_id=1, source_target_pairs={{0,4},{1,5},{2,6},{3,7},{4,0},{5,1},{6,2},{7,3},{8,12},{9,13},{10,... | collective-permute-start | bytes 497672 | tf_op jit(solution)/shard_map/ppermute | solution.py:408
  52.8 22.2 %collective-permute-start.4 = (bf16[648,128]{1,0:T(8,128)(2,1)S(1)}, bf16[648,128]{1,0:T(8,128)(2,1)S(1)}, u32[]{:S(2)}, u32[]{:S(2)}) collective-permute-start(bf16[648,128]{1,0:T(8,128)(2,1)S(1)} %get-tuple-element.35), channel_id=1, source_target_pairs={{0,5},{1,6},{2,7},{3,0},{4,1},{5,2},{6,3},{7,4},{8,13},{9,14},{10,... | collective-permute-start | bytes 497672 | tf_op jit(solution)/shard_map/ppermute | solution.py:408
  57.3 25.5 %collective-permute-start.5 = (bf16[648,128]{1,0:T(8,128)(2,1)S(1)}, bf16[648,128]{1,0:T(8,128)(2,1)S(1)}, u32[]{:S(2)}, u32[]{:S(2)}) collective-permute-start(bf16[648,128]{1,0:T(8,128)(2,1)S(1)} %get-tuple-element.36), channel_id=1, source_target_pairs={{0,6},{1,7},{2,0},{3,1},{4,2},{5,3},{6,4},{7,5},{8,14},{9,15},{10,... | collective-permute-start | bytes 497672 | tf_op jit(solution)/shard_map/ppermute | solution.py:408
  59.7 23.8 %collective-permute-start.6 = (bf16[648,128]{1,0:T(8,128)(2,1)S(1)}, bf16[648,128]{1,0:T(8,128)(2,1)S(1)}, u32[]{:S(2)}, u32[]{:S(2)}) collective-permute-start(bf16[648,128]{1,0:T(8,128)(2,1)S(1)} %get-tuple-element.37), channel_id=1, source_target_pairs={{0,7},{1,0},{2,1},{3,2},{4,3},{5,4},{6,5},{7,6},{8,15},{9,8},{10,9... | collective-permute-start | bytes 497672 | tf_op jit(solution)/shard_map/ppermute | solution.py:408
  86.2 11.5 %collective-permute-start.7 = (bf16[552,128]{1,0:T(8,128)(2,1)S(1)}, bf16[552,128]{1,0:T(8,128)(2,1)S(1)}, u32[]{:S(2)}, u32[]{:S(2)}) collective-permute-start(bf16[552,128]{1,0:T(8,128)(2,1)S(1)} %get-tuple-element.40), channel_id=1, source_target_pairs={{0,7},{1,0},{2,1},{3,2},{4,3},{5,4},{6,5},{7,6},{8,15},{9,8},{10,9... | collective-permute-start | bytes 423944 | tf_op jit(solution)/shard_map/ppermute | solution.py:408
  89.0 13.5 %collective-permute-start.8 = (bf16[552,128]{1,0:T(8,128)(2,1)S(1)}, bf16[552,128]{1,0:T(8,128)(2,1)S(1)}, u32[]{:S(2)}, u32[]{:S(2)}) collective-permute-start(bf16[552,128]{1,0:T(8,128)(2,1)S(1)} %get-tuple-element.41), channel_id=1, source_target_pairs={{0,6},{1,7},{2,0},{3,1},{4,2},{5,3},{6,4},{7,5},{8,14},{9,15},{10,... | collective-permute-start | bytes 423944 | tf_op jit(solution)/shard_map/ppermute | solution.py:408
  89.9 19.0 %collective-permute-start.9 = (bf16[552,128]{1,0:T(8,128)(2,1)}, bf16[552,128]{1,0:T(8,128)(2,1)S(1)}, u32[]{:S(2)}, u32[]{:S(2)}) collective-permute-start(bf16[552,128]{1,0:T(8,128)(2,1)} %get-tuple-element.42), channel_id=1, source_target_pairs={{0,5},{1,6},{2,7},{3,0},{4,1},{5,2},{6,3},{7,4},{8,13},{9,14},{10,... | collective-permute-start | bytes 423944 | tf_op jit(solution)/shard_map/ppermute | solution.py:408
  92.9 16.0 %collective-permute-start.10 = (bf16[552,128]{1,0:T(8,128)(2,1)}, bf16[552,128]{1,0:T(8,128)(2,1)S(1)}, u32[]{:S(2)}, u32[]{:S(2)}) collective-permute-start(bf16[552,128]{1,0:T(8,128)(2,1)} %get-tuple-element.43), channel_id=1, source_target_pairs={{0,4},{1,5},{2,6},{3,7},{4,0},{5,1},{6,2},{7,3},{8,12},{9,13},{10,... | collective-permute-start | bytes 423944 | tf_op jit(solution)/shard_map/ppermute | solution.py:408
  94.4 21.2 %collective-permute-start.11 = (bf16[552,128]{1,0:T(8,128)(2,1)}, bf16[552,128]{1,0:T(8,128)(2,1)S(1)}, u32[]{:S(2)}, u32[]{:S(2)}) collective-permute-start(bf16[552,128]{1,0:T(8,128)(2,1)} %get-tuple-element.44), channel_id=1, source_target_pairs={{0,3},{1,4},{2,5},{3,6},{4,7},{5,0},{6,1},{7,2},{8,11},{9,12},{10,... | collective-permute-start | bytes 423944 | tf_op jit(solution)/shard_map/ppermute | solution.py:408
  97.7 18.0 %collective-permute-start.12 = (bf16[552,128]{1,0:T(8,128)(2,1)}, bf16[552,128]{1,0:T(8,128)(2,1)S(1)}, u32[]{:S(2)}, u32[]{:S(2)}) collective-permute-start(bf16[552,128]{1,0:T(8,128)(2,1)} %get-tuple-element.45), channel_id=1, source_target_pairs={{0,2},{1,3},{2,4},{3,5},{4,6},{5,7},{6,0},{7,1},{8,10},{9,11},{10,... | collective-permute-start | bytes 423944 | tf_op jit(solution)/shard_map/ppermute | solution.py:408
  102.5 19.3 %collective-permute-start.13 = (bf16[552,128]{1,0:T(8,128)(2,1)}, bf16[552,128]{1,0:T(8,128)(2,1)S(1)}, u32[]{:S(2)}, u32[]{:S(2)}) collective-permute-start(bf16[552,128]{1,0:T(8,128)(2,1)} %get-tuple-element.46), channel_id=1, source_target_pairs={{0,1},{1,2},{2,3},{3,4},{4,5},{5,6},{6,7},{7,0},{8,9},{9,10},{10,1... | collective-permute-start | bytes 423944 | tf_op jit(solution)/shard_map/ppermute | solution.py:408
  102.5 1.2 copy-start.1
  103.7 1.1 copy-start.2
  104.8 0.9 copy-start.4
  123.8 6.0 %collective-permute-start.16 = (bf16[36,24,128]{2,1,0:T(8,128)(2,1)S(1)}, bf16[36,24,128]{2,1,0:T(8,128)(2,1)S(1)}, u32[]{:S(2)}, u32[]{:S(2)}) collective-permute-start(bf16[36,24,128]{2,1,0:T(8,128)(2,1)S(1)} %get-tuple-element.55), channel_id=1, source_target_pairs={{0,128},{128,0},{1,129},{129,1},{2,130},{130,2},{3,131},{131,3},{4... | collective-permute-start | bytes 663560 | tf_op jit(solution)/shard_map/ppermute | solution.py:497
  126.2 8.4 %collective-permute-start.15 = (bf16[36,24,128]{2,1,0:T(8,128)(2,1)S(1)}, bf16[36,24,128]{2,1,0:T(8,128)(2,1)S(1)}, u32[]{:S(2)}, u32[]{:S(2)}) collective-permute-start(bf16[36,24,128]{2,1,0:T(8,128)(2,1)S(1)} %get-tuple-element.53), channel_id=1, source_target_pairs={{0,128},{128,0},{1,129},{129,1},{2,130},{130,2},{3,131},{131,3},{4... | collective-permute-start | bytes 663560 | tf_op jit(solution)/shard_map/ppermute | solution.py:497
  127.4 2.4 %copy-start.5 = (f32[2,2]{1,0:T(2,128)S(1)}, f32[2,2]{1,0:T(2,128)}, u32[]{:S(2)}) copy-start(f32[2,2]{1,0:T(2,128)} %mix.5) | copy-start | bytes 52
  129.2 7.9 %collective-permute-start.14 = (bf16[20,24,128]{2,1,0:T(8,128)(2,1)S(1)}, bf16[20,24,128]{2,1,0:T(8,128)(2,1)S(1)}, u32[]{:S(2)}, u32[]{:S(2)}) collective-permute-start(bf16[20,24,128]{2,1,0:T(8,128)(2,1)S(1)} %get-tuple-element.51), channel_id=1, source_target_pairs={{0,128},{128,0},{1,129},{129,1},{2,130},{130,2},{3,131},{131,3},{4... | collective-permute-start | bytes 368648 | tf_op jit(solution)/shard_map/ppermute | solution.py:497

commit v3 on v2

--- a/solution.py
+++ b/solution.py
@@ -268,115 +268,106 @@
             put(t, c * grad[384:, lanes] - vel * grad[:384, lanes])
 
 
-def tiles_of(p):
-    return 36 if p < 2 else 20
-
-
-def join_kernel(p, probe, col, *refs):
-    count = 2 if p < 2 else 1
-    base, arrivals = refs[0], refs[1:9]
+CHUNKS = (((4, 5), (3, 4)), ((2, 3), (5, 6)), ((0, 1), (1, 2)), ((6, 7), (7, 0)))
+
+
+def needs(n):
+    return sorted(set(CHUNKS[n][0] + CHUNKS[n][1]))
+
+
+def group_of(n, me):
+    even, odd = CHUNKS[n]
+    return lax.rem(me + jnp.where(lax.rem(me, 2) == 0, even[0], odd[0]), 8) // 2
+
+
+def join_kernel(n, probe, col, *refs):
+    base, arrivals = refs[0], dict(zip(needs(n), refs[1:]))
     out, send, own, rows, sem = refs[-5:]
     first = probe[0] == 0
     me = col[0]
     low = low_lanes((24, 128))
-
-    def give(n, half0, half1):
-        send[n] = jnp.where(first, half1, half0).astype(BF16)
-        own[n] = jnp.where(first, half0, half1).astype(BF16)
-
-    def fill(odd_me):
-        for k in range(4):
-            r = [(2 * k - odd_me) % 8, (2 * k - odd_me + 1) % 8]
-            a = lax.rem(me + r[0], 8) // 2
-
-            def z_tile(b, t, r=r):
-                return arrivals[r[b]][24 * t : 24 * t + 24, :].astype(F32)
-
+    group = group_of(n, me)
+
+    def give(t, half0, half1):
+        send[t] = jnp.where(first, half1, half0).astype(BF16)
+        own[t] = jnp.where(first, half0, half1).astype(BF16)
+
+    def fill(pair):
+        def z_tile(b, t):
+            return arrivals[pair[b]][24 * t : 24 * t + 24, :].astype(F32)
+
+        tails = []
+        for yl in range(3):
+            y = 3 * group + yl
             mids = []
-            for yl in range(3):
-                y = 3 * a + yl
-                for i in range(count):
-                    v = 2 * p + i
-                    full = [z_tile(b, 7 * yl + v) for b in range(2)]
-                    t, odd = (7 * yl + 5 + p, i) if p < 2 else (21 + yl // 2, yl % 2)
-                    m = [z_tile(b, t) for b in range(2)]
-                    if odd:
-                        mid = jnp.where(low, swap(m[0]), m[1])
-                    else:
-                        mid = jnp.where(low, m[0], swap(m[1]))
-                    res = []
-                    for c, part in enumerate((full[0], mid, full[1])):
-                        lanes = slice(128 * c, 128 * c + 128)
-                        total = (base[v, y, :, lanes] + step_size * part).astype(BF16)
-                        rows[i, y, :, lanes] = total
-                        res.append(total.astype(F32))
-                    give(12 * i + y, res[0], res[2])
-                    mids.append(res[1])
-                if p < 2:
-                    pair = mids[-2:]
-                    give(24 + y, merge(0, *pair), merge(1, *pair))
-            if p == 2:
-                none = jnp.zeros((24, 128), F32)
-                give(12 + a, merge(0, mids[0], mids[1]), merge(1, mids[0], mids[1]))
-                give(16 + a, merge(0, mids[2], none), merge(1, mids[2], none))
+            for v in range(5):
+                full = [z_tile(b, 7 * yl + v) for b in range(2)]
+                t, odd = (7 * yl + 5 + v // 2, v % 2) if v < 4 else (21 + yl // 2, yl % 2)
+                m = [z_tile(b, t) for b in range(2)]
+                if odd:
+                    mid = jnp.where(low, swap(m[0]), m[1])
+                else:
+                    mid = jnp.where(low, m[0], swap(m[1]))
+                res = []
+                for c, part in enumerate((full[0], mid, full[1])):
+                    lanes = slice(128 * c, 128 * c + 128)
+                    total = (base[v, y, :, lanes] + step_size * part).astype(BF16)
+                    rows[v, yl, :, lanes] = total
+                    res.append(total.astype(F32))
+                give(5 * yl + v, res[0], res[2])
+                mids.append(res[1])
+            for q in range(2):
+                two = mids[2 * q : 2 * q + 2]
+                give(15 + 2 * yl + q, merge(0, *two), merge(1, *two))
+            tails.append(mids[4])
+        tails.append(jnp.zeros((24, 128), F32))
+        for q in range(2):
+            two = tails[2 * q : 2 * q + 2]
+            give(21 + q, merge(0, *two), merge(1, *two))
 
     for odd_me in range(2):
 
         @pl.when(lax.rem(me, 2) == odd_me)
         def _(odd_me=odd_me):
-            fill(odd_me)
-
-    copies = [
-        pltpu.make_async_copy(rows.at[i], out.at[2 * p + i], sem.at[i]) for i in range(count)
-    ]
-    for copy in copies:
-        copy.start()
-    for copy in copies:
-        copy.wait()
-
-
-def sketch_kernel(q, probe, mix, *refs):
-    count = 2 if q < 2 else 1
+            fill(CHUNKS[n][odd_me])
+
+    copy = pltpu.make_async_copy(rows, out.at[:, pl.ds(3 * group, 3)], sem)
+    copy.start()
+    copy.wait()
+
+
+def sketch_kernel(n, probe, col, mix, *refs):
     own, recv = refs[:2]
     out, rows, sem = refs[-3:]
     p = probe[0]
     low = low_lanes((24, 128))
-
-    def mixed(n, g):
-        a = (own[n].astype(F32) * mix[p, g]).astype(BF16).astype(F32)
-        b = (recv[n].astype(F32) * mix[1 - p, g]).astype(BF16).astype(F32)
+    group = group_of(n, col[0])
+
+    def mixed(t, g):
+        a = (own[t].astype(F32) * mix[p, g]).astype(BF16).astype(F32)
+        b = (recv[t].astype(F32) * mix[1 - p, g]).astype(BF16).astype(F32)
         return a + b
 
-    def put(i, g, y, full, piece):
+    def put(g, v, yl, full, piece):
         turned = swap(full)
         head = jnp.where(p == 0, full, jnp.where(low, piece, turned))
         tail = jnp.where(p == 0, piece, turned)
-        rows[i, g, y, :, 0:128] = head.astype(BF16)
-        rows[i, g, y, :, 128:192] = tail[:, :64].astype(BF16)
-
-    def body(a, carry):
-        for g in range(2):
-            for yl in range(3):
-                y = 3 * a + yl
-                if q < 2:
-                    half = mixed(24 + y, g)
-                    put(0, g, y, mixed(y, g), half)
-                    put(1, g, y, mixed(12 + y, g), swap(half))
-                else:
-                    half = mixed(12 + a if yl < 2 else 16 + a, g)
-                    put(0, g, y, mixed(y, g), swap(half) if yl == 1 else half)
-        return carry
-
-    lax.fori_loop(0, 4, body, 0)
-    copies = [
-        pltpu.make_async_copy(rows.at[i, g], out.at[g, 2 * q + i], sem.at[i, g])
-        for i in range(count)
-        for g in range(2)
-    ]
-    for copy in copies:
-        copy.start()
-    for copy in copies:
-        copy.wait()
+        rows[g, v, yl, :, 0:128] = head.astype(BF16)
+        rows[g, v, yl, :, 128:192] = tail[:, :64].astype(BF16)
+
+    for g in range(2):
+        for yl in range(3):
+            for q in range(2):
+                half = mixed(15 + 2 * yl + q, g)
+                put(g, 2 * q, yl, mixed(5 * yl + 2 * q, g), half)
+                put(g, 2 * q + 1, yl, mixed(5 * yl + 2 * q + 1, g), swap(half))
+        half = mixed(21, g)
+        put(g, 4, 0, mixed(4, g), half)
+        put(g, 4, 1, mixed(9, g), swap(half))
+        put(g, 4, 2, mixed(14, g), mixed(22, g))
+    copy = pltpu.make_async_copy(rows, out.at[:, :, pl.ds(3 * group, 3)], sem)
+    copy.start()
+    copy.wait()
 
 
 def call(kernel, out_shapes, scalars, arrays, scratch=(), kept=(), spaces=None, stay=False):
@@ -479,32 +470,27 @@
     )
     pieces = [far(back_z[0])] + [near(x) for x in back_z[1:]]
     sections, sketches, halves = [], [], []
-    for p in range(3):
-        count = 2 if p < 2 else 1
+    for n in range(4):
         section, send, own = call(
-            functools.partial(join_kernel, p),
-            [shape((5, 12, 24, 384)), held((tiles_of(p), 24, 128)), held((tiles_of(p), 24, 128))],
+            functools.partial(join_kernel, n),
+            [shape((5, 12, 24, 384)), held((23, 24, 128)), held((23, 24, 128))],
             [probe, col],
-            [near(base)] + pieces,
-            [
-                pltpu.VMEM((count, 12, 24, 384), BF16),
-                pltpu.SemaphoreType.DMA((count,)),
-            ],
+            [near(base)] + [pieces[r] for r in needs(n)],
+            [pltpu.VMEM((5, 3, 24, 384), BF16), pltpu.SemaphoreType.DMA],
             kept=sections[-1:],
             spaces=[any_space, vspec(), vspec()],
         )
         sections.append(section)
         halves.append((own, lax.ppermute(send, "probe", [(0, 1), (1, 0)])))
-    for p in range(3):
-        count = 2 if p < 2 else 1
-        own, recv = halves[p]
+    for n in range(4):
+        own, recv = halves[n]
         sketches.append(
             call(
-                functools.partial(sketch_kernel, p),
+                functools.partial(sketch_kernel, n),
                 [shape((2, 5, 12, 24, 192))],
-                [probe, test_mix],
+                [probe, col, test_mix],
                 [near(own), near(recv)],
-                [pltpu.VMEM((count, 2, 12, 24, 192), BF16), pltpu.SemaphoreType.DMA((count, 2))],
+                [pltpu.VMEM((2, 5, 3, 24, 192), BF16), pltpu.SemaphoreType.DMA],
                 kept=sketches[-1:],
                 spaces=[any_space],
             )[0]

time: 141 us -> 138 us (0.979)
  the two profiles are of different devices: /device:TPU:1 before, /device:TPU:36 now
where the time goes in v3:
time: 138 us
  waiting for transfers between devices  53.5 us (39%)
  starting transfers between devices  48.7 us (35%)
  Pallas kernels  31.5 us (23%)
  local copies, waits for them, and re-layouts  2.87 us (2%)
    ppermute x14, waiting for transfers between devices, shift(): return lax.ppermute(x, 'col', [(i, (i + distance) % 8) for i in range(8)])  37.9 us
    pallas_call x14, Pallas kernels, call(): pl.pallas_call(kernel, out_shape=out_shapes, in_specs=[sspec()] * len(sca...  31.5 us
    ppermute x14, starting transfers between devices, shift(): return lax.ppermute(x, 'col', [(i, (i + distance) % 8) for i in range(8)])  30.3 us
    all_to_all x1, waiting for transfers between devices, on_device(): lax.all_to_all(to_y.reshape(16, 336, 128), 'row', split_axis=0, concat_ax...  15.6 us
    all_to_all x1, starting transfers between devices, on_device(): lax.all_to_all(to_y.reshape(16, 336, 128), 'row', split_axis=0, concat_ax...  7.46 us
    all_to_all x1, starting transfers between devices, on_device(): lax.all_to_all(term_y, 'row', split_axis=0, concat_axis=0, tiled=True)  6.59 us
    ppermute x4, starting transfers between devices, on_device(): halves.append((own, lax.ppermute(send, 'probe', [(0, 1), (1, 0)])))  4.31 us
    unnamed x18, local copies, waits for them, and re-layouts  2.87 us
  transfers between devices with their start and end apart: 20, of which 6 were waited for; matrix products, arithmetic and copies ran while one was open for 0% of the time, Pallas kernels for 17%

profile of v3, /device:TPU:36, one launch (start us, length us, event | category | flops | bytes accessed | tf_op | source)
XLA Modules:
  0.0 137.5 jit_solution(17622608400666444343)
XLA Ops:
  0.6 2.8 %shard_map.113 = bf16[8,2,336,128]{3,2,1,0:T(8,128)(2,1)} custom-call(bf16[5,12,24,384]{3,2,1,0:T(8,128)(2,1)} %bitcast.7, bf16[12,24,384]{2,1,0:T(8,128)(2,1)} %adv_far.1), custom_call_target="tpu_custom_call" | custom-call | tf_op jit(solution)/shard_map/pallas_call | solution.py:377
  3.4 0.0 copy-start.8
  3.4 7.5 %all-to-all-start = ((bf16[16,336,128]{2,1,0:T(8,128)(2,1)}), bf16[16,336,128]{2,1,0:T(8,128)(2,1)S(1)}, u32[]{:S(2)}, u32[]{:S(2)}) async-start(bf16[16,336,128]{2,1,0:T(8,128)(2,1)} %bitcast.4), calls=%async_computation | async-start | bytes 2752512 | tf_op jit(solution)/shard_map/all_to_all | solution.py:440
  10.9 3.1 %shard_map.114 = (bf16[1152,384]{1,0:T(8,128)(2,1)}, bf16[384,192]{1,0:T(8,128)(2,1)}) custom-call(s32[1]{0:T(128)} %bitcast.1.col, bf16[2,192,192]{2,1,0:T(8,128)(2,1)} %mat_y.1, bf16[2,192,192]{2,1,0:T(8,128)(2,1)} %mat_z.1), custom_call_target="tpu_custom_call" | custom-call | tf_op jit(solution)/shard_map/pallas_call | solution.py:377
  14.0 15.6 %all-to-all-done.recv = bf16[16,336,128]{2,1,0:T(8,128)(2,1)S(1)} async-done(((bf16[16,336,128]{2,1,0:T(8,128)(2,1)}), bf16[16,336,128]{2,1,0:T(8,128)(2,1)S(1)}, u32[]{:S(2)}, u32[]{:S(2)}) %all-to-all-start) | async-done | bytes 1376288 | tf_op jit(solution)/shard_map/all_to_all | solution.py:440
  29.6 4.2 %shard_map.115 = bf16[16,336,128]{2,1,0:T(8,128)(2,1)} custom-call(f32[5]{0:T(128)S(1)} %copy-done.8, bf16[16,336,128]{2,1,0:T(8,128)(2,1)S(1)} %all-to-all-done.recv, bf16[1152,384]{1,0:T(8,128)(2,1)} %get-tuple-element.32.lines), custom_call_target="tpu_custom_call" | custom-call | tf_op jit(solution)/shard_map/pallas_call | solution.py:377
  33.8 6.6 %all-to-all-start.1 = ((bf16[16,336,128]{2,1,0:T(8,128)(2,1)}), bf16[16,336,128]{2,1,0:T(8,128)(2,1)S(1)}, u32[]{:S(2)}, u32[]{:S(2)}) async-start(bf16[16,336,128]{2,1,0:T(8,128)(2,1)} %shard_map.115), calls=%async_computation.1 | async-start | bytes 2752512 | tf_op jit(solution)/shard_map/all_to_all | solution.py:454
  40.4 0.0 copy-start.2
  40.4 2.6 %shard_map.117 = (bf16[648,128]{1,0:T(8,128)(2,1)}, bf16[648,128]{1,0:T(8,128)(2,1)S(1)}, bf16[648,128]{1,0:T(8,128)(2,1)S(1)}, bf16[648,128]{1,0:T(8,128)(2,1)S...) custom-call(s32[1]{0:T(128)} %bitcast.1.col, ...), custom_call_target="tpu_custom_call" | custom-call | tf_op jit(solution)/shard_map/pallas_call | solution.py:377
  43.0 1.9 %collective-permute-start = (bf16[648,128]{1,0:T(8,128)(2,1)S(1)}, bf16[648,128]{1,0:T(8,128)(2,1)S(1)}, u32[]{:S(2)}, u32[]{:S(2)}) collective-permute-start(bf16[648,128]{1,0:T(8,128)(2,1)S(1)} %get-tuple-element.34), channel_id=1, source_target_pairs={{0,1},{1,2},{2,3},{3,4},{4,5},{5,6},{6,7},{7,0},{8,9},{9,10},{10,1... | collective-permute-start | bytes 497672 | tf_op jit(solution)/shard_map/ppermute | solution.py:399
  44.9 4.5 %collective-permute-start.1 = (bf16[648,128]{1,0:T(8,128)(2,1)S(1)}, bf16[648,128]{1,0:T(8,128)(2,1)S(1)}, u32[]{:S(2)}, u32[]{:S(2)}) collective-permute-start(bf16[648,128]{1,0:T(8,128)(2,1)S(1)} %get-tuple-element.35), channel_id=1, source_target_pairs={{0,2},{1,3},{2,4},{3,5},{4,6},{5,7},{6,0},{7,1},{8,10},{9,11},{10,... | collective-permute-start | bytes 497672 | tf_op jit(solution)/shard_map/ppermute | solution.py:399
  49.4 1.9 %collective-permute-start.2 = (bf16[648,128]{1,0:T(8,128)(2,1)S(1)}, bf16[648,128]{1,0:T(8,128)(2,1)S(1)}, u32[]{:S(2)}, u32[]{:S(2)}) collective-permute-start(bf16[648,128]{1,0:T(8,128)(2,1)S(1)} %get-tuple-element.36), channel_id=1, source_target_pairs={{0,3},{1,4},{2,5},{3,6},{4,7},{5,0},{6,1},{7,2},{8,11},{9,12},{10,... | collective-permute-start | bytes 497672 | tf_op jit(solution)/shard_map/ppermute | solution.py:399
  51.4 1.4 %collective-permute-start.3 = (bf16[648,128]{1,0:T(8,128)(2,1)S(1)}, bf16[648,128]{1,0:T(8,128)(2,1)S(1)}, u32[]{:S(2)}, u32[]{:S(2)}) collective-permute-start(bf16[648,128]{1,0:T(8,128)(2,1)S(1)} %get-tuple-element.37), channel_id=1, source_target_pairs={{0,4},{1,5},{2,6},{3,7},{4,0},{5,1},{6,2},{7,3},{8,12},{9,13},{10,... | collective-permute-start | bytes 497672 | tf_op jit(solution)/shard_map/ppermute | solution.py:399
  52.8 3.0 %collective-permute-start.4 = (bf16[648,128]{1,0:T(8,128)(2,1)S(1)}, bf16[648,128]{1,0:T(8,128)(2,1)S(1)}, u32[]{:S(2)}, u32[]{:S(2)}) collective-permute-start(bf16[648,128]{1,0:T(8,128)(2,1)S(1)} %get-tuple-element.38), channel_id=1, source_target_pairs={{0,5},{1,6},{2,7},{3,0},{4,1},{5,2},{6,3},{7,4},{8,13},{9,14},{10,... | collective-permute-start | bytes 497672 | tf_op jit(solution)/shard_map/ppermute | solution.py:399
  55.8 0.0 collective-permute-done.refs_1_
  55.8 2.5 %collective-permute-start.5 = (bf16[648,128]{1,0:T(8,128)(2,1)S(1)}, bf16[648,128]{1,0:T(8,128)(2,1)S(1)}, u32[]{:S(2)}, u32[]{:S(2)}) collective-permute-start(bf16[648,128]{1,0:T(8,128)(2,1)S(1)} %get-tuple-element.39), channel_id=1, source_target_pairs={{0,6},{1,7},{2,0},{3,1},{4,2},{5,3},{6,4},{7,5},{8,14},{9,15},{10,... | collective-permute-start | bytes 497672 | tf_op jit(solution)/shard_map/ppermute | solution.py:399
  58.3 2.8 %collective-permute-done.1.refs_2_ = bf16[648,128]{1,0:T(8,128)(2,1)S(1)} collective-permute-done((bf16[648,128]{1,0:T(8,128)(2,1)S(1)}, bf16[648,128]{1,0:T(8,128)(2,1)S(1)}, u32[]{:S(2)}, u32[]{:S(2)}) %collective-permute-start.1) | collective-permute-done | bytes 165920 | tf_op jit(solution)/shard_map/ppermute | solution.py:399
  61.1 2.7 %collective-permute-start.6 = (bf16[648,128]{1,0:T(8,128)(2,1)S(1)}, bf16[648,128]{1,0:T(8,128)(2,1)S(1)}, u32[]{:S(2)}, u32[]{:S(2)}) collective-permute-start(bf16[648,128]{1,0:T(8,128)(2,1)S(1)} %get-tuple-element.40), channel_id=1, source_target_pairs={{0,7},{1,0},{2,1},{3,2},{4,3},{5,4},{6,5},{7,6},{8,15},{9,8},{10,9... | collective-permute-start | bytes 497672 | tf_op jit(solution)/shard_map/ppermute | solution.py:399
  63.8 12.5 %collective-permute-done.2.refs_3_ = bf16[648,128]{1,0:T(8,128)(2,1)S(1)} collective-permute-done((bf16[648,128]{1,0:T(8,128)(2,1)S(1)}, bf16[648,128]{1,0:T(8,128)(2,1)S(1)}, u32[]{:S(2)}, u32[]{:S(2)}) %collective-permute-start.2) | collective-permute-done | bytes 165920 | tf_op jit(solution)/shard_map/ppermute | solution.py:399
  76.3 6.4 %collective-permute-done.5.refs_6_ = bf16[648,128]{1,0:T(8,128)(2,1)S(1)} collective-permute-done((bf16[648,128]{1,0:T(8,128)(2,1)S(1)}, bf16[648,128]{1,0:T(8,128)(2,1)S(1)}, u32[]{:S(2)}, u32[]{:S(2)}) %collective-permute-start.5) | collective-permute-done | bytes 165920 | tf_op jit(solution)/shard_map/ppermute | solution.py:399
  82.7 2.1 %collective-permute-done.6.refs_7_ = bf16[648,128]{1,0:T(8,128)(2,1)S(1)} collective-permute-done((bf16[648,128]{1,0:T(8,128)(2,1)S(1)}, bf16[648,128]{1,0:T(8,128)(2,1)S(1)}, u32[]{:S(2)}, u32[]{:S(2)}) %collective-permute-start.6) | collective-permute-done | bytes 165920 | tf_op jit(solution)/shard_map/ppermute | solution.py:399
  84.8 2.7 %shard_map.118 = (bf16[552,128]{1,0:T(8,128)(2,1)}, bf16[552,128]{1,0:T(8,128)(2,1)}, bf16[552,128]{1,0:T(8,128)(2,1)}, bf16[552,128]{1,0:T(8,128)(2,1)S(1)}, bf...) custom-call(f32[5]{0:T(128)S(1)} %copy-done.8, ...), custom_call_target="tpu_custom_call" | custom-call | tf_op jit(solution)/shard_map/pallas_call | solution.py:377
  87.5 0.2 collective-permute-start.11
  87.7 4.8 %collective-permute-start.12 = (bf16[552,128]{1,0:T(8,128)(2,1)S(1)}, bf16[552,128]{1,0:T(8,128)(2,1)S(1)}, u32[]{:S(2)}, u32[]{:S(2)}) collective-permute-start(bf16[552,128]{1,0:T(8,128)(2,1)S(1)} %get-tuple-element.48), channel_id=1, source_target_pairs={{0,3},{1,4},{2,5},{3,6},{4,7},{5,0},{6,1},{7,2},{8,11},{9,12},{10,... | collective-permute-start | bytes 423944 | tf_op jit(solution)/shard_map/ppermute | solution.py:399
  92.5 1.1 collective-permute-start.13
  93.6 1.8 %collective-permute-start.7 = (bf16[552,128]{1,0:T(8,128)(2,1)}, bf16[552,128]{1,0:T(8,128)(2,1)S(1)}, u32[]{:S(2)}, u32[]{:S(2)}) collective-permute-start(bf16[552,128]{1,0:T(8,128)(2,1)} %get-tuple-element.43), channel_id=1, source_target_pairs={{0,2},{1,3},{2,4},{3,5},{4,6},{5,7},{6,0},{7,1},{8,10},{9,11},{10,... | collective-permute-start | bytes 423944 | tf_op jit(solution)/shard_map/ppermute | solution.py:399
  95.4 2.4 %collective-permute-start.10 = (bf16[552,128]{1,0:T(8,128)(2,1)}, bf16[552,128]{1,0:T(8,128)(2,1)S(1)}, u32[]{:S(2)}, u32[]{:S(2)}) collective-permute-start(bf16[552,128]{1,0:T(8,128)(2,1)} %get-tuple-element.46), channel_id=1, source_target_pairs={{0,6},{1,7},{2,0},{3,1},{4,2},{5,3},{6,4},{7,5},{8,14},{9,15},{10,... | collective-permute-start | bytes 423944 | tf_op jit(solution)/shard_map/ppermute | solution.py:399
  97.8 14.1 %collective-permute-done.11.refs_1_.refs_2_ = bf16[552,128]{1,0:T(8,128)(2,1)S(1)} collective-permute-done((bf16[552,128]{1,0:T(8,128)(2,1)S(1)}, bf16[552,128]{1,0:T(8,128)(2,1)S(1)}, u32[]{:S(2)}, u32[]{:S(2)}) %collective-permute-start.11) | collective-permute-done | bytes 141344 | tf_op jit(solution)/shard_map/ppermute | solution.py:399
  111.9 0.7 copy-done.3
  112.6 2.0 %collective-permute-start.8 = (bf16[552,128]{1,0:T(8,128)(2,1)}, bf16[552,128]{1,0:T(8,128)(2,1)}, u32[]{:S(2)}, u32[]{:S(2)}) collective-permute-start(bf16[552,128]{1,0:T(8,128)(2,1)} %get-tuple-element.44), channel_id=1, source_target_pairs={{0,1},{1,2},{2,3},{3,4},{4,5},{5,6},{6,7},{7,0},{8,9},{9,10},{10,1... | collective-permute-start | bytes 423944 | tf_op jit(solution)/shard_map/ppermute | solution.py:399
  114.6 1.2 copy-done.1
  115.8 0.9 copy-done.6
  116.8 3.1 %shard_map.116.refs_0_ = f32[5,12,24,384]{3,2,1,0:T(8,128)S(1)} custom-call(f32[5]{0:T(128)S(1)} %copy-done.8, bf16[5,12,24,384]{3,2,1,0:T(8,128)(2,1)S(1)} %bitcast.9, bf16[5,12,24,384]{3,2,1,0:T(8,128)(2,1)S(1)} %bitcast.11, bf16[12,24,384]{2,1,0:T(8,128)(2,1)S(1)} %copy-done.6, bf16[2,384,384]{2,1,0:T(8,128)(2,1)S(1)} %copy-done.2, ...), custom_call_target="tpu_custom_call" | custom-call | tf_op jit(solution)/shard_map/pallas_call | solution.py:377
  119.9 0.0 collective-permute-done.13.refs_2_
  119.9 1.9 %shard_map.119 = (bf16[5,12,24,384]{3,2,1,0:T(8,128)(2,1)}, bf16[23,24,128]{2,1,0:T(8,128)(2,1)S(1)}, bf16[23,24,128]{2,1,0:T(8,128)(2,1)S(1)}) custom-call(s32[1]{0:T(128)} %bitcast.probe, s32[1]{0:T(128)} %bitcast.1.col, f32[5,12,24,384]{3,2,1,0:T(8,128)S(1)} %shard_map.116.refs_0_, bf16[552,128]{1,0:T(8,128)(2,1)S(1)} %collective-permute-done.11.refs_1_.refs_2_, ...), custom_call_target="tpu_custom_call" | custom-call | tf_op jit(solution)/shard_map/pallas_call | solution.py:377
  121.8 0.0 collective-permute-done.7.refs_4_.refs_2_
  121.8 0.0 collective-permute-done.10.refs_1_.refs_3_
  121.9 1.0 shard_map.120
  122.9 1.3 collective-permute-start.16
  124.1 0.8 collective-permute-start.17
  125.0 1.9 %shard_map.121 = (bf16[5,12,24,384]{3,2,1,0:T(8,128)(2,1)}, bf16[23,24,128]{2,1,0:T(8,128)(2,1)S(1)}, bf16[23,24,128]{2,1,0:T(8,128)(2,1)S(1)}) custom-call(s32[1]{0:T(128)} %bitcast.probe, s32[1]{0:T(128)} %bitcast.1.col, f32[5,12,24,384]{3,2,1,0:T(8,128)S(1)} %shard_map.116.refs_0_, ...), custom_call_target="tpu_custom_call", output_to_operand_aliasing={{0}: (6, {})} | custom-call | tf_op jit(solution)/shard_map/pallas_call | solution.py:377
  126.9 1.3 collective-permute-start.15
  128.2 2.0 %shard_map.122 = (bf16[5,12,24,384]{3,2,1,0:T(8,128)(2,1)}, bf16[23,24,128]{2,1,0:T(8,128)(2,1)S(1)}, bf16[23,24,128]{2,1,0:T(8,128)(2,1)S(1)}) custom-call(s32[1]{0:T(128)} %bitcast.probe, s32[1]{0:T(128)} %bitcast.1.col, f32[5,12,24,384]{3,2,1,0:T(8,128)S(1)} %shard_map.116.refs_0_, ...), custom_call_target="tpu_custom_call", output_to_operand_aliasing={{0}: (6, {})} | custom-call | tf_op jit(solution)/shard_map/pallas_call | solution.py:377
  130.2 0.9 collective-permute-start.14
  131.1 1.5 %shard_map.123.refs_2_ = bf16[2,5,12,24,192]{4,3,2,1,0:T(8,128)(2,1)} custom-call(s32[1]{0:T(128)} %bitcast.probe, s32[1]{0:T(128)} %bitcast.1.col, f32[2,2]{1,0:T(2,128)S(1)} %copy-done.7, bf16[23,24,128]{2,1,0:T(8,128)(2,1)S(1)} %get-tuple-element.60.refs_0_, bf16[23,24,128]{2,1,0:T(8,128)(2,1)S(1)} %collective-permute-done.17.refs_1_), custom_call_target="tpu_custom_call" | custom-call | tf_op jit(solution)/shard_map/pallas_call | solution.py:377
  132.7 1.5 %shard_map.124.refs_2_ = bf16[2,5,12,24,192]{4,3,2,1,0:T(8,128)(2,1)} custom-call(s32[1]{0:T(128)} %bitcast.probe, s32[1]{0:T(128)} %bitcast.1.col, f32[2,2]{1,0:T(2,128)S(1)} %copy-done.7, bf16[23,24,128]{2,1,0:T(8,128)(2,1)S(1)} %get-tuple-element.58.refs_0_, ...), custom_call_target="tpu_custom_call", output_to_operand_aliasing={{}: (5, {})} | custom-call | tf_op jit(solution)/shard_map/pallas_call | solution.py:377
  134.2 1.5 %shard_map.125.refs_2_ = bf16[2,5,12,24,192]{4,3,2,1,0:T(8,128)(2,1)} custom-call(s32[1]{0:T(128)} %bitcast.probe, s32[1]{0:T(128)} %bitcast.1.col, f32[2,2]{1,0:T(2,128)S(1)} %copy-done.7, bf16[23,24,128]{2,1,0:T(8,128)(2,1)S(1)} %get-tuple-element.56.refs_0_, ...), custom_call_target="tpu_custom_call", output_to_operand_aliasing={{}: (5, {})} | custom-call | tf_op jit(solution)/shard_map/pallas_call | solution.py:377
  135.8 1.5 %shard_map.126 = bf16[2,5,12,24,192]{4,3,2,1,0:T(8,128)(2,1)} custom-call(s32[1]{0:T(128)} %bitcast.probe, s32[1]{0:T(128)} %bitcast.1.col, f32[2,2]{1,0:T(2,128)S(1)} %copy-done.7, bf16[23,24,128]{2,1,0:T(8,128)(2,1)S(1)} %get-tuple-element.54.refs_0_, bf16[23,24,128]{2,1,0:T(8,128)(2,1)S(1)} %collective-permute-done.14.refs_1_, ...), custom_call_target="tpu_custom_call", output_to_operand_aliasing={{}: (5, {})} | custom-call | tf_op jit(solution)/shard_map/pallas_call | solution.py:377
  (24 shorter events, 0.1 us)
Async XLA Ops:
  3.4 26.2 %copy-start.8 = (f32[5]{0:T(128)S(1)}, f32[5]{0:T(128)}, u32[]{:S(2)}) copy-start(f32[5]{0:T(128)} %coef.5) | copy-start | bytes 64
  3.4 26.2 %all-to-all-start = ((bf16[16,336,128]{2,1,0:T(8,128)(2,1)}), bf16[16,336,128]{2,1,0:T(8,128)(2,1)S(1)}, u32[]{:S(2)}, u32[]{:S(2)}) async-start(bf16[16,336,128]{2,1,0:T(8,128)(2,1)} %bitcast.4), calls=%async_computation | async-start | bytes 2752512 | tf_op jit(solution)/shard_map/all_to_all | solution.py:440
  33.8 6.6 %copy-start = (bf16[1,5,12,24,384]{4,3,2,1,0:T(8,128)(2,1)S(1)}, bf16[1,5,12,24,384]{4,3,2,1,0:T(8,128)(2,1)}, u32[]{:S(2)}) copy-start(bf16[1,5,12,24,384]{4,3,2,1,0:T(8,128)(2,1)} %param.10) | copy-start | bytes 3317764
  33.8 6.6 %copy-start.5 = (bf16[12,24,384]{2,1,0:T(8,128)(2,1)S(1)}, bf16[12,24,384]{2,1,0:T(8,128)(2,1)}, u32[]{:S(2)}) copy-start(bf16[12,24,384]{2,1,0:T(8,128)(2,1)} %adv.3) | copy-start | bytes 663556
  33.8 80.8 %all-to-all-start.1 = ((bf16[16,336,128]{2,1,0:T(8,128)(2,1)}), bf16[16,336,128]{2,1,0:T(8,128)(2,1)S(1)}, u32[]{:S(2)}, u32[]{:S(2)}) async-start(bf16[16,336,128]{2,1,0:T(8,128)(2,1)} %shard_map.115), calls=%async_computation.1 | async-start | bytes 2752512 | tf_op jit(solution)/shard_map/all_to_all | solution.py:454
  40.4 74.2 %copy-start.2 = (bf16[2,384,384]{2,1,0:T(8,128)(2,1)S(1)}, bf16[2,384,384]{2,1,0:T(8,128)(2,1)}, u32[]{:S(2)}) copy-start(bf16[2,384,384]{2,1,0:T(8,128)(2,1)} %mat.1) | copy-start | bytes 1769476
  43.0 12.8 %collective-permute-start = (bf16[648,128]{1,0:T(8,128)(2,1)S(1)}, bf16[648,128]{1,0:T(8,128)(2,1)S(1)}, u32[]{:S(2)}, u32[]{:S(2)}) collective-permute-start(bf16[648,128]{1,0:T(8,128)(2,1)S(1)} %get-tuple-element.34), channel_id=1, source_target_pairs={{0,1},{1,2},{2,3},{3,4},{4,5},{5,6},{6,7},{7,0},{8,9},{9,10},{10,1... | collective-permute-start | bytes 497672 | tf_op jit(solution)/shard_map/ppermute | solution.py:399
  44.9 16.1 %collective-permute-start.1 = (bf16[648,128]{1,0:T(8,128)(2,1)S(1)}, bf16[648,128]{1,0:T(8,128)(2,1)S(1)}, u32[]{:S(2)}, u32[]{:S(2)}) collective-permute-start(bf16[648,128]{1,0:T(8,128)(2,1)S(1)} %get-tuple-element.35), channel_id=1, source_target_pairs={{0,2},{1,3},{2,4},{3,5},{4,6},{5,7},{6,0},{7,1},{8,10},{9,11},{10,... | collective-permute-start | bytes 497672 | tf_op jit(solution)/shard_map/ppermute | solution.py:399
  49.4 26.9 %collective-permute-start.2 = (bf16[648,128]{1,0:T(8,128)(2,1)S(1)}, bf16[648,128]{1,0:T(8,128)(2,1)S(1)}, u32[]{:S(2)}, u32[]{:S(2)}) collective-permute-start(bf16[648,128]{1,0:T(8,128)(2,1)S(1)} %get-tuple-element.36), channel_id=1, source_target_pairs={{0,3},{1,4},{2,5},{3,6},{4,7},{5,0},{6,1},{7,2},{8,11},{9,12},{10,... | collective-permute-start | bytes 497672 | tf_op jit(solution)/shard_map/ppermute | solution.py:399
  51.4 25.0 %collective-permute-start.3 = (bf16[648,128]{1,0:T(8,128)(2,1)S(1)}, bf16[648,128]{1,0:T(8,128)(2,1)S(1)}, u32[]{:S(2)}, u32[]{:S(2)}) collective-permute-start(bf16[648,128]{1,0:T(8,128)(2,1)S(1)} %get-tuple-element.37), channel_id=1, source_target_pairs={{0,4},{1,5},{2,6},{3,7},{4,0},{5,1},{6,2},{7,3},{8,12},{9,13},{10,... | collective-permute-start | bytes 497672 | tf_op jit(solution)/shard_map/ppermute | solution.py:399
  52.8 23.5 %collective-permute-start.4 = (bf16[648,128]{1,0:T(8,128)(2,1)S(1)}, bf16[648,128]{1,0:T(8,128)(2,1)S(1)}, u32[]{:S(2)}, u32[]{:S(2)}) collective-permute-start(bf16[648,128]{1,0:T(8,128)(2,1)S(1)} %get-tuple-element.38), channel_id=1, source_target_pairs={{0,5},{1,6},{2,7},{3,0},{4,1},{5,2},{6,3},{7,4},{8,13},{9,14},{10,... | collective-permute-start | bytes 497672 | tf_op jit(solution)/shard_map/ppermute | solution.py:399
  55.8 26.9 %collective-permute-start.5 = (bf16[648,128]{1,0:T(8,128)(2,1)S(1)}, bf16[648,128]{1,0:T(8,128)(2,1)S(1)}, u32[]{:S(2)}, u32[]{:S(2)}) collective-permute-start(bf16[648,128]{1,0:T(8,128)(2,1)S(1)} %get-tuple-element.39), channel_id=1, source_target_pairs={{0,6},{1,7},{2,0},{3,1},{4,2},{5,3},{6,4},{7,5},{8,14},{9,15},{10,... | collective-permute-start | bytes 497672 | tf_op jit(solution)/shard_map/ppermute | solution.py:399
  61.1 23.7 %collective-permute-start.6 = (bf16[648,128]{1,0:T(8,128)(2,1)S(1)}, bf16[648,128]{1,0:T(8,128)(2,1)S(1)}, u32[]{:S(2)}, u32[]{:S(2)}) collective-permute-start(bf16[648,128]{1,0:T(8,128)(2,1)S(1)} %get-tuple-element.40), channel_id=1, source_target_pairs={{0,7},{1,0},{2,1},{3,2},{4,3},{5,4},{6,5},{7,6},{8,15},{9,8},{10,9... | collective-permute-start | bytes 497672 | tf_op jit(solution)/shard_map/ppermute | solution.py:399
  87.5 24.4 %collective-permute-start.11 = (bf16[552,128]{1,0:T(8,128)(2,1)S(1)}, bf16[552,128]{1,0:T(8,128)(2,1)S(1)}, u32[]{:S(2)}, u32[]{:S(2)}) collective-permute-start(bf16[552,128]{1,0:T(8,128)(2,1)S(1)} %get-tuple-element.47), channel_id=1, source_target_pairs={{0,5},{1,6},{2,7},{3,0},{4,1},{5,2},{6,3},{7,4},{8,13},{9,14},{10,... | collective-permute-start | bytes 423944 | tf_op jit(solution)/shard_map/ppermute | solution.py:399
  87.7 24.2 %collective-permute-start.12 = (bf16[552,128]{1,0:T(8,128)(2,1)S(1)}, bf16[552,128]{1,0:T(8,128)(2,1)S(1)}, u32[]{:S(2)}, u32[]{:S(2)}) collective-permute-start(bf16[552,128]{1,0:T(8,128)(2,1)S(1)} %get-tuple-element.48), channel_id=1, source_target_pairs={{0,3},{1,4},{2,5},{3,6},{4,7},{5,0},{6,1},{7,2},{8,11},{9,12},{10,... | collective-permute-start | bytes 423944 | tf_op jit(solution)/shard_map/ppermute | solution.py:399
  92.5 27.4 %collective-permute-start.13 = (bf16[552,128]{1,0:T(8,128)(2,1)}, bf16[552,128]{1,0:T(8,128)(2,1)}, u32[]{:S(2)}, u32[]{:S(2)}) collective-permute-start(bf16[552,128]{1,0:T(8,128)(2,1)} %get-tuple-element.49), channel_id=1, source_target_pairs={{0,4},{1,5},{2,6},{3,7},{4,0},{5,1},{6,2},{7,3},{8,12},{9,13},{10,... | collective-permute-start | bytes 423944 | tf_op jit(solution)/shard_map/ppermute | solution.py:399
  93.6 28.2 %collective-permute-start.7 = (bf16[552,128]{1,0:T(8,128)(2,1)}, bf16[552,128]{1,0:T(8,128)(2,1)S(1)}, u32[]{:S(2)}, u32[]{:S(2)}) collective-permute-start(bf16[552,128]{1,0:T(8,128)(2,1)} %get-tuple-element.43), channel_id=1, source_target_pairs={{0,2},{1,3},{2,4},{3,5},{4,6},{5,7},{6,0},{7,1},{8,10},{9,11},{10,... | collective-permute-start | bytes 423944 | tf_op jit(solution)/shard_map/ppermute | solution.py:399
  95.4 26.5 %collective-permute-start.10 = (bf16[552,128]{1,0:T(8,128)(2,1)}, bf16[552,128]{1,0:T(8,128)(2,1)S(1)}, u32[]{:S(2)}, u32[]{:S(2)}) collective-permute-start(bf16[552,128]{1,0:T(8,128)(2,1)} %get-tuple-element.46), channel_id=1, source_target_pairs={{0,6},{1,7},{2,0},{3,1},{4,2},{5,3},{6,4},{7,5},{8,14},{9,15},{10,... | collective-permute-start | bytes 423944 | tf_op jit(solution)/shard_map/ppermute | solution.py:399
  111.9 13.1 %collective-permute-start.9 = (bf16[552,128]{1,0:T(8,128)(2,1)}, bf16[552,128]{1,0:T(8,128)(2,1)}, u32[]{:S(2)}, u32[]{:S(2)}) collective-permute-start(bf16[552,128]{1,0:T(8,128)(2,1)} %get-tuple-element.45), channel_id=1, source_target_pairs={{0,7},{1,0},{2,1},{3,2},{4,3},{5,4},{6,5},{7,6},{8,15},{9,8},{10,9... | collective-permute-start | bytes 423944 | tf_op jit(solution)/shard_map/ppermute | solution.py:399
  111.9 0.7 copy-start.3
  112.6 15.7 %collective-permute-start.8 = (bf16[552,128]{1,0:T(8,128)(2,1)}, bf16[552,128]{1,0:T(8,128)(2,1)}, u32[]{:S(2)}, u32[]{:S(2)}) collective-permute-start(bf16[552,128]{1,0:T(8,128)(2,1)} %get-tuple-element.44), channel_id=1, source_target_pairs={{0,1},{1,2},{2,3},{3,4},{4,5},{5,6},{6,7},{7,0},{8,9},{9,10},{10,1... | collective-permute-start | bytes 423944 | tf_op jit(solution)/shard_map/ppermute | solution.py:399
  114.6 1.2 copy-start.1
  115.8 0.9 copy-start.6
  116.8 3.2 %copy-start.4 = (bf16[552,128]{1,0:T(8,128)(2,1)S(1)}, bf16[552,128]{1,0:T(8,128)(2,1)}, u32[]{:S(2)}) copy-start(bf16[552,128]{1,0:T(8,128)(2,1)} %copy-done.3) | copy-start | bytes 423940
  122.9 9.8 %collective-permute-start.16 = (bf16[23,24,128]{2,1,0:T(8,128)(2,1)S(1)}, bf16[23,24,128]{2,1,0:T(8,128)(2,1)S(1)}, u32[]{:S(2)}, u32[]{:S(2)}) collective-permute-start(bf16[23,24,128]{2,1,0:T(8,128)(2,1)S(1)} %get-tuple-element.59), channel_id=1, source_target_pairs={{0,128},{128,0},{1,129},{129,1},{2,130},{130,2},{3,131},{131,3},{4... | collective-permute-start | bytes 423944 | tf_op jit(solution)/shard_map/ppermute | solution.py:484
  124.1 7.0 %collective-permute-start.17 = (bf16[23,24,128]{2,1,0:T(8,128)(2,1)S(1)}, bf16[23,24,128]{2,1,0:T(8,128)(2,1)S(1)}, u32[]{:S(2)}, u32[]{:S(2)}) collective-permute-start(bf16[23,24,128]{2,1,0:T(8,128)(2,1)S(1)} %get-tuple-element.61), channel_id=1, source_target_pairs={{0,128},{128,0},{1,129},{129,1},{2,130},{130,2},{3,131},{131,3},{4... | collective-permute-start | bytes 423944 | tf_op jit(solution)/shard_map/ppermute | solution.py:484
  126.9 7.3 %collective-permute-start.15 = (bf16[23,24,128]{2,1,0:T(8,128)(2,1)S(1)}, bf16[23,24,128]{2,1,0:T(8,128)(2,1)S(1)}, u32[]{:S(2)}, u32[]{:S(2)}) collective-permute-start(bf16[23,24,128]{2,1,0:T(8,128)(2,1)S(1)} %get-tuple-element.57), channel_id=1, source_target_pairs={{0,128},{128,0},{1,129},{129,1},{2,130},{130,2},{3,131},{131,3},{4... | collective-permute-start | bytes 423944 | tf_op jit(solution)/shard_map/ppermute | solution.py:484
  128.2 2.9 %copy-start.7 = (f32[2,2]{1,0:T(2,128)S(1)}, f32[2,2]{1,0:T(2,128)}, u32[]{:S(2)}) copy-start(f32[2,2]{1,0:T(2,128)} %mix.7) | copy-start | bytes 52
  130.2 5.6 %collective-permute-start.14 = (bf16[23,24,128]{2,1,0:T(8,128)(2,1)S(1)}, bf16[23,24,128]{2,1,0:T(8,128)(2,1)S(1)}, u32[]{:S(2)}, u32[]{:S(2)}) collective-permute-start(bf16[23,24,128]{2,1,0:T(8,128)(2,1)S(1)} %get-tuple-element.55), channel_id=1, source_target_pairs={{0,128},{128,0},{1,129},{129,1},{2,130},{130,2},{3,131},{131,3},{4... | collective-permute-start | bytes 423944 | tf_op jit(solution)/shard_map/ppermute | solution.py:484

commit v4 on v3

--- a/solution.py
+++ b/solution.py
@@ -38,9 +38,10 @@
     return jnp.where(low, swap(first), second)
 
 
-def z_pack_kernel(col, state, adv, *outs):
+def z_pack_kernel(distances, col, state, adv, *outs):
     me = col[0]
-    for r in range(8):
+    outs = dict(zip(distances, outs))
+    for r in distances:
         dest = lax.rem(me + r, 8)
         a = dest // 2
 
@@ -268,7 +269,7 @@
             put(t, c * grad[384:, lanes] - vel * grad[:384, lanes])
 
 
-CHUNKS = (((4, 5), (3, 4)), ((2, 3), (5, 6)), ((0, 1), (1, 2)), ((6, 7), (7, 0)))
+CHUNKS = (((0, 1), (7, 0)), ((4, 5), (3, 4)), ((2, 3), (1, 2)), ((6, 7), (5, 6)))
 
 
 def needs(n):
@@ -291,6 +292,11 @@
     def give(t, half0, half1):
         send[t] = jnp.where(first, half1, half0).astype(BF16)
         own[t] = jnp.where(first, half0, half1).astype(BF16)
+
+    def copy_of(yl):
+        return pltpu.make_async_copy(
+            rows.at[:, yl], out.at[:, 3 * group + yl], sem.at[yl]
+        )
 
     def fill(pair):
         def z_tile(b, t):
@@ -320,6 +326,7 @@
                 two = mids[2 * q : 2 * q + 2]
                 give(15 + 2 * yl + q, merge(0, *two), merge(1, *two))
             tails.append(mids[4])
+            copy_of(yl).start()
         tails.append(jnp.zeros((24, 128), F32))
         for q in range(2):
             two = tails[2 * q : 2 * q + 2]
@@ -331,9 +338,8 @@
         def _(odd_me=odd_me):
             fill(CHUNKS[n][odd_me])
 
-    copy = pltpu.make_async_copy(rows, out.at[:, pl.ds(3 * group, 3)], sem)
-    copy.start()
-    copy.wait()
+    for yl in range(3):
+        copy_of(yl).wait()
 
 
 def sketch_kernel(n, probe, col, mix, *refs):
@@ -342,6 +348,9 @@
     p = probe[0]
     low = low_lanes((24, 128))
     group = group_of(n, col[0])
+
+    def copy_of(g):
+        return pltpu.make_async_copy(rows.at[g], out.at[g, :, pl.ds(3 * group, 3)], sem.at[g])
 
     def mixed(t, g):
         a = (own[t].astype(F32) * mix[p, g]).astype(BF16).astype(F32)
@@ -365,9 +374,9 @@
         put(g, 4, 0, mixed(4, g), half)
         put(g, 4, 1, mixed(9, g), swap(half))
         put(g, 4, 2, mixed(14, g), mixed(22, g))
-    copy = pltpu.make_async_copy(rows, out.at[:, :, pl.ds(3 * group, 3)], sem)
-    copy.start()
-    copy.wait()
+        copy_of(g).start()
+    for g in range(2):
+        copy_of(g).wait()
 
 
 def call(kernel, out_shapes, scalars, arrays, scratch=(), kept=(), spaces=None, stay=False):
@@ -399,7 +408,7 @@
     return lax.ppermute(x, "col", [(i, (i + distance) % 8) for i in range(8)])
 
 
-ROUTES = (3, 5, 4, 2, 6, 1, 7)
+ROUTES = (1, 7, 3, 5, 4, 2, 6)
 
 
 def on_device(
@@ -440,10 +449,17 @@
     at_y = lax.all_to_all(
         to_y.reshape(16, 336, 128), "row", split_axis=0, concat_axis=0, tiled=True
     )
-    to_z = call(z_pack_kernel, [stored((648, 128))] + [held((648, 128))] * 7, [col], [state, advect_z])
-    at_z = list(to_z)
-    for r in ROUTES:
-        at_z[r] = shift(to_z[r], r)
+    at_z = {}
+    for distances in ((1, 7), (0, 3, 5, 4, 2, 6)):
+        to_z = call(
+            functools.partial(z_pack_kernel, distances),
+            [(held if r else stored)((648, 128)) for r in distances],
+            [col],
+            [state, advect_z],
+        )
+        for r, piece in zip(distances, to_z):
+            at_z[r] = shift(piece, r) if r else piece
+    at_z = [at_z[r] for r in range(8)]
     lines_y, lines_z = call(
         matrices_kernel,
         [stored((1152, 384)), stored((384, 192))],
@@ -454,7 +470,7 @@
     back_y = lax.all_to_all(term_y, "row", split_axis=0, concat_axis=0, tiled=True)
     term_z = call(
         z_kernel,
-        [stored((552, 128))] + [held((552, 128))] * 7,
+        [stored((552, 128))] * 8,
         [diffusivity],
         [far(at_z[0])] + [near(x) for x in at_z[1:]] + [far(lines_z)],
     )
@@ -465,7 +481,7 @@
         xy_kernel,
         held((5, 12, 24, 384), F32),
         [diffusivity],
-        [state, forced, advect_x, deriv_x, near(back_y.reshape(8, 2, 336, 128))],
+        [state, far(forced), far(advect_x), far(deriv_x), near(back_y.reshape(8, 2, 336, 128))],
         [pltpu.VMEM((24, 24, 384), F32)],
     )
     pieces = [far(back_z[0])] + [near(x) for x in back_z[1:]]
@@ -476,7 +492,7 @@
             [shape((5, 12, 24, 384)), held((23, 24, 128)), held((23, 24, 128))],
             [probe, col],
             [near(base)] + [pieces[r] for r in needs(n)],
-            [pltpu.VMEM((5, 3, 24, 384), BF16), pltpu.SemaphoreType.DMA],
+            [pltpu.VMEM((5, 3, 24, 384), BF16), pltpu.SemaphoreType.DMA((3,))],
             kept=sections[-1:],
             spaces=[any_space, vspec(), vspec()],
         )
@@ -490,7 +506,7 @@
                 [shape((2, 5, 12, 24, 192))],
                 [probe, col, test_mix],
                 [near(own), near(recv)],
-                [pltpu.VMEM((2, 5, 3, 24, 192), BF16), pltpu.SemaphoreType.DMA],
+                [pltpu.VMEM((2, 5, 3, 24, 192), BF16), pltpu.SemaphoreType.DMA((2,))],
                 kept=sketches[-1:],
                 spaces=[any_space],
             )[0]

time: 138 us -> 130 us (0.942)
  the two profiles are of different devices: /device:TPU:36 before, /device:TPU:1 now
where the time goes in v4:
time: 130 us; the launch traced here: 128 us
  waiting for transfers between devices  52.9 us (41%)
  starting transfers between devices  43.8 us (34%)
  Pallas kernels  29.9 us (23%)
    ppermute x14, waiting for transfers between devices, shift(): return lax.ppermute(x, 'col', [(i, (i + distance) % 8) for i in range(8)])  33.6 us
    pallas_call x15, Pallas kernels, call(): pl.pallas_call(kernel, out_shape=out_shapes, in_specs=[sspec()] * len(sca...  29.9 us
    ppermute x14, starting transfers between devices, shift(): return lax.ppermute(x, 'col', [(i, (i + distance) % 8) for i in range(8)])  27.5 us
    all_to_all x1, waiting for transfers between devices, on_device(): lax.all_to_all(to_y.reshape(16, 336, 128), 'row', split_axis=0, concat_ax...  17.5 us
    all_to_all x1, starting transfers between devices, on_device(): lax.all_to_all(to_y.reshape(16, 336, 128), 'row', split_axis=0, concat_ax...  8.45 us
    all_to_all x1, starting transfers between devices, on_device(): lax.all_to_all(term_y, 'row', split_axis=0, concat_axis=0, tiled=True)  4.65 us
    ppermute x4, starting transfers between devices, on_device(): halves.append((own, lax.ppermute(send, 'probe', [(0, 1), (1, 0)])))  3.19 us
  transfers between devices with their start and end apart: 20, of which 9 were waited for; matrix products, arithmetic and copies ran while one was open for 0% of the time, Pallas kernels for 17%

profile of v4, /device:TPU:1, one launch (start us, length us, event | category | flops | bytes accessed | tf_op | source)
XLA Modules:
  0.0 127.6 jit_solution(8809211974249857390)
XLA Ops:
  0.6 2.8 %shard_map.113 = bf16[8,2,336,128]{3,2,1,0:T(8,128)(2,1)} custom-call(bf16[5,12,24,384]{3,2,1,0:T(8,128)(2,1)} %bitcast.7, bf16[12,24,384]{2,1,0:T(8,128)(2,1)} %adv_far.1), custom_call_target="tpu_custom_call" | custom-call | tf_op jit(solution)/shard_map/pallas_call | solution.py:386
  3.4 0.0 copy-start.3
  3.4 8.4 %all-to-all-start = ((bf16[16,336,128]{2,1,0:T(8,128)(2,1)}), bf16[16,336,128]{2,1,0:T(8,128)(2,1)S(1)}, u32[]{:S(2)}, u32[]{:S(2)}) async-start(bf16[16,336,128]{2,1,0:T(8,128)(2,1)} %bitcast.4), calls=%async_computation | async-start | bytes 2752512 | tf_op jit(solution)/shard_map/all_to_all | solution.py:449
  11.9 3.1 %shard_map.114 = (bf16[1152,384]{1,0:T(8,128)(2,1)}, bf16[384,192]{1,0:T(8,128)(2,1)}) custom-call(s32[1]{0:T(128)} %bitcast.1.col, bf16[2,192,192]{2,1,0:T(8,128)(2,1)} %mat_y.1, bf16[2,192,192]{2,1,0:T(8,128)(2,1)} %mat_z.1), custom_call_target="tpu_custom_call" | custom-call | tf_op jit(solution)/shard_map/pallas_call | solution.py:386
  15.0 17.5 %all-to-all-done.recv = bf16[16,336,128]{2,1,0:T(8,128)(2,1)S(1)} async-done(((bf16[16,336,128]{2,1,0:T(8,128)(2,1)}), bf16[16,336,128]{2,1,0:T(8,128)(2,1)S(1)}, u32[]{:S(2)}, u32[]{:S(2)}) %all-to-all-start) | async-done | bytes 1376288 | tf_op jit(solution)/shard_map/all_to_all | solution.py:449
  32.5 4.2 %shard_map.115 = bf16[16,336,128]{2,1,0:T(8,128)(2,1)} custom-call(f32[5]{0:T(128)S(1)} %copy-done.3, bf16[16,336,128]{2,1,0:T(8,128)(2,1)S(1)} %all-to-all-done.recv, bf16[1152,384]{1,0:T(8,128)(2,1)} %get-tuple-element.32.lines), custom_call_target="tpu_custom_call" | custom-call | tf_op jit(solution)/shard_map/pallas_call | solution.py:386
  36.7 4.7 %all-to-all-start.1 = ((bf16[16,336,128]{2,1,0:T(8,128)(2,1)}), bf16[16,336,128]{2,1,0:T(8,128)(2,1)S(1)}, u32[]{:S(2)}, u32[]{:S(2)}) async-start(bf16[16,336,128]{2,1,0:T(8,128)(2,1)} %shard_map.115), calls=%async_computation.1 | async-start | bytes 2752512 | tf_op jit(solution)/shard_map/all_to_all | solution.py:470
  41.3 0.5 shard_map.118
  41.8 1.7 %collective-permute-start = (bf16[648,128]{1,0:T(8,128)(2,1)S(1)}, bf16[648,128]{1,0:T(8,128)(2,1)S(1)}, u32[]{:S(2)}, u32[]{:S(2)}) collective-permute-start(bf16[648,128]{1,0:T(8,128)(2,1)S(1)} %get-tuple-element.34), channel_id=1, source_target_pairs={{0,1},{1,2},{2,3},{3,4},{4,5},{5,6},{6,7},{7,0},{8,9},{9,10},{10,1... | collective-permute-start | bytes 497672 | tf_op jit(solution)/shard_map/ppermute | solution.py:408
  43.5 4.0 %collective-permute-start.6 = (bf16[648,128]{1,0:T(8,128)(2,1)S(1)}, bf16[648,128]{1,0:T(8,128)(2,1)S(1)}, u32[]{:S(2)}, u32[]{:S(2)}) collective-permute-start(bf16[648,128]{1,0:T(8,128)(2,1)S(1)} %get-tuple-element.40), channel_id=1, source_target_pairs={{0,7},{1,0},{2,1},{3,2},{4,3},{5,4},{6,5},{7,6},{8,15},{9,8},{10,9... | collective-permute-start | bytes 497672 | tf_op jit(solution)/shard_map/ppermute | solution.py:408
  47.6 2.1 %shard_map.117 = (bf16[648,128]{1,0:T(8,128)(2,1)}, bf16[648,128]{1,0:T(8,128)(2,1)S(1)}, bf16[648,128]{1,0:T(8,128)(2,1)S(1)}, bf16[648,128]{1,0:T(8,128)(2,1)S...) custom-call(s32[1]{0:T(128)} %bitcast.1.col, bf16[5,12,24,384]{3,2,1,0:T(8,128)(2,1)S(1)} %bitcast.9, ...), custom_call_target="tpu_custom_call" | custom-call | tf_op jit(solution)/shard_map/pallas_call | solution.py:386
  49.7 0.0 collective-permute-start.1
  49.7 3.4 %collective-permute-start.2 = (bf16[648,128]{1,0:T(8,128)(2,1)S(1)}, bf16[648,128]{1,0:T(8,128)(2,1)S(1)}, u32[]{:S(2)}, u32[]{:S(2)}) collective-permute-start(bf16[648,128]{1,0:T(8,128)(2,1)S(1)} %get-tuple-element.36), channel_id=1, source_target_pairs={{0,3},{1,4},{2,5},{3,6},{4,7},{5,0},{6,1},{7,2},{8,11},{9,12},{10,... | collective-permute-start | bytes 497672 | tf_op jit(solution)/shard_map/ppermute | solution.py:408
  53.1 0.9 collective-permute-start.3
  54.0 0.0 collective-permute-done.refs_1_
  54.0 4.0 %collective-permute-start.4 = (bf16[648,128]{1,0:T(8,128)(2,1)S(1)}, bf16[648,128]{1,0:T(8,128)(2,1)S(1)}, u32[]{:S(2)}, u32[]{:S(2)}) collective-permute-start(bf16[648,128]{1,0:T(8,128)(2,1)S(1)} %get-tuple-element.38), channel_id=1, source_target_pairs={{0,5},{1,6},{2,7},{3,0},{4,1},{5,2},{6,3},{7,4},{8,13},{9,14},{10,... | collective-permute-start | bytes 497672 | tf_op jit(solution)/shard_map/ppermute | solution.py:408
  58.1 3.6 %collective-permute-start.5 = (bf16[648,128]{1,0:T(8,128)(2,1)S(1)}, bf16[648,128]{1,0:T(8,128)(2,1)S(1)}, u32[]{:S(2)}, u32[]{:S(2)}) collective-permute-start(bf16[648,128]{1,0:T(8,128)(2,1)S(1)} %get-tuple-element.39), channel_id=1, source_target_pairs={{0,6},{1,7},{2,0},{3,1},{4,2},{5,3},{6,4},{7,5},{8,14},{9,15},{10,... | collective-permute-start | bytes 497672 | tf_op jit(solution)/shard_map/ppermute | solution.py:408
  61.6 13.6 %collective-permute-done.2.refs_3_ = bf16[648,128]{1,0:T(8,128)(2,1)S(1)} collective-permute-done((bf16[648,128]{1,0:T(8,128)(2,1)S(1)}, bf16[648,128]{1,0:T(8,128)(2,1)S(1)}, u32[]{:S(2)}, u32[]{:S(2)}) %collective-permute-start.2) | collective-permute-done | bytes 165920 | tf_op jit(solution)/shard_map/ppermute | solution.py:408
  75.2 0.0 collective-permute-done.3.refs_4_
  75.2 1.5 %collective-permute-done.4.refs_5_ = bf16[648,128]{1,0:T(8,128)(2,1)S(1)} collective-permute-done((bf16[648,128]{1,0:T(8,128)(2,1)S(1)}, bf16[648,128]{1,0:T(8,128)(2,1)S(1)}, u32[]{:S(2)}, u32[]{:S(2)}) %collective-permute-start.4) | collective-permute-done | bytes 165920 | tf_op jit(solution)/shard_map/ppermute | solution.py:408
  76.8 8.1 %collective-permute-done.5.refs_6_ = bf16[648,128]{1,0:T(8,128)(2,1)S(1)} collective-permute-done((bf16[648,128]{1,0:T(8,128)(2,1)S(1)}, bf16[648,128]{1,0:T(8,128)(2,1)S(1)}, u32[]{:S(2)}, u32[]{:S(2)}) %collective-permute-start.5) | collective-permute-done | bytes 165920 | tf_op jit(solution)/shard_map/ppermute | solution.py:408
  84.8 2.8 %shard_map.119 = (bf16[552,128]{1,0:T(8,128)(2,1)}, bf16[552,128]{1,0:T(8,128)(2,1)}, bf16[552,128]{1,0:T(8,128)(2,1)}, bf16[552,128]{1,0:T(8,128)(2,1)}, bf16[5...) custom-call(f32[5]{0:T(128)S(1)} %copy-done.3, ...), custom_call_target="tpu_custom_call" | custom-call | tf_op jit(solution)/shard_map/pallas_call | solution.py:386
  87.6 2.7 %collective-permute-start.10 = (bf16[552,128]{1,0:T(8,128)(2,1)}, bf16[552,128]{1,0:T(8,128)(2,1)S(1)}, u32[]{:S(2)}, u32[]{:S(2)}) collective-permute-start(bf16[552,128]{1,0:T(8,128)(2,1)} %get-tuple-element.45), channel_id=1, source_target_pairs={{0,7},{1,0},{2,1},{3,2},{4,3},{5,4},{6,5},{7,6},{8,15},{9,8},{10,9... | collective-permute-start | bytes 423944 | tf_op jit(solution)/shard_map/ppermute | solution.py:408
  90.3 0.0 collective-permute-start.7
  90.3 4.5 %collective-permute-start.12 = (bf16[552,128]{1,0:T(8,128)(2,1)}, bf16[552,128]{1,0:T(8,128)(2,1)S(1)}, u32[]{:S(2)}, u32[]{:S(2)}) collective-permute-start(bf16[552,128]{1,0:T(8,128)(2,1)} %get-tuple-element.47), channel_id=1, source_target_pairs={{0,5},{1,6},{2,7},{3,0},{4,1},{5,2},{6,3},{7,4},{8,13},{9,14},{10,... | collective-permute-start | bytes 423944 | tf_op jit(solution)/shard_map/ppermute | solution.py:408
  94.8 0.3 collective-permute-start.13
  95.1 0.0 collective-permute-done.9.refs_3_
  95.1 2.2 %collective-permute-start.11 = (bf16[552,128]{1,0:T(8,128)(2,1)}, bf16[552,128]{1,0:T(8,128)(2,1)S(1)}, u32[]{:S(2)}, u32[]{:S(2)}) collective-permute-start(bf16[552,128]{1,0:T(8,128)(2,1)} %get-tuple-element.46), channel_id=1, source_target_pairs={{0,6},{1,7},{2,0},{3,1},{4,2},{5,3},{6,4},{7,5},{8,14},{9,15},{10,... | collective-permute-start | bytes 423944 | tf_op jit(solution)/shard_map/ppermute | solution.py:408
  97.3 0.1 collective-permute-start.8
  97.5 0.0 all-to-all-done.1
  97.5 4.0 %shard_map.116.refs_0_ = f32[5,12,24,384]{3,2,1,0:T(8,128)S(1)} custom-call(f32[5]{0:T(128)S(1)} %copy-done.3, bf16[5,12,24,384]{3,2,1,0:T(8,128)(2,1)S(1)} %bitcast.10, bf16[5,12,24,384]{3,2,1,0:T(8,128)(2,1)} %bitcast.13, bf16[12,24,384]{2,1,0:T(8,128)(2,1)} %adv.3, bf16[2,384,384]{2,1,0:T(8,128)(2,1)} %mat.1, bf16[8,2,336,128]{3,2,1,0:T(8,128)(2,1)S(1)} %bitcast.11), custom_call_target="tpu_custom_call" | custom-call | tf_op jit(solution)/shard_map/pallas_call | solution.py:386
  101.5 1.8 %shard_map.120 = (bf16[5,12,24,384]{3,2,1,0:T(8,128)(2,1)}, bf16[23,24,128]{2,1,0:T(8,128)(2,1)S(1)}, bf16[23,24,128]{2,1,0:T(8,128)(2,1)S(1)}) custom-call(s32[1]{0:T(128)} %bitcast.probe, s32[1]{0:T(128)} %bitcast.1.col, f32[5,12,24,384]{3,2,1,0:T(8,128)S(1)} %shard_map.116.refs_0_, bf16[552,128]{1,0:T(8,128)(2,1)} %get-tuple-element.49.refs_1_, ...), custom_call_target="tpu_custom_call" | custom-call | tf_op jit(solution)/shard_map/pallas_call | solution.py:386
  103.3 1.6 %collective-permute-done.7.refs_3_.refs_1_ = bf16[552,128]{1,0:T(8,128)(2,1)S(1)} collective-permute-done((bf16[552,128]{1,0:T(8,128)(2,1)}, bf16[552,128]{1,0:T(8,128)(2,1)S(1)}, u32[]{:S(2)}, u32[]{:S(2)}) %collective-permute-start.7) | collective-permute-done | bytes 141344 | tf_op jit(solution)/shard_map/ppermute | solution.py:408
  104.9 2.8 %collective-permute-done.13.refs_2_ = bf16[552,128]{1,0:T(8,128)(2,1)S(1)} collective-permute-done((bf16[552,128]{1,0:T(8,128)(2,1)}, bf16[552,128]{1,0:T(8,128)(2,1)S(1)}, u32[]{:S(2)}, u32[]{:S(2)}) %collective-permute-start.13) | collective-permute-done | bytes 141344 | tf_op jit(solution)/shard_map/ppermute | solution.py:408
  107.6 0.9 shard_map.121
  108.5 0.4 collective-permute-start.16
  109.0 1.1 collective-permute-start.17
  110.1 6.1 %collective-permute-done.11.refs_2_ = bf16[552,128]{1,0:T(8,128)(2,1)S(1)} collective-permute-done((bf16[552,128]{1,0:T(8,128)(2,1)}, bf16[552,128]{1,0:T(8,128)(2,1)S(1)}, u32[]{:S(2)}, u32[]{:S(2)}) %collective-permute-start.11) | collective-permute-done | bytes 141344 | tf_op jit(solution)/shard_map/ppermute | solution.py:408
  116.1 0.9 shard_map.122
  117.0 0.4 collective-permute-start.15
  117.4 0.9 shard_map.123
  118.3 1.2 collective-permute-start.14
  119.6 1.5 %shard_map.124.refs_2_ = bf16[2,5,12,24,192]{4,3,2,1,0:T(8,128)(2,1)} custom-call(s32[1]{0:T(128)} %bitcast.probe, s32[1]{0:T(128)} %bitcast.1.col, f32[2,2]{1,0:T(2,128)S(1)} %copy-done.2, bf16[23,24,128]{2,1,0:T(8,128)(2,1)S(1)} %get-tuple-element.60.refs_0_, bf16[23,24,128]{2,1,0:T(8,128)(2,1)S(1)} %collective-permute-done.17.refs_1_), custom_call_target="tpu_custom_call" | custom-call | tf_op jit(solution)/shard_map/pallas_call | solution.py:386
  121.1 1.5 %shard_map.125.refs_2_ = bf16[2,5,12,24,192]{4,3,2,1,0:T(8,128)(2,1)} custom-call(s32[1]{0:T(128)} %bitcast.probe, s32[1]{0:T(128)} %bitcast.1.col, f32[2,2]{1,0:T(2,128)S(1)} %copy-done.2, bf16[23,24,128]{2,1,0:T(8,128)(2,1)S(1)} %get-tuple-element.58.refs_0_, ...), custom_call_target="tpu_custom_call", output_to_operand_aliasing={{}: (5, {})} | custom-call | tf_op jit(solution)/shard_map/pallas_call | solution.py:386
  122.6 0.2 collective-permute-done.15.refs_1_
  122.9 1.5 %shard_map.126.refs_2_ = bf16[2,5,12,24,192]{4,3,2,1,0:T(8,128)(2,1)} custom-call(s32[1]{0:T(128)} %bitcast.probe, s32[1]{0:T(128)} %bitcast.1.col, f32[2,2]{1,0:T(2,128)S(1)} %copy-done.2, bf16[23,24,128]{2,1,0:T(8,128)(2,1)S(1)} %get-tuple-element.56.refs_0_, ...), custom_call_target="tpu_custom_call", output_to_operand_aliasing={{}: (5, {})} | custom-call | tf_op jit(solution)/shard_map/pallas_call | solution.py:386
  124.4 1.5 %collective-permute-done.14.refs_1_ = bf16[23,24,128]{2,1,0:T(8,128)(2,1)S(1)} collective-permute-done((bf16[23,24,128]{2,1,0:T(8,128)(2,1)S(1)}, bf16[23,24,128]{2,1,0:T(8,128)(2,1)S(1)}, u32[]{:S(2)}, u32[]{:S(2)}) %collective-permute-start.14) | collective-permute-done | bytes 141344 | tf_op jit(solution)/shard_map/ppermute | solution.py:500
  125.9 1.5 %shard_map.127 = bf16[2,5,12,24,192]{4,3,2,1,0:T(8,128)(2,1)} custom-call(s32[1]{0:T(128)} %bitcast.probe, s32[1]{0:T(128)} %bitcast.1.col, f32[2,2]{1,0:T(2,128)S(1)} %copy-done.2, bf16[23,24,128]{2,1,0:T(8,128)(2,1)S(1)} %get-tuple-element.54.refs_0_, bf16[23,24,128]{2,1,0:T(8,128)(2,1)S(1)} %collective-permute-done.14.refs_1_, ...), custom_call_target="tpu_custom_call", output_to_operand_aliasing={{}: (5, {})} | custom-call | tf_op jit(solution)/shard_map/pallas_call | solution.py:386
  (15 shorter events, 0.0 us)
Async XLA Ops:
  3.4 29.1 %copy-start.3 = (f32[5]{0:T(128)S(1)}, f32[5]{0:T(128)}, u32[]{:S(2)}) copy-start(f32[5]{0:T(128)} %coef.5) | copy-start | bytes 64
  3.4 29.1 %all-to-all-start = ((bf16[16,336,128]{2,1,0:T(8,128)(2,1)}), bf16[16,336,128]{2,1,0:T(8,128)(2,1)S(1)}, u32[]{:S(2)}, u32[]{:S(2)}) async-start(bf16[16,336,128]{2,1,0:T(8,128)(2,1)} %bitcast.4), calls=%async_computation | async-start | bytes 2752512 | tf_op jit(solution)/shard_map/all_to_all | solution.py:449
  36.7 4.7 %copy-start = (bf16[1,5,12,24,384]{4,3,2,1,0:T(8,128)(2,1)S(1)}, bf16[1,5,12,24,384]{4,3,2,1,0:T(8,128)(2,1)}, u32[]{:S(2)}) copy-start(bf16[1,5,12,24,384]{4,3,2,1,0:T(8,128)(2,1)} %param.10) | copy-start | bytes 3317764
  36.7 4.7 %copy-start.1 = (bf16[12,24,384]{2,1,0:T(8,128)(2,1)S(1)}, bf16[12,24,384]{2,1,0:T(8,128)(2,1)}, u32[]{:S(2)}) copy-start(bf16[12,24,384]{2,1,0:T(8,128)(2,1)} %adv.5) | copy-start | bytes 663556
  36.7 60.8 %all-to-all-start.1 = ((bf16[16,336,128]{2,1,0:T(8,128)(2,1)}), bf16[16,336,128]{2,1,0:T(8,128)(2,1)S(1)}, u32[]{:S(2)}, u32[]{:S(2)}) async-start(bf16[16,336,128]{2,1,0:T(8,128)(2,1)} %shard_map.115), calls=%async_computation.1 | async-start | bytes 2752512 | tf_op jit(solution)/shard_map/all_to_all | solution.py:470
  41.8 12.2 %collective-permute-start = (bf16[648,128]{1,0:T(8,128)(2,1)S(1)}, bf16[648,128]{1,0:T(8,128)(2,1)S(1)}, u32[]{:S(2)}, u32[]{:S(2)}) collective-permute-start(bf16[648,128]{1,0:T(8,128)(2,1)S(1)} %get-tuple-element.34), channel_id=1, source_target_pairs={{0,1},{1,2},{2,3},{3,4},{4,5},{5,6},{6,7},{7,0},{8,9},{9,10},{10,1... | collective-permute-start | bytes 497672 | tf_op jit(solution)/shard_map/ppermute | solution.py:408
  43.5 14.5 %collective-permute-start.6 = (bf16[648,128]{1,0:T(8,128)(2,1)S(1)}, bf16[648,128]{1,0:T(8,128)(2,1)S(1)}, u32[]{:S(2)}, u32[]{:S(2)}) collective-permute-start(bf16[648,128]{1,0:T(8,128)(2,1)S(1)} %get-tuple-element.40), channel_id=1, source_target_pairs={{0,7},{1,0},{2,1},{3,2},{4,3},{5,4},{6,5},{7,6},{8,15},{9,8},{10,9... | collective-permute-start | bytes 497672 | tf_op jit(solution)/shard_map/ppermute | solution.py:408
  49.7 11.9 %collective-permute-start.1 = (bf16[648,128]{1,0:T(8,128)(2,1)S(1)}, bf16[648,128]{1,0:T(8,128)(2,1)S(1)}, u32[]{:S(2)}, u32[]{:S(2)}) collective-permute-start(bf16[648,128]{1,0:T(8,128)(2,1)S(1)} %get-tuple-element.35), channel_id=1, source_target_pairs={{0,2},{1,3},{2,4},{3,5},{4,6},{5,7},{6,0},{7,1},{8,10},{9,11},{10,... | collective-permute-start | bytes 497672 | tf_op jit(solution)/shard_map/ppermute | solution.py:408
  49.7 25.5 %collective-permute-start.2 = (bf16[648,128]{1,0:T(8,128)(2,1)S(1)}, bf16[648,128]{1,0:T(8,128)(2,1)S(1)}, u32[]{:S(2)}, u32[]{:S(2)}) collective-permute-start(bf16[648,128]{1,0:T(8,128)(2,1)S(1)} %get-tuple-element.36), channel_id=1, source_target_pairs={{0,3},{1,4},{2,5},{3,6},{4,7},{5,0},{6,1},{7,2},{8,11},{9,12},{10,... | collective-permute-start | bytes 497672 | tf_op jit(solution)/shard_map/ppermute | solution.py:408
  53.1 22.1 %collective-permute-start.3 = (bf16[648,128]{1,0:T(8,128)(2,1)S(1)}, bf16[648,128]{1,0:T(8,128)(2,1)S(1)}, u32[]{:S(2)}, u32[]{:S(2)}) collective-permute-start(bf16[648,128]{1,0:T(8,128)(2,1)S(1)} %get-tuple-element.37), channel_id=1, source_target_pairs={{0,4},{1,5},{2,6},{3,7},{4,0},{5,1},{6,2},{7,3},{8,12},{9,13},{10,... | collective-permute-start | bytes 497672 | tf_op jit(solution)/shard_map/ppermute | solution.py:408
  54.0 22.7 %collective-permute-start.4 = (bf16[648,128]{1,0:T(8,128)(2,1)S(1)}, bf16[648,128]{1,0:T(8,128)(2,1)S(1)}, u32[]{:S(2)}, u32[]{:S(2)}) collective-permute-start(bf16[648,128]{1,0:T(8,128)(2,1)S(1)} %get-tuple-element.38), channel_id=1, source_target_pairs={{0,5},{1,6},{2,7},{3,0},{4,1},{5,2},{6,3},{7,4},{8,13},{9,14},{10,... | collective-permute-start | bytes 497672 | tf_op jit(solution)/shard_map/ppermute | solution.py:408
  58.1 26.8 %collective-permute-start.5 = (bf16[648,128]{1,0:T(8,128)(2,1)S(1)}, bf16[648,128]{1,0:T(8,128)(2,1)S(1)}, u32[]{:S(2)}, u32[]{:S(2)}) collective-permute-start(bf16[648,128]{1,0:T(8,128)(2,1)S(1)} %get-tuple-element.39), channel_id=1, source_target_pairs={{0,6},{1,7},{2,0},{3,1},{4,2},{5,3},{6,4},{7,5},{8,14},{9,15},{10,... | collective-permute-start | bytes 497672 | tf_op jit(solution)/shard_map/ppermute | solution.py:408
  87.6 7.5 %collective-permute-start.9 = (bf16[552,128]{1,0:T(8,128)(2,1)}, bf16[552,128]{1,0:T(8,128)(2,1)S(1)}, u32[]{:S(2)}, u32[]{:S(2)}) collective-permute-start(bf16[552,128]{1,0:T(8,128)(2,1)} %get-tuple-element.44), channel_id=1, source_target_pairs={{0,1},{1,2},{2,3},{3,4},{4,5},{5,6},{6,7},{7,0},{8,9},{9,10},{10,1... | collective-permute-start | bytes 423944 | tf_op jit(solution)/shard_map/ppermute | solution.py:408
  87.6 9.7 %collective-permute-start.10 = (bf16[552,128]{1,0:T(8,128)(2,1)}, bf16[552,128]{1,0:T(8,128)(2,1)S(1)}, u32[]{:S(2)}, u32[]{:S(2)}) collective-permute-start(bf16[552,128]{1,0:T(8,128)(2,1)} %get-tuple-element.45), channel_id=1, source_target_pairs={{0,7},{1,0},{2,1},{3,2},{4,3},{5,4},{6,5},{7,6},{8,15},{9,8},{10,9... | collective-permute-start | bytes 423944 | tf_op jit(solution)/shard_map/ppermute | solution.py:408
  90.3 14.5 %collective-permute-start.7 = (bf16[552,128]{1,0:T(8,128)(2,1)}, bf16[552,128]{1,0:T(8,128)(2,1)S(1)}, u32[]{:S(2)}, u32[]{:S(2)}) collective-permute-start(bf16[552,128]{1,0:T(8,128)(2,1)} %get-tuple-element.42), channel_id=1, source_target_pairs={{0,3},{1,4},{2,5},{3,6},{4,7},{5,0},{6,1},{7,2},{8,11},{9,12},{10,... | collective-permute-start | bytes 423944 | tf_op jit(solution)/shard_map/ppermute | solution.py:408
  90.3 14.5 %collective-permute-start.12 = (bf16[552,128]{1,0:T(8,128)(2,1)}, bf16[552,128]{1,0:T(8,128)(2,1)S(1)}, u32[]{:S(2)}, u32[]{:S(2)}) collective-permute-start(bf16[552,128]{1,0:T(8,128)(2,1)} %get-tuple-element.47), channel_id=1, source_target_pairs={{0,5},{1,6},{2,7},{3,0},{4,1},{5,2},{6,3},{7,4},{8,13},{9,14},{10,... | collective-permute-start | bytes 423944 | tf_op jit(solution)/shard_map/ppermute | solution.py:408
  94.8 12.9 %collective-permute-start.13 = (bf16[552,128]{1,0:T(8,128)(2,1)}, bf16[552,128]{1,0:T(8,128)(2,1)S(1)}, u32[]{:S(2)}, u32[]{:S(2)}) collective-permute-start(bf16[552,128]{1,0:T(8,128)(2,1)} %get-tuple-element.48), channel_id=1, source_target_pairs={{0,4},{1,5},{2,6},{3,7},{4,0},{5,1},{6,2},{7,3},{8,12},{9,13},{10,... | collective-permute-start | bytes 423944 | tf_op jit(solution)/shard_map/ppermute | solution.py:408
  95.1 21.1 %collective-permute-start.11 = (bf16[552,128]{1,0:T(8,128)(2,1)}, bf16[552,128]{1,0:T(8,128)(2,1)S(1)}, u32[]{:S(2)}, u32[]{:S(2)}) collective-permute-start(bf16[552,128]{1,0:T(8,128)(2,1)} %get-tuple-element.46), channel_id=1, source_target_pairs={{0,6},{1,7},{2,0},{3,1},{4,2},{5,3},{6,4},{7,5},{8,14},{9,15},{10,... | collective-permute-start | bytes 423944 | tf_op jit(solution)/shard_map/ppermute | solution.py:408
  97.3 20.1 %collective-permute-start.8 = (bf16[552,128]{1,0:T(8,128)(2,1)}, bf16[552,128]{1,0:T(8,128)(2,1)S(1)}, u32[]{:S(2)}, u32[]{:S(2)}) collective-permute-start(bf16[552,128]{1,0:T(8,128)(2,1)} %get-tuple-element.43), channel_id=1, source_target_pairs={{0,2},{1,3},{2,4},{3,5},{4,6},{5,7},{6,0},{7,1},{8,10},{9,11},{10,... | collective-permute-start | bytes 423944 | tf_op jit(solution)/shard_map/ppermute | solution.py:408
  108.5 12.6 %collective-permute-start.16 = (bf16[23,24,128]{2,1,0:T(8,128)(2,1)S(1)}, bf16[23,24,128]{2,1,0:T(8,128)(2,1)S(1)}, u32[]{:S(2)}, u32[]{:S(2)}) collective-permute-start(bf16[23,24,128]{2,1,0:T(8,128)(2,1)S(1)} %get-tuple-element.59), channel_id=1, source_target_pairs={{0,128},{128,0},{1,129},{129,1},{2,130},{130,2},{3,131},{131,3},{4... | collective-permute-start | bytes 423944 | tf_op jit(solution)/shard_map/ppermute | solution.py:500
  109.0 10.6 %collective-permute-start.17 = (bf16[23,24,128]{2,1,0:T(8,128)(2,1)S(1)}, bf16[23,24,128]{2,1,0:T(8,128)(2,1)S(1)}, u32[]{:S(2)}, u32[]{:S(2)}) collective-permute-start(bf16[23,24,128]{2,1,0:T(8,128)(2,1)S(1)} %get-tuple-element.61), channel_id=1, source_target_pairs={{0,128},{128,0},{1,129},{129,1},{2,130},{130,2},{3,131},{131,3},{4... | collective-permute-start | bytes 423944 | tf_op jit(solution)/shard_map/ppermute | solution.py:500
  117.0 5.8 %collective-permute-start.15 = (bf16[23,24,128]{2,1,0:T(8,128)(2,1)S(1)}, bf16[23,24,128]{2,1,0:T(8,128)(2,1)S(1)}, u32[]{:S(2)}, u32[]{:S(2)}) collective-permute-start(bf16[23,24,128]{2,1,0:T(8,128)(2,1)S(1)} %get-tuple-element.57), channel_id=1, source_target_pairs={{0,128},{128,0},{1,129},{129,1},{2,130},{130,2},{3,131},{131,3},{4... | collective-permute-start | bytes 423944 | tf_op jit(solution)/shard_map/ppermute | solution.py:500
  117.4 2.1 %copy-start.2 = (f32[2,2]{1,0:T(2,128)S(1)}, f32[2,2]{1,0:T(2,128)}, u32[]{:S(2)}) copy-start(f32[2,2]{1,0:T(2,128)} %mix.7) | copy-start | bytes 52
  118.3 7.6 %collective-permute-start.14 = (bf16[23,24,128]{2,1,0:T(8,128)(2,1)S(1)}, bf16[23,24,128]{2,1,0:T(8,128)(2,1)S(1)}, u32[]{:S(2)}, u32[]{:S(2)}) collective-permute-start(bf16[23,24,128]{2,1,0:T(8,128)(2,1)S(1)} %get-tuple-element.55), channel_id=1, source_target_pairs={{0,128},{128,0},{1,129},{129,1},{2,130},{130,2},{3,131},{131,3},{4... | collective-permute-start | bytes 423944 | tf_op jit(solution)/shard_map/ppermute | solution.py:500

commit v5 on v4

--- a/solution.py
+++ b/solution.py
@@ -38,26 +38,27 @@
     return jnp.where(low, swap(first), second)
 
 
-def z_pack_kernel(distances, col, state, adv, *outs):
+def z_pack_kernel(distances, col, state, adv, *refs):
     me = col[0]
-    outs = dict(zip(distances, outs))
-    for r in distances:
+    held, sem = refs[-2:]
+    copies = []
+    for n, r in enumerate(distances):
         dest = lax.rem(me + r, 8)
         a = dest // 2
 
-        def fill(b, r=r, a=a):
+        def fill(b, n=n, a=a):
             def body(yl, carry):
                 y = 3 * a + yl
                 base = pl.multiple_of(yl * 216, 8)
                 full = slice(256 * b, 256 * b + 128)
                 for u in range(6):
                     src = state[u, y, :, full] if u < 5 else adv[y, :, full]
-                    outs[r][pl.ds(base + 24 * u, 24), :] = src
+                    held[n, pl.ds(base + 24 * u, 24), :] = src
                 mid = [state[u, y, :, 128:256].astype(F32) for u in range(5)]
                 mid.append(adv[y, :, 128:256].astype(F32))
                 for q in range(3):
                     tile = merge(b, mid[2 * q], mid[2 * q + 1])
-                    outs[r][pl.ds(base + 144 + 24 * q, 24), :] = tile.astype(BF16)
+                    held[n, pl.ds(base + 144 + 24 * q, 24), :] = tile.astype(BF16)
                 return carry
 
             lax.fori_loop(0, 3, body, 0)
@@ -70,8 +71,13 @@
         def _():
             fill(1)
 
-
-def y_pack_kernel(state_far, adv_far, out, state, adv, sem):
+        copies.append(pltpu.make_async_copy(held.at[n], refs[n], sem.at[n]))
+        copies[-1].start()
+    for copy in copies:
+        copy.wait()
+
+
+def y_pack_kernel(state_far, adv_far, out_far, state, adv, out, sem):
     copies = [
         pltpu.make_async_copy(state_far.at[0:2], state.at[0:2], sem.at[0]),
         pltpu.make_async_copy(state_far.at[2:4], state.at[2:4], sem.at[1]),
@@ -80,6 +86,13 @@
     ]
     for copy in copies:
         copy.start()
+    leaving = []
+
+    def ship(n, first, last):
+        rows = slice(first, last)
+        copy = pltpu.make_async_copy(out.at[:, :, rows], out_far.at[:, :, rows], sem.at[4 + n])
+        copy.start()
+        leaving.append(copy)
 
     def lines(p, c):
         lanes = slice(128 * c, 128 * c + 128)
@@ -94,6 +107,7 @@
             copy.wait()
         for b in range(2):
             out[:, b, 72 * p : 72 * p + 72, :] = lines(p, 2 * b).reshape(8, 72, 128).astype(BF16)
+        ship(p, 72 * p, 72 * p + 72)
     mid = [lines(p, 1) for p in range(2)]
     for b in range(2):
         tile = merge(b, mid[0], mid[1])
@@ -103,6 +117,9 @@
     for b in range(2):
         out[:, b, 288:312, :] = merge(b, last[:, 0], last[:, 1]).astype(BF16)
         out[:, b, 312:336, :] = merge(b, last[:, 2], none).astype(BF16)
+    ship(3, 216, 336)
+    for copy in leaving:
+        copy.wait()
 
 
 def xy_kernel(coef, state, forcing, adv, mat, back_y, out, work):
@@ -187,7 +204,7 @@
 
 
 def z_kernel(coef, *refs):
-    recv, lines, outs = refs[:8], refs[8], refs[9:]
+    recv, lines, outs, held, sem = refs[:8], refs[8], refs[9:17], refs[17], refs[18]
     low = low_lanes((192, 128))
     lhs = lines[...]
 
@@ -197,7 +214,15 @@
 
     def put(t, term):
         for r in range(8):
-            outs[r][24 * t : 24 * t + 24, :] = term[24 * r : 24 * r + 24].astype(BF16)
+            held[r, 24 * t : 24 * t + 24, :] = term[24 * r : 24 * r + 24].astype(BF16)
+
+    copies = []
+
+    def ship(n, rows):
+        for r in range(8):
+            copy = pltpu.make_async_copy(held.at[r, rows], outs[r].at[rows], sem.at[n, r])
+            copy.start()
+            copies.append(copy)
 
     tails = []
     for yl in range(3):
@@ -220,8 +245,12 @@
                     put(yl * 7 + 5 + q, c * g1 - vel_half * g0)
                 else:
                     tails.append(coef[4] * g1 - vel_half * g0)
+        ship(yl, slice(168 * yl, 168 * yl + 168))
     put(21, jnp.where(low, tails[0], swap(tails[1])))
     put(22, jnp.where(low, tails[2], 0.0))
+    ship(3, slice(504, 552))
+    for copy in copies:
+        copy.wait()
 
 
 def y_kernel(coef, recv, lines, out):
@@ -269,7 +298,7 @@
             put(t, c * grad[384:, lanes] - vel * grad[:384, lanes])
 
 
-CHUNKS = (((0, 1), (7, 0)), ((4, 5), (3, 4)), ((2, 3), (1, 2)), ((6, 7), (5, 6)))
+CHUNKS = (((6, 7), (7, 0)), ((2, 3), (5, 6)), ((4, 5), (3, 4)), ((0, 1), (1, 2)))
 
 
 def needs(n):
@@ -408,7 +437,9 @@
     return lax.ppermute(x, "col", [(i, (i + distance) % 8) for i in range(8)])
 
 
-ROUTES = (1, 7, 3, 5, 4, 2, 6)
+ROUTES = (3, 5, 4, 2, 6, 1, 7)
+RETURNS = (7, 3, 6, 2, 5, 4, 1)
+FIRST = 2
 
 
 def on_device(
@@ -438,24 +469,32 @@
         return pltpu.HBM(s, t)
 
     any_space = pl.BlockSpec(memory_space=pl.ANY)
-    to_y = call(y_pack_kernel, held((8, 2, 336, 128)), [], [far(state), far(advect_y)],
+    to_y = call(
+        y_pack_kernel, [stored((8, 2, 336, 128))], [], [far(state), far(advect_y)],
         [
             pltpu.VMEM((5, 12, 24, 384), BF16),
             pltpu.VMEM((12, 24, 384), BF16),
-            pltpu.SemaphoreType.DMA((4,)),
+            pltpu.VMEM((8, 2, 336, 128), BF16),
+            pltpu.SemaphoreType.DMA((8,)),
         ],
         stay=True,
-    )
+        spaces=[any_space],
+    )[0]
     at_y = lax.all_to_all(
         to_y.reshape(16, 336, 128), "row", split_axis=0, concat_axis=0, tiled=True
     )
     at_z = {}
-    for distances in ((1, 7), (0, 3, 5, 4, 2, 6)):
+    for distances in (ROUTES[:FIRST], (0,) + ROUTES[FIRST:]):
         to_z = call(
             functools.partial(z_pack_kernel, distances),
-            [(held if r else stored)((648, 128)) for r in distances],
+            [stored((648, 128)) for _ in distances],
             [col],
             [state, advect_z],
+            [
+                pltpu.VMEM((len(distances), 648, 128), BF16),
+                pltpu.SemaphoreType.DMA((len(distances),)),
+            ],
+            spaces=[any_space] * len(distances),
         )
         for r, piece in zip(distances, to_z):
             at_z[r] = shift(piece, r) if r else piece
@@ -472,10 +511,12 @@
         z_kernel,
         [stored((552, 128))] * 8,
         [diffusivity],
-        [far(at_z[0])] + [near(x) for x in at_z[1:]] + [far(lines_z)],
+        [near(x) for x in at_z] + [near(lines_z)],
+        [pltpu.VMEM((8, 552, 128), BF16), pltpu.SemaphoreType.DMA((4, 8))],
+        spaces=[any_space] * 8,
     )
     back_z = list(term_z)
-    for r in ROUTES:
+    for r in RETURNS:
         back_z[r] = shift(term_z[r], -r)
     base = call(
         xy_kernel,
@@ -484,7 +525,7 @@
         [state, far(forced), far(advect_x), far(deriv_x), near(back_y.reshape(8, 2, 336, 128))],
         [pltpu.VMEM((24, 24, 384), F32)],
     )
-    pieces = [far(back_z[0])] + [near(x) for x in back_z[1:]]
+    pieces = [near(x) for x in back_z]
     sections, sketches, halves = [], [], []
     for n in range(4):
         section, send, own = call(

time: 130 us -> 127 us (0.977)
  waiting for transfers between devices: 52.9 us -> 43.7 us
  starting transfers between devices: 43.8 us -> 50.2 us
    ppermute x14, waiting for transfers between devices: 33.6 us -> 22.5 us  [shift(): return lax.ppermute(x, 'col', [(i, (i + distance) % 8) for i in range(8)])]
    ppermute x14, starting transfers between devices: 27.5 us -> 33.9 us  [shift(): return lax.ppermute(x, 'col', [(i, (i + distance) % 8) for i in range(8)])]
    ppermute x4, waiting for transfers between devices: 1.75 us -> 3.66 us  [on_device(): halves.append((own, lax.ppermute(send, 'probe', [(0, 1), (1, 0)])))]
  transfers between devices with their start and end apart: 20 -> 20, of which waited for: 9 -> 10; matrix products, arithmetic and copies ran while one was open for 0% -> 0% of each run, Pallas kernels for 17% -> 17%
where the time goes in v5:
time: 127 us; the launch traced here: 125 us
  starting transfers between devices  50.2 us (40%)
  waiting for transfers between devices  43.7 us (34%)
  Pallas kernels  29.1 us (23%)
    ppermute x14, starting transfers between devices, shift(): return lax.ppermute(x, 'col', [(i, (i + distance) % 8) for i in range(8)])  33.9 us
    pallas_call x15, Pallas kernels, call(): pl.pallas_call(kernel, out_shape=out_shapes, in_specs=[sspec()] * len(sca...  29.1 us
    ppermute x14, waiting for transfers between devices, shift(): return lax.ppermute(x, 'col', [(i, (i + distance) % 8) for i in range(8)])  22.5 us
    all_to_all x1, waiting for transfers between devices, on_device(): lax.all_to_all(to_y.reshape(16, 336, 128), 'row', split_axis=0, concat_ax...  17.5 us
    all_to_all x1, starting transfers between devices, on_device(): lax.all_to_all(to_y.reshape(16, 336, 128), 'row', split_axis=0, concat_ax...  8.45 us
    all_to_all x1, starting transfers between devices, on_device(): lax.all_to_all(term_y, 'row', split_axis=0, concat_axis=0, tiled=True)  4.65 us
    ppermute x4, waiting for transfers between devices, on_device(): halves.append((own, lax.ppermute(send, 'probe', [(0, 1), (1, 0)])))  3.66 us
    ppermute x4, starting transfers between devices, on_device(): halves.append((own, lax.ppermute(send, 'probe', [(0, 1), (1, 0)])))  3.19 us
  transfers between devices with their start and end apart: 20, of which 10 were waited for; matrix products, arithmetic and copies ran while one was open for 0% of the time, Pallas kernels for 17%

profile of v5, /device:TPU:1, one launch (start us, length us, event | category | flops | bytes accessed | tf_op | source)
XLA Modules:
  0.0 125.0 jit_solution(11356671534576326525)
XLA Ops:
  0.6 2.6 %shard_map.113 = bf16[8,2,336,128]{3,2,1,0:T(8,128)(2,1)} custom-call(bf16[5,12,24,384]{3,2,1,0:T(8,128)(2,1)} %bitcast.7, bf16[12,24,384]{2,1,0:T(8,128)(2,1)} %adv_far.1), custom_call_target="tpu_custom_call" | custom-call | tf_op jit(solution)/shard_map/pallas_call | solution.py:415
  3.2 0.0 copy-start.6
  3.2 8.4 %all-to-all-start = ((bf16[16,336,128]{2,1,0:T(8,128)(2,1)}), bf16[16,336,128]{2,1,0:T(8,128)(2,1)S(1)}, u32[]{:S(2)}, u32[]{:S(2)}) async-start(bf16[16,336,128]{2,1,0:T(8,128)(2,1)} %bitcast.13), calls=%async_computation | async-start | bytes 2752512 | tf_op jit(solution)/shard_map/all_to_all | solution.py:483
  11.6 3.1 %shard_map.114 = (bf16[1152,384]{1,0:T(8,128)(2,1)}, bf16[384,192]{1,0:T(8,128)(2,1)}) custom-call(s32[1]{0:T(128)} %bitcast.1.col, bf16[2,192,192]{2,1,0:T(8,128)(2,1)} %mat_y.1, bf16[2,192,192]{2,1,0:T(8,128)(2,1)} %mat_z.1), custom_call_target="tpu_custom_call" | custom-call | tf_op jit(solution)/shard_map/pallas_call | solution.py:415
  14.7 17.5 %all-to-all-done.recv = bf16[16,336,128]{2,1,0:T(8,128)(2,1)S(1)} async-done(((bf16[16,336,128]{2,1,0:T(8,128)(2,1)}), bf16[16,336,128]{2,1,0:T(8,128)(2,1)S(1)}, u32[]{:S(2)}, u32[]{:S(2)}) %all-to-all-start) | async-done | bytes 1376288 | tf_op jit(solution)/shard_map/all_to_all | solution.py:483
  32.3 4.2 %shard_map.115 = bf16[16,336,128]{2,1,0:T(8,128)(2,1)} custom-call(f32[5]{0:T(128)S(1)} %copy-done.6, bf16[16,336,128]{2,1,0:T(8,128)(2,1)S(1)} %all-to-all-done.recv, bf16[1152,384]{1,0:T(8,128)(2,1)} %get-tuple-element.32.lines), custom_call_target="tpu_custom_call" | custom-call | tf_op jit(solution)/shard_map/pallas_call | solution.py:415
  36.4 4.6 %all-to-all-start.1 = ((bf16[16,336,128]{2,1,0:T(8,128)(2,1)}), bf16[16,336,128]{2,1,0:T(8,128)(2,1)S(1)}, u32[]{:S(2)}, u32[]{:S(2)}) async-start(bf16[16,336,128]{2,1,0:T(8,128)(2,1)} %shard_map.115), calls=%async_computation.1 | async-start | bytes 2752512 | tf_op jit(solution)/shard_map/all_to_all | solution.py:509
  41.1 1.2 shard_map.118
  42.3 4.4 %collective-permute-start.2 = (bf16[648,128]{1,0:T(8,128)(2,1)}, bf16[648,128]{1,0:T(8,128)(2,1)S(1)}, u32[]{:S(2)}, u32[]{:S(2)}) collective-permute-start(bf16[648,128]{1,0:T(8,128)(2,1)} %get-tuple-element.36), channel_id=1, source_target_pairs={{0,3},{1,4},{2,5},{3,6},{4,7},{5,0},{6,1},{7,2},{8,11},{9,12},{10,... | collective-permute-start | bytes 497672 | tf_op jit(solution)/shard_map/ppermute | solution.py:437
  46.7 2.2 %collective-permute-start.4 = (bf16[648,128]{1,0:T(8,128)(2,1)}, bf16[648,128]{1,0:T(8,128)(2,1)S(1)}, u32[]{:S(2)}, u32[]{:S(2)}) collective-permute-start(bf16[648,128]{1,0:T(8,128)(2,1)} %get-tuple-element.38), channel_id=1, source_target_pairs={{0,5},{1,6},{2,7},{3,0},{4,1},{5,2},{6,3},{7,4},{8,13},{9,14},{10,... | collective-permute-start | bytes 497672 | tf_op jit(solution)/shard_map/ppermute | solution.py:437
  48.9 2.2 %shard_map.117 = (bf16[648,128]{1,0:T(8,128)(2,1)}, bf16[648,128]{1,0:T(8,128)(2,1)}, bf16[648,128]{1,0:T(8,128)(2,1)}, bf16[648,128]{1,0:T(8,128)(2,1)}, bf16[6...) custom-call(s32[1]{0:T(128)} %bitcast.1.col, bf16[5,12,24,384]{3,2,1,0:T(8,128)(2,1)S(1)} %bitcast.9, ...), custom_call_target="tpu_custom_call" | custom-call | tf_op jit(solution)/shard_map/pallas_call | solution.py:415
  51.1 0.8 collective-permute-start
  51.9 1.1 collective-permute-start.1
  53.0 4.3 %collective-permute-start.3 = (bf16[648,128]{1,0:T(8,128)(2,1)}, bf16[648,128]{1,0:T(8,128)(2,1)S(1)}, u32[]{:S(2)}, u32[]{:S(2)}) collective-permute-start(bf16[648,128]{1,0:T(8,128)(2,1)} %get-tuple-element.37), channel_id=1, source_target_pairs={{0,4},{1,5},{2,6},{3,7},{4,0},{5,1},{6,2},{7,3},{8,12},{9,13},{10,... | collective-permute-start | bytes 497672 | tf_op jit(solution)/shard_map/ppermute | solution.py:437
  57.3 1.2 collective-permute-done.2.refs_3_
  58.5 5.1 %collective-permute-start.5 = (bf16[648,128]{1,0:T(8,128)(2,1)}, bf16[648,128]{1,0:T(8,128)(2,1)S(1)}, u32[]{:S(2)}, u32[]{:S(2)}) collective-permute-start(bf16[648,128]{1,0:T(8,128)(2,1)} %get-tuple-element.39), channel_id=1, source_target_pairs={{0,6},{1,7},{2,0},{3,1},{4,2},{5,3},{6,4},{7,5},{8,14},{9,15},{10,... | collective-permute-start | bytes 497672 | tf_op jit(solution)/shard_map/ppermute | solution.py:437
  63.6 0.0 collective-permute-start.6
  63.6 0.0 collective-permute-done.refs_1_
  63.6 6.0 %collective-permute-done.1.refs_2_ = bf16[648,128]{1,0:T(8,128)(2,1)S(1)} collective-permute-done((bf16[648,128]{1,0:T(8,128)(2,1)}, bf16[648,128]{1,0:T(8,128)(2,1)S(1)}, u32[]{:S(2)}, u32[]{:S(2)}) %collective-permute-start.1) | collective-permute-done | bytes 165920 | tf_op jit(solution)/shard_map/ppermute | solution.py:437
  69.7 6.8 %collective-permute-done.3.refs_4_ = bf16[648,128]{1,0:T(8,128)(2,1)S(1)} collective-permute-done((bf16[648,128]{1,0:T(8,128)(2,1)}, bf16[648,128]{1,0:T(8,128)(2,1)S(1)}, u32[]{:S(2)}, u32[]{:S(2)}) %collective-permute-start.3) | collective-permute-done | bytes 165920 | tf_op jit(solution)/shard_map/ppermute | solution.py:437
  76.5 0.7 collective-permute-done.5.refs_6_
  77.2 1.9 %collective-permute-done.6.refs_7_ = bf16[648,128]{1,0:T(8,128)(2,1)S(1)} collective-permute-done((bf16[648,128]{1,0:T(8,128)(2,1)}, bf16[648,128]{1,0:T(8,128)(2,1)S(1)}, u32[]{:S(2)}, u32[]{:S(2)}) %collective-permute-start.6) | collective-permute-done | bytes 165920 | tf_op jit(solution)/shard_map/ppermute | solution.py:437
  79.1 0.9 copy-done.4
  80.0 2.4 %shard_map.119 = (bf16[552,128]{1,0:T(8,128)(2,1)}, bf16[552,128]{1,0:T(8,128)(2,1)}, bf16[552,128]{1,0:T(8,128)(2,1)}, bf16[552,128]{1,0:T(8,128)(2,1)}, bf16[5...) custom-call(f32[5]{0:T(128)S(1)} %copy-done.6, ...), custom_call_target="tpu_custom_call" | custom-call | tf_op jit(solution)/shard_map/pallas_call | solution.py:415
  82.4 1.4 %collective-permute-start.12 = (bf16[552,128]{1,0:T(8,128)(2,1)}, bf16[552,128]{1,0:T(8,128)(2,1)S(1)}, u32[]{:S(2)}, u32[]{:S(2)}) collective-permute-start(bf16[552,128]{1,0:T(8,128)(2,1)} %get-tuple-element.48), channel_id=1, source_target_pairs={{0,2},{1,3},{2,4},{3,5},{4,6},{5,7},{6,0},{7,1},{8,10},{9,11},{10,... | collective-permute-start | bytes 423944 | tf_op jit(solution)/shard_map/ppermute | solution.py:437
  83.7 3.3 %collective-permute-start.13 = (bf16[552,128]{1,0:T(8,128)(2,1)}, bf16[552,128]{1,0:T(8,128)(2,1)S(1)}, u32[]{:S(2)}, u32[]{:S(2)}) collective-permute-start(bf16[552,128]{1,0:T(8,128)(2,1)} %get-tuple-element.49), channel_id=1, source_target_pairs={{0,1},{1,2},{2,3},{3,4},{4,5},{5,6},{6,7},{7,0},{8,9},{9,10},{10,1... | collective-permute-start | bytes 423944 | tf_op jit(solution)/shard_map/ppermute | solution.py:437
  87.0 1.0 collective-permute-start.8
  88.0 2.3 %collective-permute-start.9 = (bf16[552,128]{1,0:T(8,128)(2,1)}, bf16[552,128]{1,0:T(8,128)(2,1)S(1)}, u32[]{:S(2)}, u32[]{:S(2)}) collective-permute-start(bf16[552,128]{1,0:T(8,128)(2,1)} %get-tuple-element.45), channel_id=1, source_target_pairs={{0,5},{1,6},{2,7},{3,0},{4,1},{5,2},{6,3},{7,4},{8,13},{9,14},{10,... | collective-permute-start | bytes 423944 | tf_op jit(solution)/shard_map/ppermute | solution.py:437
  90.3 1.0 collective-permute-start.11
  91.2 7.1 %collective-permute-start.10 = (bf16[552,128]{1,0:T(8,128)(2,1)}, bf16[552,128]{1,0:T(8,128)(2,1)S(1)}, u32[]{:S(2)}, u32[]{:S(2)}) collective-permute-start(bf16[552,128]{1,0:T(8,128)(2,1)} %get-tuple-element.46), channel_id=1, source_target_pairs={{0,4},{1,5},{2,6},{3,7},{4,0},{5,1},{6,2},{7,3},{8,12},{9,13},{10,... | collective-permute-start | bytes 423944 | tf_op jit(solution)/shard_map/ppermute | solution.py:437
  98.4 0.0 copy-start.2
  98.4 4.0 %shard_map.116.refs_0_ = f32[5,12,24,384]{3,2,1,0:T(8,128)S(1)} custom-call(f32[5]{0:T(128)S(1)} %copy-done.6, bf16[5,12,24,384]{3,2,1,0:T(8,128)(2,1)S(1)} %bitcast.10, bf16[5,12,24,384]{3,2,1,0:T(8,128)(2,1)} %bitcast.14, bf16[12,24,384]{2,1,0:T(8,128)(2,1)} %adv.3, bf16[2,384,384]{2,1,0:T(8,128)(2,1)} %mat.1, bf16[8,2,336,128]{3,2,1,0:T(8,128)(2,1)S(1)} %bitcast.11), custom_call_target="tpu_custom_call" | custom-call | tf_op jit(solution)/shard_map/pallas_call | solution.py:415
  102.4 0.9 shard_map.120
  103.3 0.1 collective-permute-done.9.refs_2_.refs_1_
  103.4 5.7 %collective-permute-done.11.refs_3_ = bf16[552,128]{1,0:T(8,128)(2,1)S(1)} collective-permute-done((bf16[552,128]{1,0:T(8,128)(2,1)}, bf16[552,128]{1,0:T(8,128)(2,1)S(1)}, u32[]{:S(2)}, u32[]{:S(2)}) %collective-permute-start.11) | collective-permute-done | bytes 141344 | tf_op jit(solution)/shard_map/ppermute | solution.py:437
  109.2 0.9 shard_map.121
  110.1 0.4 collective-permute-start.16
  110.5 1.1 collective-permute-start.17
  111.6 0.9 shard_map.122
  112.5 0.4 collective-permute-start.15
  112.9 0.9 shard_map.123
  113.8 1.2 collective-permute-start.14
  115.0 2.2 %collective-permute-done.17.refs_1_ = bf16[23,24,128]{2,1,0:T(8,128)(2,1)S(1)} collective-permute-done((bf16[23,24,128]{2,1,0:T(8,128)(2,1)S(1)}, bf16[23,24,128]{2,1,0:T(8,128)(2,1)S(1)}, u32[]{:S(2)}, u32[]{:S(2)}) %collective-permute-start.17) | collective-permute-done | bytes 141344 | tf_op jit(solution)/shard_map/ppermute | solution.py:541
  117.2 1.5 %shard_map.124.refs_2_ = bf16[2,5,12,24,192]{4,3,2,1,0:T(8,128)(2,1)} custom-call(s32[1]{0:T(128)} %bitcast.probe, s32[1]{0:T(128)} %bitcast.1.col, f32[2,2]{1,0:T(2,128)S(1)} %copy-done.5, bf16[23,24,128]{2,1,0:T(8,128)(2,1)S(1)} %get-tuple-element.60.refs_0_, bf16[23,24,128]{2,1,0:T(8,128)(2,1)S(1)} %collective-permute-done.17.refs_1_), custom_call_target="tpu_custom_call" | custom-call | tf_op jit(solution)/shard_map/pallas_call | solution.py:415
  118.8 1.5 %shard_map.125.refs_2_ = bf16[2,5,12,24,192]{4,3,2,1,0:T(8,128)(2,1)} custom-call(s32[1]{0:T(128)} %bitcast.probe, s32[1]{0:T(128)} %bitcast.1.col, f32[2,2]{1,0:T(2,128)S(1)} %copy-done.5, bf16[23,24,128]{2,1,0:T(8,128)(2,1)S(1)} %get-tuple-element.58.refs_0_, ...), custom_call_target="tpu_custom_call", output_to_operand_aliasing={{}: (5, {})} | custom-call | tf_op jit(solution)/shard_map/pallas_call | solution.py:415
  120.3 1.5 %shard_map.126.refs_2_ = bf16[2,5,12,24,192]{4,3,2,1,0:T(8,128)(2,1)} custom-call(s32[1]{0:T(128)} %bitcast.probe, s32[1]{0:T(128)} %bitcast.1.col, f32[2,2]{1,0:T(2,128)S(1)} %copy-done.5, bf16[23,24,128]{2,1,0:T(8,128)(2,1)S(1)} %get-tuple-element.56.refs_0_, ...), custom_call_target="tpu_custom_call", output_to_operand_aliasing={{}: (5, {})} | custom-call | tf_op jit(solution)/shard_map/pallas_call | solution.py:415
  121.8 1.5 %collective-permute-done.14.refs_1_ = bf16[23,24,128]{2,1,0:T(8,128)(2,1)S(1)} collective-permute-done((bf16[23,24,128]{2,1,0:T(8,128)(2,1)S(1)}, bf16[23,24,128]{2,1,0:T(8,128)(2,1)S(1)}, u32[]{:S(2)}, u32[]{:S(2)}) %collective-permute-start.14) | collective-permute-done | bytes 141344 | tf_op jit(solution)/shard_map/ppermute | solution.py:541
  123.3 1.5 %shard_map.127 = bf16[2,5,12,24,192]{4,3,2,1,0:T(8,128)(2,1)} custom-call(s32[1]{0:T(128)} %bitcast.probe, s32[1]{0:T(128)} %bitcast.1.col, f32[2,2]{1,0:T(2,128)S(1)} %copy-done.5, bf16[23,24,128]{2,1,0:T(8,128)(2,1)S(1)} %get-tuple-element.54.refs_0_, bf16[23,24,128]{2,1,0:T(8,128)(2,1)S(1)} %collective-permute-done.14.refs_1_, ...), custom_call_target="tpu_custom_call", output_to_operand_aliasing={{}: (5, {})} | custom-call | tf_op jit(solution)/shard_map/pallas_call | solution.py:415
  (21 shorter events, 0.0 us)
Async XLA Ops:
  3.2 29.1 %copy-start.6 = (f32[5]{0:T(128)S(1)}, f32[5]{0:T(128)}, u32[]{:S(2)}) copy-start(f32[5]{0:T(128)} %coef.5) | copy-start | bytes 64
  3.2 29.1 %all-to-all-start = ((bf16[16,336,128]{2,1,0:T(8,128)(2,1)}), bf16[16,336,128]{2,1,0:T(8,128)(2,1)S(1)}, u32[]{:S(2)}, u32[]{:S(2)}) async-start(bf16[16,336,128]{2,1,0:T(8,128)(2,1)} %bitcast.13), calls=%async_computation | async-start | bytes 2752512 | tf_op jit(solution)/shard_map/all_to_all | solution.py:483
  36.4 4.7 %copy-start = (bf16[1,5,12,24,384]{4,3,2,1,0:T(8,128)(2,1)S(1)}, bf16[1,5,12,24,384]{4,3,2,1,0:T(8,128)(2,1)}, u32[]{:S(2)}) copy-start(bf16[1,5,12,24,384]{4,3,2,1,0:T(8,128)(2,1)} %param.10) | copy-start | bytes 3317764
  36.4 4.7 %copy-start.1 = (bf16[12,24,384]{2,1,0:T(8,128)(2,1)S(1)}, bf16[12,24,384]{2,1,0:T(8,128)(2,1)}, u32[]{:S(2)}) copy-start(bf16[12,24,384]{2,1,0:T(8,128)(2,1)} %adv.5) | copy-start | bytes 663556
  36.4 61.9 %all-to-all-start.1 = ((bf16[16,336,128]{2,1,0:T(8,128)(2,1)}), bf16[16,336,128]{2,1,0:T(8,128)(2,1)S(1)}, u32[]{:S(2)}, u32[]{:S(2)}) async-start(bf16[16,336,128]{2,1,0:T(8,128)(2,1)} %shard_map.115), calls=%async_computation.1 | async-start | bytes 2752512 | tf_op jit(solution)/shard_map/all_to_all | solution.py:509
  41.1 38.0 %copy-start.3 = (bf16[384,192]{1,0:T(8,128)(2,1)S(1)}, bf16[384,192]{1,0:T(8,128)(2,1)}, u32[]{:S(2)}) copy-start(bf16[384,192]{1,0:T(8,128)(2,1)} %get-tuple-element.41.refs_8_) | copy-start | bytes 442372
  42.3 16.2 %collective-permute-start.2 = (bf16[648,128]{1,0:T(8,128)(2,1)}, bf16[648,128]{1,0:T(8,128)(2,1)S(1)}, u32[]{:S(2)}, u32[]{:S(2)}) collective-permute-start(bf16[648,128]{1,0:T(8,128)(2,1)} %get-tuple-element.36), channel_id=1, source_target_pairs={{0,3},{1,4},{2,5},{3,6},{4,7},{5,0},{6,1},{7,2},{8,11},{9,12},{10,... | collective-permute-start | bytes 497672 | tf_op jit(solution)/shard_map/ppermute | solution.py:437
  46.7 16.9 %collective-permute-start.4 = (bf16[648,128]{1,0:T(8,128)(2,1)}, bf16[648,128]{1,0:T(8,128)(2,1)S(1)}, u32[]{:S(2)}, u32[]{:S(2)}) collective-permute-start(bf16[648,128]{1,0:T(8,128)(2,1)} %get-tuple-element.38), channel_id=1, source_target_pairs={{0,5},{1,6},{2,7},{3,0},{4,1},{5,2},{6,3},{7,4},{8,13},{9,14},{10,... | collective-permute-start | bytes 497672 | tf_op jit(solution)/shard_map/ppermute | solution.py:437
  51.1 12.5 %collective-permute-start = (bf16[648,128]{1,0:T(8,128)(2,1)}, bf16[648,128]{1,0:T(8,128)(2,1)S(1)}, u32[]{:S(2)}, u32[]{:S(2)}) collective-permute-start(bf16[648,128]{1,0:T(8,128)(2,1)} %get-tuple-element.34), channel_id=1, source_target_pairs={{0,1},{1,2},{2,3},{3,4},{4,5},{5,6},{6,7},{7,0},{8,9},{9,10},{10,1... | collective-permute-start | bytes 497672 | tf_op jit(solution)/shard_map/ppermute | solution.py:437
  51.9 17.8 %collective-permute-start.1 = (bf16[648,128]{1,0:T(8,128)(2,1)}, bf16[648,128]{1,0:T(8,128)(2,1)S(1)}, u32[]{:S(2)}, u32[]{:S(2)}) collective-permute-start(bf16[648,128]{1,0:T(8,128)(2,1)} %get-tuple-element.35), channel_id=1, source_target_pairs={{0,2},{1,3},{2,4},{3,5},{4,6},{5,7},{6,0},{7,1},{8,10},{9,11},{10,... | collective-permute-start | bytes 497672 | tf_op jit(solution)/shard_map/ppermute | solution.py:437
  53.0 23.5 %collective-permute-start.3 = (bf16[648,128]{1,0:T(8,128)(2,1)}, bf16[648,128]{1,0:T(8,128)(2,1)S(1)}, u32[]{:S(2)}, u32[]{:S(2)}) collective-permute-start(bf16[648,128]{1,0:T(8,128)(2,1)} %get-tuple-element.37), channel_id=1, source_target_pairs={{0,4},{1,5},{2,6},{3,7},{4,0},{5,1},{6,2},{7,3},{8,12},{9,13},{10,... | collective-permute-start | bytes 497672 | tf_op jit(solution)/shard_map/ppermute | solution.py:437
  58.5 18.7 %collective-permute-start.5 = (bf16[648,128]{1,0:T(8,128)(2,1)}, bf16[648,128]{1,0:T(8,128)(2,1)S(1)}, u32[]{:S(2)}, u32[]{:S(2)}) collective-permute-start(bf16[648,128]{1,0:T(8,128)(2,1)} %get-tuple-element.39), channel_id=1, source_target_pairs={{0,6},{1,7},{2,0},{3,1},{4,2},{5,3},{6,4},{7,5},{8,14},{9,15},{10,... | collective-permute-start | bytes 497672 | tf_op jit(solution)/shard_map/ppermute | solution.py:437
  63.6 15.4 %collective-permute-start.6 = (bf16[648,128]{1,0:T(8,128)(2,1)}, bf16[648,128]{1,0:T(8,128)(2,1)S(1)}, u32[]{:S(2)}, u32[]{:S(2)}) collective-permute-start(bf16[648,128]{1,0:T(8,128)(2,1)} %get-tuple-element.40), channel_id=1, source_target_pairs={{0,7},{1,0},{2,1},{3,2},{4,3},{5,4},{6,5},{7,6},{8,15},{9,8},{10,9... | collective-permute-start | bytes 497672 | tf_op jit(solution)/shard_map/ppermute | solution.py:437
  79.1 0.9 copy-start.4
  82.4 8.9 %collective-permute-start.12 = (bf16[552,128]{1,0:T(8,128)(2,1)}, bf16[552,128]{1,0:T(8,128)(2,1)S(1)}, u32[]{:S(2)}, u32[]{:S(2)}) collective-permute-start(bf16[552,128]{1,0:T(8,128)(2,1)} %get-tuple-element.48), channel_id=1, source_target_pairs={{0,2},{1,3},{2,4},{3,5},{4,6},{5,7},{6,0},{7,1},{8,10},{9,11},{10,... | collective-permute-start | bytes 423944 | tf_op jit(solution)/shard_map/ppermute | solution.py:437
  83.7 14.6 %collective-permute-start.13 = (bf16[552,128]{1,0:T(8,128)(2,1)}, bf16[552,128]{1,0:T(8,128)(2,1)S(1)}, u32[]{:S(2)}, u32[]{:S(2)}) collective-permute-start(bf16[552,128]{1,0:T(8,128)(2,1)} %get-tuple-element.49), channel_id=1, source_target_pairs={{0,1},{1,2},{2,3},{3,4},{4,5},{5,6},{6,7},{7,0},{8,9},{9,10},{10,1... | collective-permute-start | bytes 423944 | tf_op jit(solution)/shard_map/ppermute | solution.py:437
  87.0 16.3 %collective-permute-start.8 = (bf16[552,128]{1,0:T(8,128)(2,1)}, bf16[552,128]{1,0:T(8,128)(2,1)S(1)}, u32[]{:S(2)}, u32[]{:S(2)}) collective-permute-start(bf16[552,128]{1,0:T(8,128)(2,1)} %get-tuple-element.44), channel_id=1, source_target_pairs={{0,6},{1,7},{2,0},{3,1},{4,2},{5,3},{6,4},{7,5},{8,14},{9,15},{10,... | collective-permute-start | bytes 423944 | tf_op jit(solution)/shard_map/ppermute | solution.py:437
  88.0 15.4 %collective-permute-start.9 = (bf16[552,128]{1,0:T(8,128)(2,1)}, bf16[552,128]{1,0:T(8,128)(2,1)S(1)}, u32[]{:S(2)}, u32[]{:S(2)}) collective-permute-start(bf16[552,128]{1,0:T(8,128)(2,1)} %get-tuple-element.45), channel_id=1, source_target_pairs={{0,5},{1,6},{2,7},{3,0},{4,1},{5,2},{6,3},{7,4},{8,13},{9,14},{10,... | collective-permute-start | bytes 423944 | tf_op jit(solution)/shard_map/ppermute | solution.py:437
  90.3 18.9 %collective-permute-start.11 = (bf16[552,128]{1,0:T(8,128)(2,1)}, bf16[552,128]{1,0:T(8,128)(2,1)S(1)}, u32[]{:S(2)}, u32[]{:S(2)}) collective-permute-start(bf16[552,128]{1,0:T(8,128)(2,1)} %get-tuple-element.47), channel_id=1, source_target_pairs={{0,3},{1,4},{2,5},{3,6},{4,7},{5,0},{6,1},{7,2},{8,11},{9,12},{10,... | collective-permute-start | bytes 423944 | tf_op jit(solution)/shard_map/ppermute | solution.py:437
  91.2 20.4 %collective-permute-start.10 = (bf16[552,128]{1,0:T(8,128)(2,1)}, bf16[552,128]{1,0:T(8,128)(2,1)S(1)}, u32[]{:S(2)}, u32[]{:S(2)}) collective-permute-start(bf16[552,128]{1,0:T(8,128)(2,1)} %get-tuple-element.46), channel_id=1, source_target_pairs={{0,4},{1,5},{2,6},{3,7},{4,0},{5,1},{6,2},{7,3},{8,12},{9,13},{10,... | collective-permute-start | bytes 423944 | tf_op jit(solution)/shard_map/ppermute | solution.py:437
  98.4 14.6 %collective-permute-start.7 = (bf16[552,128]{1,0:T(8,128)(2,1)}, bf16[552,128]{1,0:T(8,128)(2,1)S(1)}, u32[]{:S(2)}, u32[]{:S(2)}) collective-permute-start(bf16[552,128]{1,0:T(8,128)(2,1)} %get-tuple-element.43), channel_id=1, source_target_pairs={{0,7},{1,0},{2,1},{3,2},{4,3},{5,4},{6,5},{7,6},{8,15},{9,8},{10,9... | collective-permute-start | bytes 423944 | tf_op jit(solution)/shard_map/ppermute | solution.py:437
  98.4 4.0 %copy-start.2 = (bf16[552,128]{1,0:T(8,128)(2,1)S(1)}, bf16[552,128]{1,0:T(8,128)(2,1)}, u32[]{:S(2)}) copy-start(bf16[552,128]{1,0:T(8,128)(2,1)} %get-tuple-element.42.refs_1_) | copy-start | bytes 423940
  110.1 8.7 %collective-permute-start.16 = (bf16[23,24,128]{2,1,0:T(8,128)(2,1)S(1)}, bf16[23,24,128]{2,1,0:T(8,128)(2,1)S(1)}, u32[]{:S(2)}, u32[]{:S(2)}) collective-permute-start(bf16[23,24,128]{2,1,0:T(8,128)(2,1)S(1)} %get-tuple-element.59), channel_id=1, source_target_pairs={{0,128},{128,0},{1,129},{129,1},{2,130},{130,2},{3,131},{131,3},{4... | collective-permute-start | bytes 423944 | tf_op jit(solution)/shard_map/ppermute | solution.py:541
  110.5 6.8 %collective-permute-start.17 = (bf16[23,24,128]{2,1,0:T(8,128)(2,1)S(1)}, bf16[23,24,128]{2,1,0:T(8,128)(2,1)S(1)}, u32[]{:S(2)}, u32[]{:S(2)}) collective-permute-start(bf16[23,24,128]{2,1,0:T(8,128)(2,1)S(1)} %get-tuple-element.61), channel_id=1, source_target_pairs={{0,128},{128,0},{1,129},{129,1},{2,130},{130,2},{3,131},{131,3},{4... | collective-permute-start | bytes 423944 | tf_op jit(solution)/shard_map/ppermute | solution.py:541
  112.5 7.8 %collective-permute-start.15 = (bf16[23,24,128]{2,1,0:T(8,128)(2,1)S(1)}, bf16[23,24,128]{2,1,0:T(8,128)(2,1)S(1)}, u32[]{:S(2)}, u32[]{:S(2)}) collective-permute-start(bf16[23,24,128]{2,1,0:T(8,128)(2,1)S(1)} %get-tuple-element.57), channel_id=1, source_target_pairs={{0,128},{128,0},{1,129},{129,1},{2,130},{130,2},{3,131},{131,3},{4... | collective-permute-start | bytes 423944 | tf_op jit(solution)/shard_map/ppermute | solution.py:541
  112.9 4.3 %copy-start.5 = (f32[2,2]{1,0:T(2,128)S(1)}, f32[2,2]{1,0:T(2,128)}, u32[]{:S(2)}) copy-start(f32[2,2]{1,0:T(2,128)} %mix.7) | copy-start | bytes 52
  113.8 9.5 %collective-permute-start.14 = (bf16[23,24,128]{2,1,0:T(8,128)(2,1)S(1)}, bf16[23,24,128]{2,1,0:T(8,128)(2,1)S(1)}, u32[]{:S(2)}, u32[]{:S(2)}) collective-permute-start(bf16[23,24,128]{2,1,0:T(8,128)(2,1)S(1)} %get-tuple-element.55), channel_id=1, source_target_pairs={{0,128},{128,0},{1,129},{129,1},{2,130},{130,2},{3,131},{131,3},{4... | collective-permute-start | bytes 423944 | tf_op jit(solution)/shard_map/ppermute | solution.py:541

commit v6 on v5

--- a/solution.py
+++ b/solution.py
@@ -371,9 +371,17 @@
         copy_of(yl).wait()
 
 
-def sketch_kernel(n, probe, col, mix, *refs):
-    own, recv = refs[:2]
+def sketch_kernel(chunks, probe, col, mix, *refs):
     out, rows, sem = refs[-3:]
+    for k, n in enumerate(chunks):
+        own, recv = refs[2 * k : 2 * k + 2]
+        sketch_part(n, probe, col, mix, own, recv, out, rows.at[k], sem.at[k])
+    for k in range(len(chunks)):
+        for g in range(2):
+            pltpu.make_async_copy(rows.at[k, g], out.at[g, :, 0:3], sem.at[k, g]).wait()
+
+
+def sketch_part(n, probe, col, mix, own, recv, out, rows, sem):
     p = probe[0]
     low = low_lanes((24, 128))
     group = group_of(n, col[0])
@@ -404,8 +412,6 @@
         put(g, 4, 1, mixed(9, g), swap(half))
         put(g, 4, 2, mixed(14, g), mixed(22, g))
         copy_of(g).start()
-    for g in range(2):
-        copy_of(g).wait()
 
 
 def call(kernel, out_shapes, scalars, arrays, scratch=(), kept=(), spaces=None, stay=False):
@@ -539,15 +545,17 @@
         )
         sections.append(section)
         halves.append((own, lax.ppermute(send, "probe", [(0, 1), (1, 0)])))
-    for n in range(4):
-        own, recv = halves[n]
+    for chunks in ((0, 1), (2,), (3,)):
         sketches.append(
             call(
-                functools.partial(sketch_kernel, n),
+                functools.partial(sketch_kernel, chunks),
                 [shape((2, 5, 12, 24, 192))],
                 [probe, col, test_mix],
-                [near(own), near(recv)],
-                [pltpu.VMEM((2, 5, 3, 24, 192), BF16), pltpu.SemaphoreType.DMA((2,))],
+                [near(x) for n in chunks for x in halves[n]],
+                [
+                    pltpu.VMEM((len(chunks), 2, 5, 3, 24, 192), BF16),
+                    pltpu.SemaphoreType.DMA((len(chunks), 2)),
+                ],
                 kept=sketches[-1:],
                 spaces=[any_space],
             )[0]

time: 127 us -> 126 us (level)
    pallas_call x15 -> x14, Pallas kernels: 29.1 us -> 27.9 us  [call(): pl.pallas_call(kernel, out_shape=out_shapes, in_specs=[sspec()] * len(sca...]
  transfers between devices with their start and end apart: 20 -> 20, of which waited for: 10 -> 11; matrix products, arithmetic and copies ran while one was open for 0% -> 0% of each run, Pallas kernels for 17% -> 16%
where the time goes in v6:
time: 126 us; the launch traced here: 125 us
  starting transfers between devices  50.2 us (40%)
  waiting for transfers between devices  44.9 us (36%)
  Pallas kernels  27.9 us (22%)
    ppermute x14, starting transfers between devices, shift(): return lax.ppermute(x, 'col', [(i, (i + distance) % 8) for i in range(8)])  33.9 us
    pallas_call x14, Pallas kernels, call(): pl.pallas_call(kernel, out_shape=out_shapes, in_specs=[sspec()] * len(sca...  27.9 us
    ppermute x14, waiting for transfers between devices, shift(): return lax.ppermute(x, 'col', [(i, (i + distance) % 8) for i in range(8)])  22.5 us
    all_to_all x1, waiting for transfers between devices, on_device(): lax.all_to_all(to_y.reshape(16, 336, 128), 'row', split_axis=0, concat_ax...  17.5 us
    all_to_all x1, starting transfers between devices, on_device(): lax.all_to_all(to_y.reshape(16, 336, 128), 'row', split_axis=0, concat_ax...  8.45 us
    ppermute x4, waiting for transfers between devices, on_device(): halves.append((own, lax.ppermute(send, 'probe', [(0, 1), (1, 0)])))  4.93 us
    all_to_all x1, starting transfers between devices, on_device(): lax.all_to_all(term_y, 'row', split_axis=0, concat_axis=0, tiled=True)  4.65 us
    ppermute x4, starting transfers between devices, on_device(): halves.append((own, lax.ppermute(send, 'probe', [(0, 1), (1, 0)])))  3.19 us
  transfers between devices with their start and end apart: 20, of which 11 were waited for; matrix products, arithmetic and copies ran while one was open for 0% of the time, Pallas kernels for 16%

profile of v6, /device:TPU:1, one launch (start us, length us, event | category | flops | bytes accessed | tf_op | source)
XLA Modules:
  0.0 125.0 jit_solution(11481386237162532817)
XLA Ops:
  0.6 2.6 %shard_map.113 = bf16[8,2,336,128]{3,2,1,0:T(8,128)(2,1)} custom-call(bf16[5,12,24,384]{3,2,1,0:T(8,128)(2,1)} %bitcast.7, bf16[12,24,384]{2,1,0:T(8,128)(2,1)} %adv_far.1), custom_call_target="tpu_custom_call" | custom-call | tf_op jit(solution)/shard_map/pallas_call | solution.py:421
  3.2 0.0 copy-start.6
  3.2 8.4 %all-to-all-start = ((bf16[16,336,128]{2,1,0:T(8,128)(2,1)}), bf16[16,336,128]{2,1,0:T(8,128)(2,1)S(1)}, u32[]{:S(2)}, u32[]{:S(2)}) async-start(bf16[16,336,128]{2,1,0:T(8,128)(2,1)} %bitcast.13), calls=%async_computation | async-start | bytes 2752512 | tf_op jit(solution)/shard_map/all_to_all | solution.py:489
  11.6 3.1 %shard_map.114 = (bf16[1152,384]{1,0:T(8,128)(2,1)}, bf16[384,192]{1,0:T(8,128)(2,1)}) custom-call(s32[1]{0:T(128)} %bitcast.1.col, bf16[2,192,192]{2,1,0:T(8,128)(2,1)} %mat_y.1, bf16[2,192,192]{2,1,0:T(8,128)(2,1)} %mat_z.1), custom_call_target="tpu_custom_call" | custom-call | tf_op jit(solution)/shard_map/pallas_call | solution.py:421
  14.7 17.5 %all-to-all-done.recv = bf16[16,336,128]{2,1,0:T(8,128)(2,1)S(1)} async-done(((bf16[16,336,128]{2,1,0:T(8,128)(2,1)}), bf16[16,336,128]{2,1,0:T(8,128)(2,1)S(1)}, u32[]{:S(2)}, u32[]{:S(2)}) %all-to-all-start) | async-done | bytes 1376288 | tf_op jit(solution)/shard_map/all_to_all | solution.py:489
  32.3 4.2 %shard_map.115 = bf16[16,336,128]{2,1,0:T(8,128)(2,1)} custom-call(f32[5]{0:T(128)S(1)} %copy-done.6, bf16[16,336,128]{2,1,0:T(8,128)(2,1)S(1)} %all-to-all-done.recv, bf16[1152,384]{1,0:T(8,128)(2,1)} %get-tuple-element.32.lines), custom_call_target="tpu_custom_call" | custom-call | tf_op jit(solution)/shard_map/pallas_call | solution.py:421
  36.4 4.6 %all-to-all-start.1 = ((bf16[16,336,128]{2,1,0:T(8,128)(2,1)}), bf16[16,336,128]{2,1,0:T(8,128)(2,1)S(1)}, u32[]{:S(2)}, u32[]{:S(2)}) async-start(bf16[16,336,128]{2,1,0:T(8,128)(2,1)} %shard_map.115), calls=%async_computation.1 | async-start | bytes 2752512 | tf_op jit(solution)/shard_map/all_to_all | solution.py:515
  41.1 1.2 shard_map.118
  42.3 4.4 %collective-permute-start.2 = (bf16[648,128]{1,0:T(8,128)(2,1)}, bf16[648,128]{1,0:T(8,128)(2,1)S(1)}, u32[]{:S(2)}, u32[]{:S(2)}) collective-permute-start(bf16[648,128]{1,0:T(8,128)(2,1)} %get-tuple-element.36), channel_id=1, source_target_pairs={{0,3},{1,4},{2,5},{3,6},{4,7},{5,0},{6,1},{7,2},{8,11},{9,12},{10,... | collective-permute-start | bytes 497672 | tf_op jit(solution)/shard_map/ppermute | solution.py:443
  46.7 2.2 %collective-permute-start.4 = (bf16[648,128]{1,0:T(8,128)(2,1)}, bf16[648,128]{1,0:T(8,128)(2,1)S(1)}, u32[]{:S(2)}, u32[]{:S(2)}) collective-permute-start(bf16[648,128]{1,0:T(8,128)(2,1)} %get-tuple-element.38), channel_id=1, source_target_pairs={{0,5},{1,6},{2,7},{3,0},{4,1},{5,2},{6,3},{7,4},{8,13},{9,14},{10,... | collective-permute-start | bytes 497672 | tf_op jit(solution)/shard_map/ppermute | solution.py:443
  48.9 2.2 %shard_map.117 = (bf16[648,128]{1,0:T(8,128)(2,1)}, bf16[648,128]{1,0:T(8,128)(2,1)}, bf16[648,128]{1,0:T(8,128)(2,1)}, bf16[648,128]{1,0:T(8,128)(2,1)}, bf16[6...) custom-call(s32[1]{0:T(128)} %bitcast.1.col, bf16[5,12,24,384]{3,2,1,0:T(8,128)(2,1)S(1)} %bitcast.9, ...), custom_call_target="tpu_custom_call" | custom-call | tf_op jit(solution)/shard_map/pallas_call | solution.py:421
  51.1 0.8 collective-permute-start
  51.9 1.1 collective-permute-start.1
  53.0 4.3 %collective-permute-start.3 = (bf16[648,128]{1,0:T(8,128)(2,1)}, bf16[648,128]{1,0:T(8,128)(2,1)S(1)}, u32[]{:S(2)}, u32[]{:S(2)}) collective-permute-start(bf16[648,128]{1,0:T(8,128)(2,1)} %get-tuple-element.37), channel_id=1, source_target_pairs={{0,4},{1,5},{2,6},{3,7},{4,0},{5,1},{6,2},{7,3},{8,12},{9,13},{10,... | collective-permute-start | bytes 497672 | tf_op jit(solution)/shard_map/ppermute | solution.py:443
  57.3 1.2 collective-permute-done.2.refs_3_
  58.5 5.1 %collective-permute-start.5 = (bf16[648,128]{1,0:T(8,128)(2,1)}, bf16[648,128]{1,0:T(8,128)(2,1)S(1)}, u32[]{:S(2)}, u32[]{:S(2)}) collective-permute-start(bf16[648,128]{1,0:T(8,128)(2,1)} %get-tuple-element.39), channel_id=1, source_target_pairs={{0,6},{1,7},{2,0},{3,1},{4,2},{5,3},{6,4},{7,5},{8,14},{9,15},{10,... | collective-permute-start | bytes 497672 | tf_op jit(solution)/shard_map/ppermute | solution.py:443
  63.6 0.0 collective-permute-start.6
  63.6 0.0 collective-permute-done.refs_1_
  63.6 6.0 %collective-permute-done.1.refs_2_ = bf16[648,128]{1,0:T(8,128)(2,1)S(1)} collective-permute-done((bf16[648,128]{1,0:T(8,128)(2,1)}, bf16[648,128]{1,0:T(8,128)(2,1)S(1)}, u32[]{:S(2)}, u32[]{:S(2)}) %collective-permute-start.1) | collective-permute-done | bytes 165920 | tf_op jit(solution)/shard_map/ppermute | solution.py:443
  69.7 6.8 %collective-permute-done.3.refs_4_ = bf16[648,128]{1,0:T(8,128)(2,1)S(1)} collective-permute-done((bf16[648,128]{1,0:T(8,128)(2,1)}, bf16[648,128]{1,0:T(8,128)(2,1)S(1)}, u32[]{:S(2)}, u32[]{:S(2)}) %collective-permute-start.3) | collective-permute-done | bytes 165920 | tf_op jit(solution)/shard_map/ppermute | solution.py:443
  76.5 0.7 collective-permute-done.5.refs_6_
  77.2 1.9 %collective-permute-done.6.refs_7_ = bf16[648,128]{1,0:T(8,128)(2,1)S(1)} collective-permute-done((bf16[648,128]{1,0:T(8,128)(2,1)}, bf16[648,128]{1,0:T(8,128)(2,1)S(1)}, u32[]{:S(2)}, u32[]{:S(2)}) %collective-permute-start.6) | collective-permute-done | bytes 165920 | tf_op jit(solution)/shard_map/ppermute | solution.py:443
  79.1 0.9 copy-done.4
  80.0 2.4 %shard_map.119 = (bf16[552,128]{1,0:T(8,128)(2,1)}, bf16[552,128]{1,0:T(8,128)(2,1)}, bf16[552,128]{1,0:T(8,128)(2,1)}, bf16[552,128]{1,0:T(8,128)(2,1)}, bf16[5...) custom-call(f32[5]{0:T(128)S(1)} %copy-done.6, ...), custom_call_target="tpu_custom_call" | custom-call | tf_op jit(solution)/shard_map/pallas_call | solution.py:421
  82.4 1.4 %collective-permute-start.12 = (bf16[552,128]{1,0:T(8,128)(2,1)}, bf16[552,128]{1,0:T(8,128)(2,1)S(1)}, u32[]{:S(2)}, u32[]{:S(2)}) collective-permute-start(bf16[552,128]{1,0:T(8,128)(2,1)} %get-tuple-element.48), channel_id=1, source_target_pairs={{0,2},{1,3},{2,4},{3,5},{4,6},{5,7},{6,0},{7,1},{8,10},{9,11},{10,... | collective-permute-start | bytes 423944 | tf_op jit(solution)/shard_map/ppermute | solution.py:443
  83.7 3.3 %collective-permute-start.13 = (bf16[552,128]{1,0:T(8,128)(2,1)}, bf16[552,128]{1,0:T(8,128)(2,1)S(1)}, u32[]{:S(2)}, u32[]{:S(2)}) collective-permute-start(bf16[552,128]{1,0:T(8,128)(2,1)} %get-tuple-element.49), channel_id=1, source_target_pairs={{0,1},{1,2},{2,3},{3,4},{4,5},{5,6},{6,7},{7,0},{8,9},{9,10},{10,1... | collective-permute-start | bytes 423944 | tf_op jit(solution)/shard_map/ppermute | solution.py:443
  87.0 1.0 collective-permute-start.8
  88.0 2.3 %collective-permute-start.9 = (bf16[552,128]{1,0:T(8,128)(2,1)}, bf16[552,128]{1,0:T(8,128)(2,1)S(1)}, u32[]{:S(2)}, u32[]{:S(2)}) collective-permute-start(bf16[552,128]{1,0:T(8,128)(2,1)} %get-tuple-element.45), channel_id=1, source_target_pairs={{0,5},{1,6},{2,7},{3,0},{4,1},{5,2},{6,3},{7,4},{8,13},{9,14},{10,... | collective-permute-start | bytes 423944 | tf_op jit(solution)/shard_map/ppermute | solution.py:443
  90.3 1.0 collective-permute-start.11
  91.2 7.1 %collective-permute-start.10 = (bf16[552,128]{1,0:T(8,128)(2,1)}, bf16[552,128]{1,0:T(8,128)(2,1)S(1)}, u32[]{:S(2)}, u32[]{:S(2)}) collective-permute-start(bf16[552,128]{1,0:T(8,128)(2,1)} %get-tuple-element.46), channel_id=1, source_target_pairs={{0,4},{1,5},{2,6},{3,7},{4,0},{5,1},{6,2},{7,3},{8,12},{9,13},{10,... | collective-permute-start | bytes 423944 | tf_op jit(solution)/shard_map/ppermute | solution.py:443
  98.4 0.0 copy-start.2
  98.4 4.0 %shard_map.116.refs_0_ = f32[5,12,24,384]{3,2,1,0:T(8,128)S(1)} custom-call(f32[5]{0:T(128)S(1)} %copy-done.6, bf16[5,12,24,384]{3,2,1,0:T(8,128)(2,1)S(1)} %bitcast.10, bf16[5,12,24,384]{3,2,1,0:T(8,128)(2,1)} %bitcast.14, bf16[12,24,384]{2,1,0:T(8,128)(2,1)} %adv.3, bf16[2,384,384]{2,1,0:T(8,128)(2,1)} %mat.1, bf16[8,2,336,128]{3,2,1,0:T(8,128)(2,1)S(1)} %bitcast.11), custom_call_target="tpu_custom_call" | custom-call | tf_op jit(solution)/shard_map/pallas_call | solution.py:421
  102.4 0.9 shard_map.120
  103.3 0.1 collective-permute-done.9.refs_2_.refs_1_
  103.4 5.7 %collective-permute-done.11.refs_3_ = bf16[552,128]{1,0:T(8,128)(2,1)S(1)} collective-permute-done((bf16[552,128]{1,0:T(8,128)(2,1)}, bf16[552,128]{1,0:T(8,128)(2,1)S(1)}, u32[]{:S(2)}, u32[]{:S(2)}) %collective-permute-start.11) | collective-permute-done | bytes 141344 | tf_op jit(solution)/shard_map/ppermute | solution.py:443
  109.2 0.9 shard_map.121
  110.1 0.4 collective-permute-start.17
  110.5 1.1 collective-permute-start.16
  111.6 0.9 shard_map.122
  112.5 0.4 collective-permute-start.15
  112.9 0.9 shard_map.123
  113.8 1.2 collective-permute-start.14
  115.0 2.2 %collective-permute-done.16.refs_1_ = bf16[23,24,128]{2,1,0:T(8,128)(2,1)S(1)} collective-permute-done((bf16[23,24,128]{2,1,0:T(8,128)(2,1)S(1)}, bf16[23,24,128]{2,1,0:T(8,128)(2,1)S(1)}, u32[]{:S(2)}, u32[]{:S(2)}) %collective-permute-start.16) | collective-permute-done | bytes 141344 | tf_op jit(solution)/shard_map/ppermute | solution.py:547
  117.2 1.8 %shard_map.124.refs_2_ = bf16[2,5,12,24,192]{4,3,2,1,0:T(8,128)(2,1)} custom-call(s32[1]{0:T(128)} %bitcast.probe, s32[1]{0:T(128)} %bitcast.1.col, f32[2,2]{1,0:T(2,128)S(1)} %copy-done.5, bf16[23,24,128]{2,1,0:T(8,128)(2,1)S(1)} %get-tuple-element.58.refs_0_, bf16[23,24,128]{2,1,0:T(8,128)(2,1)S(1)} %collective-permute-done.16.refs_1_, ...), custom_call_target="tpu_custom_call" | custom-call | tf_op jit(solution)/shard_map/pallas_call | solution.py:421
  119.0 1.2 collective-permute-done.15.refs_1_
  120.3 1.5 %shard_map.125.refs_2_ = bf16[2,5,12,24,192]{4,3,2,1,0:T(8,128)(2,1)} custom-call(s32[1]{0:T(128)} %bitcast.probe, s32[1]{0:T(128)} %bitcast.1.col, f32[2,2]{1,0:T(2,128)S(1)} %copy-done.5, bf16[23,24,128]{2,1,0:T(8,128)(2,1)S(1)} %get-tuple-element.56.refs_0_, ...), custom_call_target="tpu_custom_call", output_to_operand_aliasing={{}: (5, {})} | custom-call | tf_op jit(solution)/shard_map/pallas_call | solution.py:421
  121.8 1.5 %collective-permute-done.14.refs_1_ = bf16[23,24,128]{2,1,0:T(8,128)(2,1)S(1)} collective-permute-done((bf16[23,24,128]{2,1,0:T(8,128)(2,1)S(1)}, bf16[23,24,128]{2,1,0:T(8,128)(2,1)S(1)}, u32[]{:S(2)}, u32[]{:S(2)}) %collective-permute-start.14) | collective-permute-done | bytes 141344 | tf_op jit(solution)/shard_map/ppermute | solution.py:547
  123.3 1.5 %shard_map.126 = bf16[2,5,12,24,192]{4,3,2,1,0:T(8,128)(2,1)} custom-call(s32[1]{0:T(128)} %bitcast.probe, s32[1]{0:T(128)} %bitcast.1.col, f32[2,2]{1,0:T(2,128)S(1)} %copy-done.5, bf16[23,24,128]{2,1,0:T(8,128)(2,1)S(1)} %get-tuple-element.54.refs_0_, bf16[23,24,128]{2,1,0:T(8,128)(2,1)S(1)} %collective-permute-done.14.refs_1_, ...), custom_call_target="tpu_custom_call", output_to_operand_aliasing={{}: (5, {})} | custom-call | tf_op jit(solution)/shard_map/pallas_call | solution.py:421
  (20 shorter events, 0.0 us)
Async XLA Ops:
  3.2 29.1 %copy-start.6 = (f32[5]{0:T(128)S(1)}, f32[5]{0:T(128)}, u32[]{:S(2)}) copy-start(f32[5]{0:T(128)} %coef.5) | copy-start | bytes 64
  3.2 29.1 %all-to-all-start = ((bf16[16,336,128]{2,1,0:T(8,128)(2,1)}), bf16[16,336,128]{2,1,0:T(8,128)(2,1)S(1)}, u32[]{:S(2)}, u32[]{:S(2)}) async-start(bf16[16,336,128]{2,1,0:T(8,128)(2,1)} %bitcast.13), calls=%async_computation | async-start | bytes 2752512 | tf_op jit(solution)/shard_map/all_to_all | solution.py:489
  36.4 4.7 %copy-start = (bf16[1,5,12,24,384]{4,3,2,1,0:T(8,128)(2,1)S(1)}, bf16[1,5,12,24,384]{4,3,2,1,0:T(8,128)(2,1)}, u32[]{:S(2)}) copy-start(bf16[1,5,12,24,384]{4,3,2,1,0:T(8,128)(2,1)} %param.10) | copy-start | bytes 3317764
  36.4 4.7 %copy-start.1 = (bf16[12,24,384]{2,1,0:T(8,128)(2,1)S(1)}, bf16[12,24,384]{2,1,0:T(8,128)(2,1)}, u32[]{:S(2)}) copy-start(bf16[12,24,384]{2,1,0:T(8,128)(2,1)} %adv.5) | copy-start | bytes 663556
  36.4 61.9 %all-to-all-start.1 = ((bf16[16,336,128]{2,1,0:T(8,128)(2,1)}), bf16[16,336,128]{2,1,0:T(8,128)(2,1)S(1)}, u32[]{:S(2)}, u32[]{:S(2)}) async-start(bf16[16,336,128]{2,1,0:T(8,128)(2,1)} %shard_map.115), calls=%async_computation.1 | async-start | bytes 2752512 | tf_op jit(solution)/shard_map/all_to_all | solution.py:515
  41.1 38.0 %copy-start.3 = (bf16[384,192]{1,0:T(8,128)(2,1)S(1)}, bf16[384,192]{1,0:T(8,128)(2,1)}, u32[]{:S(2)}) copy-start(bf16[384,192]{1,0:T(8,128)(2,1)} %get-tuple-element.41.refs_8_) | copy-start | bytes 442372
  42.3 16.2 %collective-permute-start.2 = (bf16[648,128]{1,0:T(8,128)(2,1)}, bf16[648,128]{1,0:T(8,128)(2,1)S(1)}, u32[]{:S(2)}, u32[]{:S(2)}) collective-permute-start(bf16[648,128]{1,0:T(8,128)(2,1)} %get-tuple-element.36), channel_id=1, source_target_pairs={{0,3},{1,4},{2,5},{3,6},{4,7},{5,0},{6,1},{7,2},{8,11},{9,12},{10,... | collective-permute-start | bytes 497672 | tf_op jit(solution)/shard_map/ppermute | solution.py:443
  46.7 16.9 %collective-permute-start.4 = (bf16[648,128]{1,0:T(8,128)(2,1)}, bf16[648,128]{1,0:T(8,128)(2,1)S(1)}, u32[]{:S(2)}, u32[]{:S(2)}) collective-permute-start(bf16[648,128]{1,0:T(8,128)(2,1)} %get-tuple-element.38), channel_id=1, source_target_pairs={{0,5},{1,6},{2,7},{3,0},{4,1},{5,2},{6,3},{7,4},{8,13},{9,14},{10,... | collective-permute-start | bytes 497672 | tf_op jit(solution)/shard_map/ppermute | solution.py:443
  51.1 12.5 %collective-permute-start = (bf16[648,128]{1,0:T(8,128)(2,1)}, bf16[648,128]{1,0:T(8,128)(2,1)S(1)}, u32[]{:S(2)}, u32[]{:S(2)}) collective-permute-start(bf16[648,128]{1,0:T(8,128)(2,1)} %get-tuple-element.34), channel_id=1, source_target_pairs={{0,1},{1,2},{2,3},{3,4},{4,5},{5,6},{6,7},{7,0},{8,9},{9,10},{10,1... | collective-permute-start | bytes 497672 | tf_op jit(solution)/shard_map/ppermute | solution.py:443
  51.9 17.8 %collective-permute-start.1 = (bf16[648,128]{1,0:T(8,128)(2,1)}, bf16[648,128]{1,0:T(8,128)(2,1)S(1)}, u32[]{:S(2)}, u32[]{:S(2)}) collective-permute-start(bf16[648,128]{1,0:T(8,128)(2,1)} %get-tuple-element.35), channel_id=1, source_target_pairs={{0,2},{1,3},{2,4},{3,5},{4,6},{5,7},{6,0},{7,1},{8,10},{9,11},{10,... | collective-permute-start | bytes 497672 | tf_op jit(solution)/shard_map/ppermute | solution.py:443
  53.0 23.5 %collective-permute-start.3 = (bf16[648,128]{1,0:T(8,128)(2,1)}, bf16[648,128]{1,0:T(8,128)(2,1)S(1)}, u32[]{:S(2)}, u32[]{:S(2)}) collective-permute-start(bf16[648,128]{1,0:T(8,128)(2,1)} %get-tuple-element.37), channel_id=1, source_target_pairs={{0,4},{1,5},{2,6},{3,7},{4,0},{5,1},{6,2},{7,3},{8,12},{9,13},{10,... | collective-permute-start | bytes 497672 | tf_op jit(solution)/shard_map/ppermute | solution.py:443
  58.5 18.7 %collective-permute-start.5 = (bf16[648,128]{1,0:T(8,128)(2,1)}, bf16[648,128]{1,0:T(8,128)(2,1)S(1)}, u32[]{:S(2)}, u32[]{:S(2)}) collective-permute-start(bf16[648,128]{1,0:T(8,128)(2,1)} %get-tuple-element.39), channel_id=1, source_target_pairs={{0,6},{1,7},{2,0},{3,1},{4,2},{5,3},{6,4},{7,5},{8,14},{9,15},{10,... | collective-permute-start | bytes 497672 | tf_op jit(solution)/shard_map/ppermute | solution.py:443
  63.6 15.4 %collective-permute-start.6 = (bf16[648,128]{1,0:T(8,128)(2,1)}, bf16[648,128]{1,0:T(8,128)(2,1)S(1)}, u32[]{:S(2)}, u32[]{:S(2)}) collective-permute-start(bf16[648,128]{1,0:T(8,128)(2,1)} %get-tuple-element.40), channel_id=1, source_target_pairs={{0,7},{1,0},{2,1},{3,2},{4,3},{5,4},{6,5},{7,6},{8,15},{9,8},{10,9... | collective-permute-start | bytes 497672 | tf_op jit(solution)/shard_map/ppermute | solution.py:443
  79.1 0.9 copy-start.4
  82.4 8.9 %collective-permute-start.12 = (bf16[552,128]{1,0:T(8,128)(2,1)}, bf16[552,128]{1,0:T(8,128)(2,1)S(1)}, u32[]{:S(2)}, u32[]{:S(2)}) collective-permute-start(bf16[552,128]{1,0:T(8,128)(2,1)} %get-tuple-element.48), channel_id=1, source_target_pairs={{0,2},{1,3},{2,4},{3,5},{4,6},{5,7},{6,0},{7,1},{8,10},{9,11},{10,... | collective-permute-start | bytes 423944 | tf_op jit(solution)/shard_map/ppermute | solution.py:443
  83.7 14.6 %collective-permute-start.13 = (bf16[552,128]{1,0:T(8,128)(2,1)}, bf16[552,128]{1,0:T(8,128)(2,1)S(1)}, u32[]{:S(2)}, u32[]{:S(2)}) collective-permute-start(bf16[552,128]{1,0:T(8,128)(2,1)} %get-tuple-element.49), channel_id=1, source_target_pairs={{0,1},{1,2},{2,3},{3,4},{4,5},{5,6},{6,7},{7,0},{8,9},{9,10},{10,1... | collective-permute-start | bytes 423944 | tf_op jit(solution)/shard_map/ppermute | solution.py:443
  87.0 16.3 %collective-permute-start.8 = (bf16[552,128]{1,0:T(8,128)(2,1)}, bf16[552,128]{1,0:T(8,128)(2,1)S(1)}, u32[]{:S(2)}, u32[]{:S(2)}) collective-permute-start(bf16[552,128]{1,0:T(8,128)(2,1)} %get-tuple-element.44), channel_id=1, source_target_pairs={{0,6},{1,7},{2,0},{3,1},{4,2},{5,3},{6,4},{7,5},{8,14},{9,15},{10,... | collective-permute-start | bytes 423944 | tf_op jit(solution)/shard_map/ppermute | solution.py:443
  88.0 15.4 %collective-permute-start.9 = (bf16[552,128]{1,0:T(8,128)(2,1)}, bf16[552,128]{1,0:T(8,128)(2,1)S(1)}, u32[]{:S(2)}, u32[]{:S(2)}) collective-permute-start(bf16[552,128]{1,0:T(8,128)(2,1)} %get-tuple-element.45), channel_id=1, source_target_pairs={{0,5},{1,6},{2,7},{3,0},{4,1},{5,2},{6,3},{7,4},{8,13},{9,14},{10,... | collective-permute-start | bytes 423944 | tf_op jit(solution)/shard_map/ppermute | solution.py:443
  90.3 18.9 %collective-permute-start.11 = (bf16[552,128]{1,0:T(8,128)(2,1)}, bf16[552,128]{1,0:T(8,128)(2,1)S(1)}, u32[]{:S(2)}, u32[]{:S(2)}) collective-permute-start(bf16[552,128]{1,0:T(8,128)(2,1)} %get-tuple-element.47), channel_id=1, source_target_pairs={{0,3},{1,4},{2,5},{3,6},{4,7},{5,0},{6,1},{7,2},{8,11},{9,12},{10,... | collective-permute-start | bytes 423944 | tf_op jit(solution)/shard_map/ppermute | solution.py:443
  91.2 20.4 %collective-permute-start.10 = (bf16[552,128]{1,0:T(8,128)(2,1)}, bf16[552,128]{1,0:T(8,128)(2,1)S(1)}, u32[]{:S(2)}, u32[]{:S(2)}) collective-permute-start(bf16[552,128]{1,0:T(8,128)(2,1)} %get-tuple-element.46), channel_id=1, source_target_pairs={{0,4},{1,5},{2,6},{3,7},{4,0},{5,1},{6,2},{7,3},{8,12},{9,13},{10,... | collective-permute-start | bytes 423944 | tf_op jit(solution)/shard_map/ppermute | solution.py:443
  98.4 14.6 %collective-permute-start.7 = (bf16[552,128]{1,0:T(8,128)(2,1)}, bf16[552,128]{1,0:T(8,128)(2,1)S(1)}, u32[]{:S(2)}, u32[]{:S(2)}) collective-permute-start(bf16[552,128]{1,0:T(8,128)(2,1)} %get-tuple-element.43), channel_id=1, source_target_pairs={{0,7},{1,0},{2,1},{3,2},{4,3},{5,4},{6,5},{7,6},{8,15},{9,8},{10,9... | collective-permute-start | bytes 423944 | tf_op jit(solution)/shard_map/ppermute | solution.py:443
  98.4 4.0 %copy-start.2 = (bf16[552,128]{1,0:T(8,128)(2,1)S(1)}, bf16[552,128]{1,0:T(8,128)(2,1)}, u32[]{:S(2)}) copy-start(bf16[552,128]{1,0:T(8,128)(2,1)} %get-tuple-element.42.refs_1_) | copy-start | bytes 423940
  110.1 5.0 %collective-permute-start.17 = (bf16[23,24,128]{2,1,0:T(8,128)(2,1)S(1)}, bf16[23,24,128]{2,1,0:T(8,128)(2,1)S(1)}, u32[]{:S(2)}, u32[]{:S(2)}) collective-permute-start(bf16[23,24,128]{2,1,0:T(8,128)(2,1)S(1)} %get-tuple-element.61), channel_id=1, source_target_pairs={{0,128},{128,0},{1,129},{129,1},{2,130},{130,2},{3,131},{131,3},{4... | collective-permute-start | bytes 423944 | tf_op jit(solution)/shard_map/ppermute | solution.py:547
  110.5 6.8 %collective-permute-start.16 = (bf16[23,24,128]{2,1,0:T(8,128)(2,1)S(1)}, bf16[23,24,128]{2,1,0:T(8,128)(2,1)S(1)}, u32[]{:S(2)}, u32[]{:S(2)}) collective-permute-start(bf16[23,24,128]{2,1,0:T(8,128)(2,1)S(1)} %get-tuple-element.59), channel_id=1, source_target_pairs={{0,128},{128,0},{1,129},{129,1},{2,130},{130,2},{3,131},{131,3},{4... | collective-permute-start | bytes 423944 | tf_op jit(solution)/shard_map/ppermute | solution.py:547
  112.5 7.8 %collective-permute-start.15 = (bf16[23,24,128]{2,1,0:T(8,128)(2,1)S(1)}, bf16[23,24,128]{2,1,0:T(8,128)(2,1)S(1)}, u32[]{:S(2)}, u32[]{:S(2)}) collective-permute-start(bf16[23,24,128]{2,1,0:T(8,128)(2,1)S(1)} %get-tuple-element.57), channel_id=1, source_target_pairs={{0,128},{128,0},{1,129},{129,1},{2,130},{130,2},{3,131},{131,3},{4... | collective-permute-start | bytes 423944 | tf_op jit(solution)/shard_map/ppermute | solution.py:547
  112.9 4.3 %copy-start.5 = (f32[2,2]{1,0:T(2,128)S(1)}, f32[2,2]{1,0:T(2,128)}, u32[]{:S(2)}) copy-start(f32[2,2]{1,0:T(2,128)} %mix.5) | copy-start | bytes 52
  113.8 9.5 %collective-permute-start.14 = (bf16[23,24,128]{2,1,0:T(8,128)(2,1)S(1)}, bf16[23,24,128]{2,1,0:T(8,128)(2,1)S(1)}, u32[]{:S(2)}, u32[]{:S(2)}) collective-permute-start(bf16[23,24,128]{2,1,0:T(8,128)(2,1)S(1)} %get-tuple-element.55), channel_id=1, source_target_pairs={{0,128},{128,0},{1,129},{129,1},{2,130},{130,2},{3,131},{131,3},{4... | collective-permute-start | bytes 423944 | tf_op jit(solution)/shard_map/ppermute | solution.py:547
